TPU v7x, 1024 devices: a whole 8x8x8 slice. The times are simulated.
1024 devices in a mesh: ctx: 64 (over z, y), head: 8 (over x), pipe: 2 (over core).
Axes of the slice: x: 8, y: 8, z: 8, core: 2. Of those that a mesh axis runs over, the one named last changes fastest.
Arguments:
- queries: bfloat16 [2, 16384, 4096], P('pipe', 'ctx', 'head'), may hold values from -0.52734375 to 0.52734375
- keys: bfloat16 [2, 16384, 4096], P('pipe', 'ctx', 'head'), may hold values from -0.52734375 to 0.52734375
- values: bfloat16 [2, 16384, 4096], P('pipe', 'ctx', 'head'), may hold values from -0.52734375 to 0.52734375
- out_grad: bfloat16 [2, 16384, 4096], P('pipe', 'ctx', 'head'), may hold values from -6 to 6
- log_decay: float32 [2, 32, 16384], P('pipe', 'head', 'ctx'), may hold values from -1 to 0
- segment_ids: int32 [2, 16384], P('pipe', 'ctx'), may hold values from 0 to 15, never falling along the last dimension, each value on 1 to 2048 neighbouring positions
- w_value: bfloat16 [2, 6144, 4096], P('pipe', None, 'head'), may hold values from -0.09375 to 0.09375
Outputs:
- grad_queries: bfloat16 [2, 16384, 4096], P('pipe', 'ctx', 'head')
- grad_keys: bfloat16 [2, 16384, 4096], P('pipe', 'ctx', 'head')
- grad_values: bfloat16 [2, 16384, 4096], P('pipe', 'ctx', 'head')
- grad_input_prev: bfloat16 [2, 16384, 6144], P('pipe', 'ctx', 'head')
Inputs may be any that keep to these rules, and one draw needn't show every extreme that they name: `segment_ids`: never falls along a section's tokens; each document holds at most 2048 tokens, and one holds exactly that many.
All inputs are finite; a program needn't handle non-finite values.
Results may differ from a plain program's by a relative error of at most 0.027.
Values may be sent and summed in bfloat16 or wider, within the bound.
No kernel may reach another device: no remote copies, remote signals or barrier semaphores. Data moves between devices by JAX's collectives and lax.ppermute only.
A program may use at most 64 MiB of HBM per device.

v0:
```python
import jax
import jax.numpy as jnp
from jax import lax
from jax.sharding import PartitionSpec as P

precise = lax.Precision.HIGHEST


def as_sent(value):
    return jax.tree.map(lambda a: a.astype(jnp.bfloat16) if a.dtype == jnp.float32 else a, value)


def from_behind(value, axis, steps):
    count = lax.axis_size(axis)
    leading, last = (max(0, -steps), min(count, count - steps))
    return lax.ppermute(value, axis, [(source, source + steps) for source in range(leading, last)])


def passed_along(block, axis, distance):
    devices = range(lax.axis_size(axis))
    route = [((i - distance) % len(devices), i) for i in devices]
    return lax.ppermute(block, axis, route)


def join_forward(earlier, succeeding):
    tags_in, decay_in, state_in = earlier
    tags_out, decay_out, state_out = succeeding
    joined = (tags_out[..., 0] == tags_in[..., 1]) | (tags_out[..., 0] < 0) | (tags_in[..., 1] < 0)
    factor = jnp.where(joined, 1.0, 0.0)[..., None] * decay_out
    first_id = jnp.where(tags_in[..., 0] < 0, tags_out[..., 0], tags_in[..., 0])
    last_id = jnp.where(tags_out[..., 1] < 0, tags_in[..., 1], tags_out[..., 1])
    return (
        jnp.stack([first_id, last_id], axis=-1),
        factor * decay_in,
        state_out + factor[..., None, None] * state_in,
    )


def join_backward(earlier, succeeding):
    tags_in, decay_in, state_in = earlier
    tags_out, decay_out, state_out = succeeding
    joined = (tags_in[..., 0] == tags_out[..., 1]) | (tags_in[..., 0] < 0) | (tags_out[..., 1] < 0)
    factor = jnp.where(joined, 1.0, 0.0)[..., None] * decay_out
    first_id = jnp.where(tags_out[..., 0] < 0, tags_in[..., 0], tags_out[..., 0])
    last_id = jnp.where(tags_in[..., 1] < 0, tags_out[..., 1], tags_in[..., 1])
    return (
        jnp.stack([first_id, last_id], axis=-1),
        factor * decay_in,
        state_out + factor[..., None, None] * state_in,
    )


def body(queries, keys, values, out_grad, log_decay, segment_ids, w_value):
    tok_rows = queries.shape[1]
    head_count = log_decay.shape[1]
    head_width = queries.shape[2] // head_count

    def split_heads(array):
        return array[0].reshape(tok_rows, head_count, head_width)

    query_heads = split_heads(queries)
    key_heads = split_heads(keys)
    value_heads = split_heads(values)
    grad_heads = split_heads(out_grad)
    log_rates = log_decay[0]
    seg_ids = segment_ids[0]
    positions = jnp.arange(tok_rows)
    upper_mask = (positions[:, None] <= positions[None, :]).astype(jnp.float32)
    cumulative = jnp.dot(log_rates, upper_mask, precision=precise)
    decay_end = cumulative[:, -1]
    first_id = seg_ids[0]
    last_id = seg_ids[-1]
    causal = (positions[None, :] <= positions[:, None]) & (seg_ids[:, None] == seg_ids[None, :])
    gaps = cumulative[:, :, None] - cumulative[:, None, :]
    decay_weights = jnp.where(causal[None], jnp.exp(jnp.where(causal[None], gaps, 0.0)), 0.0)
    through = jnp.exp(decay_end) * jnp.where(first_id == last_id, 1.0, 0.0)
    tags = jnp.stack([first_id, last_id]).astype(jnp.float32)
    fwd_scale = jnp.where(
        seg_ids[None, :] == last_id, jnp.exp(decay_end[:, None] - cumulative), 0.0
    )
    scaled_keys = key_heads.astype(jnp.float32) * fwd_scale.T[:, :, None]
    fwd_local = jnp.einsum(
        "thd,the->hde", scaled_keys, value_heads.astype(jnp.float32), precision=precise
    )
    rev_scale = jnp.where(seg_ids[None, :] == first_id, jnp.exp(cumulative), 0.0)
    scaled_queries = query_heads.astype(jnp.float32) * rev_scale.T[:, :, None]
    rev_local = jnp.einsum(
        "thd,the->hde", scaled_queries, grad_heads.astype(jnp.float32), precision=precise
    )
    forward_item = (tags, through, fwd_local)
    backward_item = (tags, through, rev_local)
    ahead = forward_item
    trailing_offset = backward_item
    levels = (lax.axis_size("ctx") - 1).bit_length()
    for round_index in range(levels + 1):
        distance = 1 if round_index == 0 else 2 ** (round_index - 1)
        arrived = from_behind(
            (as_sent(ahead[0]), as_sent(ahead[1]), as_sent(ahead[2])), "ctx", distance
        )
        ahead = arrived if round_index == 0 else join_forward(arrived, ahead)
    for round_index in range(levels + 1):
        distance = 1 if round_index == 0 else 2 ** (round_index - 1)
        arrived = from_behind(
            (as_sent(trailing_offset[0]), as_sent(trailing_offset[1]), as_sent(trailing_offset[2])),
            "ctx",
            -distance,
        )
        trailing_offset = arrived if round_index == 0 else join_backward(arrived, trailing_offset)
    fwd_carry = ahead[2].astype(jnp.bfloat16)
    bwd_carry = trailing_offset[2].astype(jnp.bfloat16)
    seg_float = seg_ids.astype(jnp.float32)
    fwd_gain = jnp.where(seg_float[None, :] == ahead[0][1], jnp.exp(cumulative), 0.0).T[:, :, None]
    bwd_gain = jnp.where(
        seg_float[None, :] == trailing_offset[0][0], jnp.exp(decay_end[:, None] - cumulative), 0.0
    ).T[:, :, None]
    value_scores = (
        jnp.einsum("thd,shd->hts", grad_heads, value_heads, preferred_element_type=jnp.float32)
        * decay_weights
    ).astype(jnp.bfloat16)
    key_scores = (
        jnp.einsum("thd,shd->hts", query_heads, key_heads, preferred_element_type=jnp.float32)
        * decay_weights
    ).astype(jnp.bfloat16)
    grad_query = jnp.einsum(
        "hts,shd->thd", value_scores, key_heads, preferred_element_type=jnp.float32
    ) + fwd_gain * jnp.einsum(
        "the,hde->thd", grad_heads, fwd_carry, preferred_element_type=jnp.float32
    )
    grad_key = jnp.einsum(
        "hts,thd->shd", value_scores, query_heads, preferred_element_type=jnp.float32
    ) + bwd_gain * jnp.einsum(
        "the,hde->thd", value_heads, bwd_carry, preferred_element_type=jnp.float32
    )
    grad_value = jnp.einsum(
        "hts,thd->shd", key_scores, grad_heads, preferred_element_type=jnp.float32
    ) + bwd_gain * jnp.einsum(
        "thd,hde->the", key_heads, bwd_carry, preferred_element_type=jnp.float32
    )
    flat_width = head_count * head_width
    grad_query = grad_query.reshape(tok_rows, flat_width).astype(jnp.bfloat16)
    grad_key = grad_key.reshape(tok_rows, flat_width).astype(jnp.bfloat16)
    grad_value = grad_value.reshape(tok_rows, flat_width).astype(jnp.bfloat16)
    weight_local = w_value[0]
    summed_rows = lax.psum_scatter(
        lax.dot_general(
            weight_local, grad_value, (((1,), (1,)), ((), ())), preferred_element_type=jnp.float32
        ).astype(jnp.bfloat16),
        "head",
        scatter_dimension=0,
        tiled=True,
    )
    contracted_result = summed_rows.T
    shifted = passed_along(contracted_result, "pipe", -1)
    return (grad_query[None], grad_key[None], grad_value[None], shifted[None])


def solution(mesh):
    in_specs = (
        P("pipe", "ctx", "head"),
        P("pipe", "ctx", "head"),
        P("pipe", "ctx", "head"),
        P("pipe", "ctx", "head"),
        P("pipe", "head", "ctx"),
        P("pipe", "ctx"),
        P("pipe", None, "head"),
    )
    out_specs = (
        P("pipe", "ctx", "head"),
        P("pipe", "ctx", "head"),
        P("pipe", "ctx", "head"),
        P("pipe", "ctx", "head"),
    )
    return jax.shard_map(body, mesh=mesh, in_specs=in_specs, out_specs=out_specs, check_vma=False)
```

profile of v0, /device:TPU:1, one launch (start us, length us, event | category | flops | bytes accessed | tf_op | source)
XLA Modules:
  0.0 295.9 jit_solution(16606249017757533722)
XLA Ops:
  11.1 4.8 %collective-permute-start = (bf16[2]{0:T(256)(128)(2,1)S(1)}, bf16[2]{0:T(256)(128)(2,1)S(1)}, u32[]{:S(2)}, u32[]{:S(2)}) collective-permute-start(bf16[2]{0:T(256)(128)(2,1)S(1)} %fusion.34), channel_id=1, source_target_pairs={{0,16},{16,32},{32,48},{48,64},{64,80},{80,96},{96,112},{112,128},... | collective-permute-start | bytes 20 | tf_op jit(solution)/shard_map/ppermute | solution.py:16
  26.0 4.6 %collective-permute-start.1 = (bf16[2]{0:T(256)(128)(2,1)S(1)}, bf16[2]{0:T(256)(128)(2,1)S(1)}, u32[]{:S(2)}, u32[]{:S(2)}) collective-permute-start(bf16[2]{0:T(256)(128)(2,1)S(1)} %collective-permute-done), channel_id=1, source_target_pairs={{0,16},{16,32},{32,48},{48,64},{64,80},{80,96},{96,112},{112,128},... | collective-permute-start | bytes 20 | tf_op jit(solution)/shard_map/ppermute | solution.py:16
  39.7 6.3 %collective-permute-start.2 = (bf16[2]{0:T(256)(128)(2,1)S(1)}, bf16[2]{0:T(256)(128)(2,1)S(1)}, u32[]{:S(2)}, u32[]{:S(2)}) collective-permute-start(bf16[2]{0:T(256)(128)(2,1)S(1)} %pad_maximum_fusion), channel_id=1, source_target_pairs={{0,32},{16,48},{32,64},{48,80},{64,96},{80,112},{96,128},{112,144}... | collective-permute-start | bytes 20 | tf_op jit(solution)/shard_map/ppermute | solution.py:16
  52.6 8.4 %collective-permute-start.3 = (bf16[2]{0:T(256)(128)(2,1)S(1)}, bf16[2]{0:T(256)(128)(2,1)S(1)}, u32[]{:S(2)}, u32[]{:S(2)}) collective-permute-start(bf16[2]{0:T(256)(128)(2,1)S(1)} %pad_maximum_fusion.1), channel_id=1, source_target_pairs={{0,64},{16,80},{32,96},{48,112},{64,128},{80,144},{96,160},{112,17... | collective-permute-start | bytes 20 | tf_op jit(solution)/shard_map/ppermute | solution.py:16
  67.8 7.9 %collective-permute-start.4 = (bf16[2]{0:T(256)(128)(2,1)S(1)}, bf16[2]{0:T(256)(128)(2,1)S(1)}, u32[]{:S(2)}, u32[]{:S(2)}) collective-permute-start(bf16[2]{0:T(256)(128)(2,1)S(1)} %pad_maximum_fusion.2), channel_id=1, source_target_pairs={{0,128},{16,144},{32,160},{48,176},{64,192},{80,208},{96,224},{112... | collective-permute-start | bytes 20 | tf_op jit(solution)/shard_map/ppermute | solution.py:16
  82.0 8.2 %collective-permute-start.5 = (bf16[2]{0:T(256)(128)(2,1)S(1)}, bf16[2]{0:T(256)(128)(2,1)S(1)}, u32[]{:S(2)}, u32[]{:S(2)}) collective-permute-start(bf16[2]{0:T(256)(128)(2,1)S(1)} %pad_maximum_fusion.3), channel_id=1, source_target_pairs={{0,256},{16,272},{32,288},{48,304},{64,320},{80,336},{96,352},{112... | collective-permute-start | bytes 20 | tf_op jit(solution)/shard_map/ppermute | solution.py:16
  96.5 11.2 %collective-permute-start.6 = (bf16[2]{0:T(256)(128)(2,1)S(1)}, bf16[2]{0:T(256)(128)(2,1)S(1)}, u32[]{:S(2)}, u32[]{:S(2)}) collective-permute-start(bf16[2]{0:T(256)(128)(2,1)S(1)} %pad_maximum_fusion.4), channel_id=1, source_target_pairs={{0,512},{16,528},{32,544},{48,560},{64,576},{80,592},{96,608},{112... | collective-permute-start | bytes 20 | tf_op jit(solution)/shard_map/ppermute | solution.py:16
  124.7 3.2 %collective-permute-done.29 = bf16[4,128,128]{2,1,0:T(8,128)(2,1)S(1)} collective-permute-done((bf16[4,128,128]{2,1,0:T(8,128)(2,1)S(1)}, bf16[4,128,128]{2,1,0:T(8,128)(2,1)S(1)}, u32[]{:S(2)}, u32[]{:S(2)}) %collective-permute-start.29) | collective-permute-done | bytes 131104 | tf_op jit(solution)/shard_map/ppermute | solution.py:16
  131.9 4.8 %collective-permute-done.31 = bf16[4,128,128]{2,1,0:T(8,128)(2,1)S(1)} collective-permute-done((bf16[4,128,128]{2,1,0:T(8,128)(2,1)S(1)}, bf16[4,128,128]{2,1,0:T(8,128)(2,1)S(1)}, u32[]{:S(2)}, u32[]{:S(2)}) %collective-permute-start.31) | collective-permute-done | bytes 131104 | tf_op jit(solution)/shard_map/ppermute | solution.py:16
  142.1 5.6 %collective-permute-done.33 = bf16[4,128,128]{2,1,0:T(8,128)(2,1)S(1)} collective-permute-done((bf16[4,128,128]{2,1,0:T(8,128)(2,1)S(1)}, bf16[4,128,128]{2,1,0:T(8,128)(2,1)S(1)}, u32[]{:S(2)}, u32[]{:S(2)}) %collective-permute-start.33) | collective-permute-done | bytes 131104 | tf_op jit(solution)/shard_map/ppermute | solution.py:16
  152.9 9.3 %collective-permute-done.35 = bf16[4,128,128]{2,1,0:T(8,128)(2,1)S(1)} collective-permute-done((bf16[4,128,128]{2,1,0:T(8,128)(2,1)S(1)}, bf16[4,128,128]{2,1,0:T(8,128)(2,1)S(1)}, u32[]{:S(2)}, u32[]{:S(2)}) %collective-permute-start.35) | collective-permute-done | bytes 131104 | tf_op jit(solution)/shard_map/ppermute | solution.py:16
  165.6 5.7 %collective-permute-done.37 = bf16[4,128,128]{2,1,0:T(8,128)(2,1)S(1)} collective-permute-done((bf16[4,128,128]{2,1,0:T(8,128)(2,1)S(1)}, bf16[4,128,128]{2,1,0:T(8,128)(2,1)S(1)}, u32[]{:S(2)}, u32[]{:S(2)}) %collective-permute-start.37) | collective-permute-done | bytes 131104 | tf_op jit(solution)/shard_map/ppermute | solution.py:16
  173.3 9.4 %collective-permute-done.39 = bf16[4,128,128]{2,1,0:T(8,128)(2,1)S(1)} collective-permute-done((bf16[4,128,128]{2,1,0:T(8,128)(2,1)S(1)}, bf16[4,128,128]{2,1,0:T(8,128)(2,1)S(1)}, u32[]{:S(2)}, u32[]{:S(2)}) %collective-permute-start.39) | collective-permute-done | bytes 131104 | tf_op jit(solution)/shard_map/ppermute | solution.py:16
  183.1 6.3 %fusion = bf16[6144,256]{0,1:T(8,128)(2,1)} fusion(bf16[256,512]{0,1:T(8,128)(2,1)S(1)} %bitcast.116, bf16[1,6144,512]{2,1,0:T(8,128)(2,1)} %param.13), kind=kOutput, calls=%fused_computation.1 | convolution fusion | flops 1612185600 | bytes 9699328 | tf_op jit(solution)/shard_map/dot_general | solution.py:145
  192.0 5.7 %collective-permute-start.7 = (bf16[4,128,128]{2,1,0:T(8,128)(2,1)S(1)}, bf16[4,128,128]{2,1,0:T(8,128)(2,1)S(1)}, u32[]{:S(2)}, u32[]{:S(2)}) collective-permute-start(bf16[4,128,128]{2,1,0:T(8,128)(2,1)S(1)} %convolution_convert_fusion.2), channel_id=1, source_target_pairs={{0,16},{16,32},{32,48},{48,64},{64,80},{80,96},{96,112},{112,128},... | collective-permute-start | bytes 393224 | tf_op jit(solution)/shard_map/ppermute | solution.py:16
  205.1 3.6 %collective-permute-start.9 = (bf16[4,128,128]{2,1,0:T(8,128)(2,1)S(1)}, bf16[4,128,128]{2,1,0:T(8,128)(2,1)S(1)}, u32[]{:S(2)}, u32[]{:S(2)}) collective-permute-start(bf16[4,128,128]{2,1,0:T(8,128)(2,1)S(1)} %collective-permute-done.7), channel_id=1, source_target_pairs={{0,16},{16,32},{32,48},{48,64},{64,80},{80,96},{96,112},{112,128},... | collective-permute-start | bytes 393224 | tf_op jit(solution)/shard_map/ppermute | solution.py:16
  208.7 5.2 %collective-permute-start.12 = (bf16[4]{0:T(256)(128)(2,1)S(1)}, bf16[4]{0:T(256)(128)(2,1)S(1)}, u32[]{:S(2)}, u32[]{:S(2)}) collective-permute-start(bf16[4]{0:T(256)(128)(2,1)S(1)} %get-tuple-element.34), channel_id=1, source_target_pairs={{0,32},{16,48},{32,64},{48,80},{64,96},{80,112},{96,128},{112,144}... | collective-permute-start | bytes 32 | tf_op jit(solution)/shard_map/ppermute | solution.py:16
  215.3 2.7 collective-permute-start.11
  218.0 11.9 %collective-permute-start.14 = (bf16[4]{0:T(256)(128)(2,1)S(1)}, bf16[4]{0:T(256)(128)(2,1)S(1)}, u32[]{:S(2)}, u32[]{:S(2)}) collective-permute-start(bf16[4]{0:T(256)(128)(2,1)S(1)} %get-tuple-element.32), channel_id=1, source_target_pairs={{0,64},{16,80},{32,96},{48,112},{64,128},{80,144},{96,160},{112,17... | collective-permute-start | bytes 32 | tf_op jit(solution)/shard_map/ppermute | solution.py:16
  232.8 3.7 %collective-permute-start.13 = (bf16[4,128,128]{2,1,0:T(8,128)(2,1)S(1)}, bf16[4,128,128]{2,1,0:T(8,128)(2,1)S(1)}, u32[]{:S(2)}, u32[]{:S(2)}) collective-permute-start(bf16[4,128,128]{2,1,0:T(8,128)(2,1)S(1)} %multiply_add_fusion.9), channel_id=1, source_target_pairs={{0,64},{16,80},{32,96},{48,112},{64,128},{80,144},{96,160},{112,17... | collective-permute-start | bytes 393224 | tf_op jit(solution)/shard_map/ppermute | solution.py:16
  240.2 6.4 %collective-permute-start.15 = (bf16[4,128,128]{2,1,0:T(8,128)(2,1)S(1)}, bf16[4,128,128]{2,1,0:T(8,128)(2,1)S(1)}, u32[]{:S(2)}, u32[]{:S(2)}) collective-permute-start(bf16[4,128,128]{2,1,0:T(8,128)(2,1)S(1)} %multiply_add_fusion.8), channel_id=1, source_target_pairs={{0,128},{16,144},{32,160},{48,176},{64,192},{80,208},{96,224},{112... | collective-permute-start | bytes 393224 | tf_op jit(solution)/shard_map/ppermute | solution.py:16
  246.7 3.6 %collective-permute-start.18 = (bf16[4]{0:T(256)(128)(2,1)S(1)}, bf16[4]{0:T(256)(128)(2,1)S(1)}, u32[]{:S(2)}, u32[]{:S(2)}) collective-permute-start(bf16[4]{0:T(256)(128)(2,1)S(1)} %get-tuple-element.28), channel_id=1, source_target_pairs={{0,256},{16,272},{32,288},{48,304},{64,320},{80,336},{96,352},{112... | collective-permute-start | bytes 32 | tf_op jit(solution)/shard_map/ppermute | solution.py:16
  254.7 11.2 %collective-permute-start.19 = (bf16[4,128,128]{2,1,0:T(8,128)(2,1)S(1)}, bf16[4,128,128]{2,1,0:T(8,128)(2,1)S(1)}, u32[]{:S(2)}, u32[]{:S(2)}) collective-permute-start(bf16[4,128,128]{2,1,0:T(8,128)(2,1)S(1)} %multiply_add_fusion.6), channel_id=1, source_target_pairs={{0,512},{16,528},{32,544},{48,560},{64,576},{80,592},{96,608},{112... | collective-permute-start | bytes 393224 | tf_op jit(solution)/shard_map/ppermute | solution.py:16
  266.8 19.3 %collective-permute-start.40 = (bf16[256,768]{1,0:T(8,128)(2,1)}, bf16[256,768]{1,0:T(8,128)(2,1)S(1)}, u32[]{:S(2)}, u32[]{:S(2)}) collective-permute-start(bf16[256,768]{1,0:T(8,128)(2,1)} %bitcast.135), channel_id=1, source_target_pairs={{1,0},{0,1},{3,2},{2,3},{5,4},{4,5},{7,6},{6,7},{9,8},{8,9},{11,10... | collective-permute-start | bytes 1179656 | tf_op jit(solution)/shard_map/ppermute | solution.py:22
  (134 shorter events, 70.7 us)
Async XLA Ops:
  7.2 259.6 %reduce-scatter.2.cloned.1.call-start = ((), (), s32[]{:S(2)}) async-start(), calls=%async_computation.1 | async-start | bytes 3538944 | tf_op jit(solution)/shard_map/reduce_scatter | solution.py:144
  9.9 12.3 %collective-permute-start.20 = (bf16[2]{0:T(256)(128)(2,1)S(1)}, bf16[2]{0:T(256)(128)(2,1)S(1)}, u32[]{:S(2)}, u32[]{:S(2)}) collective-permute-start(bf16[2]{0:T(256)(128)(2,1)S(1)} %fusion.34), channel_id=1, source_target_pairs={{16,0},{32,16},{48,32},{64,48},{80,64},{96,80},{112,96},{128,112},... | collective-permute-start | bytes 20 | tf_op jit(solution)/shard_map/ppermute | solution.py:16
  11.1 12.3 %collective-permute-start = (bf16[2]{0:T(256)(128)(2,1)S(1)}, bf16[2]{0:T(256)(128)(2,1)S(1)}, u32[]{:S(2)}, u32[]{:S(2)}) collective-permute-start(bf16[2]{0:T(256)(128)(2,1)S(1)} %fusion.34), channel_id=1, source_target_pairs={{0,16},{16,32},{32,48},{48,64},{64,80},{80,96},{96,112},{112,128},... | collective-permute-start | bytes 20 | tf_op jit(solution)/shard_map/ppermute | solution.py:16
  17.6 99.2 %collective-permute-start.28 = (bf16[4]{0:T(256)(128)(2,1)S(1)}, bf16[4]{0:T(256)(128)(2,1)S(1)}, u32[]{:S(2)}, u32[]{:S(2)}) collective-permute-start(bf16[4]{0:T(256)(128)(2,1)S(1)} %multiply_convert_fusion), channel_id=1, source_target_pairs={{16,0},{32,16},{48,32},{64,48},{80,64},{96,80},{112,96},{128,112},... | collective-permute-start | bytes 32 | tf_op jit(solution)/shard_map/ppermute | solution.py:16
  34.6 11.4 %collective-permute-start.22 = (bf16[2]{0:T(256)(128)(2,1)S(1)}, bf16[2]{0:T(256)(128)(2,1)S(1)}, u32[]{:S(2)}, u32[]{:S(2)}) collective-permute-start(bf16[2]{0:T(256)(128)(2,1)S(1)} %pad_maximum_fusion.5), channel_id=1, source_target_pairs={{32,0},{48,16},{64,32},{80,48},{96,64},{112,80},{128,96},{144,112}... | collective-permute-start | bytes 20 | tf_op jit(solution)/shard_map/ppermute | solution.py:16
  48.6 12.4 %collective-permute-start.23 = (bf16[2]{0:T(256)(128)(2,1)S(1)}, bf16[2]{0:T(256)(128)(2,1)S(1)}, u32[]{:S(2)}, u32[]{:S(2)}) collective-permute-start(bf16[2]{0:T(256)(128)(2,1)S(1)} %pad_maximum_fusion.6), channel_id=1, source_target_pairs={{64,0},{80,16},{96,32},{112,48},{128,64},{144,80},{160,96},{176,11... | collective-permute-start | bytes 20 | tf_op jit(solution)/shard_map/ppermute | solution.py:16
  52.6 12.5 %collective-permute-start.3 = (bf16[2]{0:T(256)(128)(2,1)S(1)}, bf16[2]{0:T(256)(128)(2,1)S(1)}, u32[]{:S(2)}, u32[]{:S(2)}) collective-permute-start(bf16[2]{0:T(256)(128)(2,1)S(1)} %pad_maximum_fusion.1), channel_id=1, source_target_pairs={{0,64},{16,80},{32,96},{48,112},{64,128},{80,144},{96,160},{112,17... | collective-permute-start | bytes 20 | tf_op jit(solution)/shard_map/ppermute | solution.py:16
  63.8 11.9 %collective-permute-start.24 = (bf16[2]{0:T(256)(128)(2,1)S(1)}, bf16[2]{0:T(256)(128)(2,1)S(1)}, u32[]{:S(2)}, u32[]{:S(2)}) collective-permute-start(bf16[2]{0:T(256)(128)(2,1)S(1)} %pad_maximum_fusion.7), channel_id=1, source_target_pairs={{128,0},{144,16},{160,32},{176,48},{192,64},{208,80},{224,96},{240... | collective-permute-start | bytes 20 | tf_op jit(solution)/shard_map/ppermute | solution.py:16
  67.8 11.7 %collective-permute-start.4 = (bf16[2]{0:T(256)(128)(2,1)S(1)}, bf16[2]{0:T(256)(128)(2,1)S(1)}, u32[]{:S(2)}, u32[]{:S(2)}) collective-permute-start(bf16[2]{0:T(256)(128)(2,1)S(1)} %pad_maximum_fusion.2), channel_id=1, source_target_pairs={{0,128},{16,144},{32,160},{48,176},{64,192},{80,208},{96,224},{112... | collective-permute-start | bytes 20 | tf_op jit(solution)/shard_map/ppermute | solution.py:16
  78.2 12.1 %collective-permute-start.25 = (bf16[2]{0:T(256)(128)(2,1)S(1)}, bf16[2]{0:T(256)(128)(2,1)S(1)}, u32[]{:S(2)}, u32[]{:S(2)}) collective-permute-start(bf16[2]{0:T(256)(128)(2,1)S(1)} %pad_maximum_fusion.8), channel_id=1, source_target_pairs={{256,0},{272,16},{288,32},{304,48},{320,64},{336,80},{352,96},{368... | collective-permute-start | bytes 20 | tf_op jit(solution)/shard_map/ppermute | solution.py:16
  82.0 11.9 %collective-permute-start.5 = (bf16[2]{0:T(256)(128)(2,1)S(1)}, bf16[2]{0:T(256)(128)(2,1)S(1)}, u32[]{:S(2)}, u32[]{:S(2)}) collective-permute-start(bf16[2]{0:T(256)(128)(2,1)S(1)} %pad_maximum_fusion.3), channel_id=1, source_target_pairs={{0,256},{16,272},{32,288},{48,304},{64,320},{80,336},{96,352},{112... | collective-permute-start | bytes 20 | tf_op jit(solution)/shard_map/ppermute | solution.py:16
  92.6 15.1 %collective-permute-start.26 = (bf16[2]{0:T(256)(128)(2,1)S(1)}, bf16[2]{0:T(256)(128)(2,1)S(1)}, u32[]{:S(2)}, u32[]{:S(2)}) collective-permute-start(bf16[2]{0:T(256)(128)(2,1)S(1)} %pad_maximum_fusion.9), channel_id=1, source_target_pairs={{512,0},{528,16},{544,32},{560,48},{576,64},{592,80},{608,96},{624... | collective-permute-start | bytes 20 | tf_op jit(solution)/shard_map/ppermute | solution.py:16
  96.5 11.9 %collective-permute-start.6 = (bf16[2]{0:T(256)(128)(2,1)S(1)}, bf16[2]{0:T(256)(128)(2,1)S(1)}, u32[]{:S(2)}, u32[]{:S(2)}) collective-permute-start(bf16[2]{0:T(256)(128)(2,1)S(1)} %pad_maximum_fusion.4), channel_id=1, source_target_pairs={{0,512},{16,528},{32,544},{48,560},{64,576},{80,592},{96,608},{112... | collective-permute-start | bytes 20 | tf_op jit(solution)/shard_map/ppermute | solution.py:16
  129.4 11.4 %collective-permute-start.34 = (bf16[4]{0:T(256)(128)(2,1)S(1)}, bf16[4]{0:T(256)(128)(2,1)S(1)}, u32[]{:S(2)}, u32[]{:S(2)}) collective-permute-start(bf16[4]{0:T(256)(128)(2,1)S(1)} %get-tuple-element.22), channel_id=1, source_target_pairs={{64,0},{80,16},{96,32},{112,48},{128,64},{144,80},{160,96},{176,11... | collective-permute-start | bytes 32 | tf_op jit(solution)/shard_map/ppermute | solution.py:16
  136.8 10.9 %collective-permute-start.33 = (bf16[4,128,128]{2,1,0:T(8,128)(2,1)S(1)}, bf16[4,128,128]{2,1,0:T(8,128)(2,1)S(1)}, u32[]{:S(2)}, u32[]{:S(2)}) collective-permute-start(bf16[4,128,128]{2,1,0:T(8,128)(2,1)S(1)} %multiply_add_fusion.4), channel_id=1, source_target_pairs={{64,0},{80,16},{96,32},{112,48},{128,64},{144,80},{160,96},{176,11... | collective-permute-start | bytes 393224 | tf_op jit(solution)/shard_map/ppermute | solution.py:16
  147.8 14.4 %collective-permute-start.35 = (bf16[4,128,128]{2,1,0:T(8,128)(2,1)S(1)}, bf16[4,128,128]{2,1,0:T(8,128)(2,1)S(1)}, u32[]{:S(2)}, u32[]{:S(2)}) collective-permute-start(bf16[4,128,128]{2,1,0:T(8,128)(2,1)S(1)} %multiply_add_fusion.3), channel_id=1, source_target_pairs={{128,0},{144,16},{160,32},{176,48},{192,64},{208,80},{224,96},{240... | collective-permute-start | bytes 393224 | tf_op jit(solution)/shard_map/ppermute | solution.py:16
  151.6 14.0 %collective-permute-start.38 = (bf16[4]{0:T(256)(128)(2,1)S(1)}, bf16[4]{0:T(256)(128)(2,1)S(1)}, u32[]{:S(2)}, u32[]{:S(2)}) collective-permute-start(bf16[4]{0:T(256)(128)(2,1)S(1)} %get-tuple-element.18), channel_id=1, source_target_pairs={{256,0},{272,16},{288,32},{304,48},{320,64},{336,80},{352,96},{368... | collective-permute-start | bytes 32 | tf_op jit(solution)/shard_map/ppermute | solution.py:16
  171.3 11.4 %collective-permute-start.39 = (bf16[4,128,128]{2,1,0:T(8,128)(2,1)S(1)}, bf16[4,128,128]{2,1,0:T(8,128)(2,1)S(1)}, u32[]{:S(2)}, u32[]{:S(2)}) collective-permute-start(bf16[4,128,128]{2,1,0:T(8,128)(2,1)S(1)} %multiply_add_fusion.1), channel_id=1, source_target_pairs={{512,0},{528,16},{544,32},{560,48},{576,64},{592,80},{608,96},{624... | collective-permute-start | bytes 393224 | tf_op jit(solution)/shard_map/ppermute | solution.py:16
  189.4 11.0 %collective-permute-start.8 = (bf16[4]{0:T(256)(128)(2,1)S(1)}, bf16[4]{0:T(256)(128)(2,1)S(1)}, u32[]{:S(2)}, u32[]{:S(2)}) collective-permute-start(bf16[4]{0:T(256)(128)(2,1)S(1)} %multiply_convert_fusion), channel_id=1, source_target_pairs={{0,16},{16,32},{32,48},{48,64},{64,80},{80,96},{96,112},{112,128},... | collective-permute-start | bytes 32 | tf_op jit(solution)/shard_map/ppermute | solution.py:16
  192.0 13.2 %collective-permute-start.7 = (bf16[4,128,128]{2,1,0:T(8,128)(2,1)S(1)}, bf16[4,128,128]{2,1,0:T(8,128)(2,1)S(1)}, u32[]{:S(2)}, u32[]{:S(2)}) collective-permute-start(bf16[4,128,128]{2,1,0:T(8,128)(2,1)S(1)} %convolution_convert_fusion.2), channel_id=1, source_target_pairs={{0,16},{16,32},{32,48},{48,64},{64,80},{80,96},{96,112},{112,128},... | collective-permute-start | bytes 393224 | tf_op jit(solution)/shard_map/ppermute | solution.py:16
  215.3 17.4 %collective-permute-start.11 = (bf16[4,128,128]{2,1,0:T(8,128)(2,1)S(1)}, bf16[4,128,128]{2,1,0:T(8,128)(2,1)S(1)}, u32[]{:S(2)}, u32[]{:S(2)}) collective-permute-start(bf16[4,128,128]{2,1,0:T(8,128)(2,1)S(1)} %multiply_add_fusion.10), channel_id=1, source_target_pairs={{0,32},{16,48},{32,64},{48,80},{64,96},{80,112},{96,128},{112,144}... | collective-permute-start | bytes 393224 | tf_op jit(solution)/shard_map/ppermute | solution.py:16
  218.0 18.5 %collective-permute-start.14 = (bf16[4]{0:T(256)(128)(2,1)S(1)}, bf16[4]{0:T(256)(128)(2,1)S(1)}, u32[]{:S(2)}, u32[]{:S(2)}) collective-permute-start(bf16[4]{0:T(256)(128)(2,1)S(1)} %get-tuple-element.32), channel_id=1, source_target_pairs={{0,64},{16,80},{32,96},{48,112},{64,128},{80,144},{96,160},{112,17... | collective-permute-start | bytes 32 | tf_op jit(solution)/shard_map/ppermute | solution.py:16
  254.7 32.4 %collective-permute-start.19 = (bf16[4,128,128]{2,1,0:T(8,128)(2,1)S(1)}, bf16[4,128,128]{2,1,0:T(8,128)(2,1)S(1)}, u32[]{:S(2)}, u32[]{:S(2)}) collective-permute-start(bf16[4,128,128]{2,1,0:T(8,128)(2,1)S(1)} %multiply_add_fusion.6), channel_id=1, source_target_pairs={{0,512},{16,528},{32,544},{48,560},{64,576},{80,592},{96,608},{112... | collective-permute-start | bytes 393224 | tf_op jit(solution)/shard_map/ppermute | solution.py:16
  266.8 21.5 %collective-permute-start.40 = (bf16[256,768]{1,0:T(8,128)(2,1)}, bf16[256,768]{1,0:T(8,128)(2,1)S(1)}, u32[]{:S(2)}, u32[]{:S(2)}) collective-permute-start(bf16[256,768]{1,0:T(8,128)(2,1)} %bitcast.135), channel_id=1, source_target_pairs={{1,0},{0,1},{3,2},{2,3},{5,4},{4,5},{7,6},{6,7},{9,8},{8,9},{11,10... | collective-permute-start | bytes 1179656 | tf_op jit(solution)/shard_map/ppermute | solution.py:22
  (20 other events, 164.6 us)
Sparse Core Ops, SparseCore 0:
  189.5 64.8 reduce-scatter.1
where the time goes:
time: 298 us; the launch traced here: 296 us
  starting transfers between devices  158 us (53%)
  between operations  56.3 us (19%)
  waiting for transfers between devices  49.7 us (17%)
  local copies, waits for them, and re-layouts  16.2 us (5%)
  matrix products  9.79 us (3%)
  other arithmetic  6.06 us (2%)
    ppermute x40, starting transfers between devices, from_behind(): lax.ppermute(value, axis, [(source, source + steps) for source in range(l...  139 us
    ppermute x40, waiting for transfers between devices, from_behind(): lax.ppermute(value, axis, [(source, source + steps) for source in range(l...  49.7 us
    ppermute x1, starting transfers between devices, passed_along(): return lax.ppermute(block, axis, route)  19.3 us
    dot_general x1, matrix products, body(): lax.dot_general(weight_local, grad_value, (((1,), (1,)), ((), ())), prefe...  6.31 us
  transfers between devices with their start and end apart: 42, of which 13 were waited for; matrix products, arithmetic and copies ran while one was open for 7% of the time, Pallas kernels for 0%

commit v1 on v0

v1 whole, which is shorter than its diff:
```python
import jax
import jax.numpy as jnp
import numpy as np
from jax import lax
from jax.experimental import pallas as pl
from jax.experimental.pallas import tpu as pltpu
from jax.sharding import Mesh
from jax.sharding import PartitionSpec as P

f32, bf16 = jnp.float32, jnp.bfloat16
HIGHEST = lax.Precision.HIGHEST
ROW = 8
META = 16
NEVER = -1e30


def dot(a, b, dims):
    return lax.dot_general(a, b, (dims, ((), ())), preferred_element_type=f32)


def iota2(n, axis):
    return lax.broadcasted_iota(jnp.int32, (n, n), axis)


def cumulative_columns(rates):
    n = rates.shape[1]
    lower = (iota2(n, 1) <= iota2(n, 0)).astype(f32)
    return lax.dot_general(lower, rates, (((1,), (1,)), ((), ())), precision=HIGHEST, preferred_element_type=f32)


def cumulative_rows(rates):
    n = rates.shape[1]
    upper = (iota2(n, 0) <= iota2(n, 1)).astype(f32)
    return lax.dot_general(rates, upper, (((1,), (0,)), ((), ())), precision=HIGHEST, preferred_element_type=f32)


def write_message(out, h, state, first, last, through, width):
    share = state.shape[0] // 2
    high = through.astype(bf16)
    low = (through - high.astype(f32)).astype(bf16)
    row = lax.broadcasted_iota(jnp.int32, (META, width), 0)
    meta = jnp.where(row == 0, first, jnp.where(row == 1, last, 0.0))
    meta = jnp.where(row == 2, high.astype(f32), jnp.where(row == 3, low.astype(f32), meta)).astype(bf16)
    for half in range(2):
        p = 2 * h + half
        out[p, 0:share, :] = state[half * share : (half + 1) * share].astype(bf16)
        out[p, share : share + META, :] = meta


def ids_column(seg_row):
    n = seg_row.shape[1]
    on_diagonal = iota2(n, 0) == iota2(n, 1)
    return jnp.sum(jnp.where(on_diagonal, seg_row[...].astype(f32), 0.0), axis=1, keepdims=True)


def block_ids(seg):
    n = seg.shape[0]
    return seg[0:1, :], seg[n - 1 : n, :]


def backward_local_kernel(q, o, rates, seg_row, out):
    cum = cumulative_columns(rates[0])
    heads = rates.shape[1]
    n = cum.shape[0]
    dh = q.shape[2] // heads
    seg = ids_column(seg_row)
    first, last = block_ids(seg)
    scale = jnp.where(seg == seg[0:1, :], jnp.exp(cum), 0.0)
    for h in range(heads):
        cols = slice(h * dh, (h + 1) * dh)
        scaled = (q[0, :, cols].astype(f32) * scale[:, h : h + 1]).astype(bf16)
        state = dot(scaled, o[0, :, cols], ((0,), (0,)))
        write_message(out, h, state, first, last, jnp.exp(cum[n - 1 : n, h : h + 1]), dh)


def scores(a, b, weight):
    return (dot(a, b, ((1,), (1,))) * weight).astype(bf16)


def decay_weight(cum_col, cum_row, keep):
    return jnp.exp(jnp.where(keep, cum_col - cum_row, NEVER))


def forward_local_kernel(q, k, v, o, rates, seg_row, out, gv, gain):
    cum = cumulative_columns(rates[0])
    cum_t = cumulative_rows(rates[0])
    heads = rates.shape[1]
    n = cum.shape[0]
    dh = q.shape[2] // heads
    seg = ids_column(seg_row)
    first, last = block_ids(seg)
    keep = (iota2(n, 1) <= iota2(n, 0)) & (seg == seg_row[...].astype(f32))
    scale = jnp.where(seg == seg[n - 1 : n, :], jnp.exp(cum[n - 1 : n, :] - cum), 0.0)
    for h in range(heads):
        cols = slice(h * dh, (h + 1) * dh)
        kh = k[0, :, cols]
        scaled = (kh.astype(f32) * scale[:, h : h + 1]).astype(bf16)
        state = dot(scaled, v[0, :, cols], ((0,), (0,)))
        write_message(out, h, state, first, last, jnp.exp(cum[n - 1 : n, h : h + 1]), dh)
        weight = decay_weight(cum[:, h : h + 1], cum_t[h : h + 1, :], keep)
        ks = scores(q[0, :, cols], kh, weight)
        gv[:, cols] = dot(ks, o[0, :, cols], ((0,), (0,)))
        gain[:, h * dh : (h + 1) * dh] = jnp.broadcast_to(scale[:, h : h + 1], (n, dh))


def unpack(msg, y):
    share = msg.shape[1] - META
    block = msg[y].astype(f32)
    meta = block[share:, :]
    return block[:share], meta[0:1], meta[1:2], meta[2:3] + meta[3:4]


def order(reverse):
    return range(ROW - 1, -1, -1) if reverse else range(ROW)


def row_total_kernel(reverse, msg, out):
    share = msg.shape[1] - META
    tag, total = None, None
    for y in order(reverse):
        state, first, last, through = unpack(msg, y)
        if total is None:
            total = state
        else:
            same = jnp.where((first == last) & (tag == last), through, 0.0)
            total = same * total + state
        tag = first if reverse else last
    out[0:share, :] = total.astype(bf16)
    out[share:, :] = jnp.broadcast_to(tag, (META, tag.shape[1])).astype(bf16)


def row_scan_kernel(reverse, msg, carried, out):
    share = msg.shape[1] - META
    running = carried[0:share, :].astype(f32)
    tag = carried[share : share + META, :].astype(f32)[0:1]
    for y in order(reverse):
        state, first, last, through = unpack(msg, y)
        edge = last if reverse else first
        out[y] = jnp.where(edge == tag, running, 0.0).astype(bf16)
        same = jnp.where((first == last) & (tag == last), through, 0.0)
        running = same * running + state
        tag = first if reverse else last


def weight_kernel(local, gain, k, state, w, gv, out, kept):
    heads = gv.shape[1] // state.shape[1]
    dh = state.shape[1]

    @pl.when(pl.program_id(0) == 0)
    def _():
        for h in range(heads):
            cols = slice(h * dh, (h + 1) * dh)
            b = state[h * dh : (h + 1) * dh, :]
            far = dot(k[0, :, cols], b, ((1,), (0,)))
            kept[:, cols] = (local[:, cols] + gain[:, cols] * far).astype(bf16)
        gv[...] = kept[...]

    out[0] = dot(kept[...], w[0], ((1,), (1,))).astype(bf16)


def query_key_kernel(q, k, v, o, rates, seg_row, fwd, bwd, gain, dq, dk):
    cum = cumulative_columns(rates[0])
    cum_t = cumulative_rows(rates[0])
    heads = rates.shape[1]
    n = cum.shape[0]
    dh = q.shape[2] // heads
    seg = ids_column(seg_row)
    keep = (iota2(n, 1) <= iota2(n, 0)) & (seg == seg_row[...].astype(f32))
    reach = jnp.where(seg == seg[0:1, :], jnp.exp(cum), 0.0)
    for h in range(heads):
        cols = slice(h * dh, (h + 1) * dh)
        weight = decay_weight(cum[:, h : h + 1], cum_t[h : h + 1, :], keep)
        vs = scores(o[0, :, cols], v[0, :, cols], weight)
        f = fwd[h * dh : (h + 1) * dh, :]
        b = bwd[h * dh : (h + 1) * dh, :]
        far_q = dot(o[0, :, cols], f, ((1,), (1,)))
        far_k = dot(v[0, :, cols], b, ((1,), (1,)))
        dq[:, cols] = (dot(vs, k[0, :, cols], ((1,), (0,))) + reach[:, h : h + 1] * far_q).astype(bf16)
        dk[:, cols] = (dot(vs, q[0, :, cols], ((0,), (0,))) + gain[:, cols] * far_k).astype(bf16)


def call(kernel, shapes, name):
    return pl.pallas_call(kernel, out_shape=shapes, name=name)


def body(queries, keys, values, out_grad, log_decay, segment_ids, w_value):
    n, width = queries.shape[1:]
    heads = log_decay.shape[1]
    dh = width // heads
    rows = lax.axis_size("plane")
    groups = lax.axis_size("head")
    share = heads * dh // ROW
    message = jax.ShapeDtypeStruct((ROW, share + META, dh), bf16)
    total = jax.ShapeDtypeStruct((share + META, dh), bf16)
    states = jax.ShapeDtypeStruct((ROW, share, dh), bf16)

    def exchange(array):
        return lax.all_to_all(array, "line", 0, 0, tiled=True)

    def relay(msg, reverse, tag):
        own = call(lambda *refs: row_total_kernel(reverse, *refs), total, "total_" + tag)(msg)
        pairs = [(z, z - 1) for z in range(1, rows)] if reverse else [(z - 1, z) for z in range(1, rows)]
        return lax.ppermute(own, "plane", pairs)

    def scan(msg, carried, reverse, tag):
        out = call(lambda *refs: row_scan_kernel(reverse, *refs), states, "scan_" + tag)(msg, carried)
        return exchange(out).reshape(heads * dh, dh)

    sent = call(backward_local_kernel, message, "backward_local")(queries, out_grad, log_decay, segment_ids)
    got = exchange(sent)
    carried = relay(got, True, "backward")
    fwd_sent, gv_local, gain = call(
        forward_local_kernel,
        (message, jax.ShapeDtypeStruct((n, width), f32), jax.ShapeDtypeStruct((n, width), f32)),
        "forward_local",
    )(queries, keys, values, out_grad, log_decay, segment_ids)
    bwd = scan(got, carried, True, "backward")

    slice_rows = w_value.shape[1] // groups
    whole = lambda *shape: pl.BlockSpec(shape, lambda i: (0,) * len(shape))
    grad_value, partials = pl.pallas_call(
        weight_kernel,
        grid=(groups,),
        in_specs=[
            whole(n, width),
            whole(n, width),
            whole(1, n, width),
            whole(heads * dh, dh),
            pl.BlockSpec((1, slice_rows, width), lambda i: (i, 0, 0)),
        ],
        out_specs=[whole(n, width), pl.BlockSpec((1, n, slice_rows), lambda i: (i, 0, 0))],
        out_shape=(
            jax.ShapeDtypeStruct((n, width), bf16),
            jax.ShapeDtypeStruct((groups, n, slice_rows), bf16),
        ),
        scratch_shapes=[pltpu.VMEM((n, width), bf16)],
        name="weight",
    )(gv_local, gain, keys, bwd, w_value.reshape(groups, slice_rows, width))
    fwd_sent, partials = lax.optimization_barrier((fwd_sent, partials))
    summed = lax.psum_scatter(partials, "head", scatter_dimension=0, tiled=False)

    fwd_got = exchange(fwd_sent)
    fwd = scan(fwd_got, relay(fwd_got, False, "forward"), False, "forward")
    summed, fwd = lax.optimization_barrier((summed, fwd))
    grad_query, grad_key = call(
        query_key_kernel,
        (jax.ShapeDtypeStruct((n, width), bf16), jax.ShapeDtypeStruct((n, width), bf16)),
        "query_key",
    )(queries, keys, values, out_grad, log_decay, segment_ids, fwd, bwd, gain)

    sections = lax.axis_size("pipe")
    shifted = lax.ppermute(summed, "pipe", [((i + 1) % sections, i) for i in range(sections)])
    return (grad_query[None], grad_key[None], grad_value[None], shifted[None])


def solution(mesh):
    ctx, head, pipe = (mesh.shape[name] for name in ("ctx", "head", "pipe"))
    grid = Mesh(np.asarray(mesh.devices).reshape(ctx // ROW, ROW, head, pipe), ("plane", "line", "head", "pipe"))
    seq = ("plane", "line")
    tokens = P("pipe", seq, "head")
    return jax.shard_map(
        body,
        mesh=grid,
        in_specs=(tokens, tokens, tokens, tokens, P("pipe", "head", seq), P("pipe", seq), P("pipe", None, "head")),
        out_specs=(tokens, tokens, tokens, tokens),
        check_vma=False,
    )
```

time: 298 us -> 131 us (0.44)
  starting transfers between devices: 158 us -> 14 us
  between operations: 56.3 us -> 14.1 us
  blocking collectives: 0 us -> 39.7 us
  Pallas kernels: 0 us -> 25.6 us
  waiting for transfers between devices: 49.7 us -> 34.4 us
  local copies, waits for them, and re-layouts: 16.2 us -> 2.62 us
  matrix products: 9.79 us -> 0 us
  other arithmetic: 6.06 us -> 0 us
    ppermute x41 -> x3, starting transfers between devices: 158 us -> 10.6 us  [the longest x2 5.76 us: relay(): return lax.ppermute(own, 'plane', pairs)]
    ppermute x41 -> x3, waiting for transfers between devices: 49.7 us -> 6.37 us  [the longest x2 6.37 us: relay(): return lax.ppermute(own, 'plane', pairs)]
    all_to_all x0 -> x3, blocking collectives: none -> 39.7 us  [exchange(): return lax.all_to_all(array, 'line', 0, 0, tiled=True)]
    pallas_call x0 -> x8, Pallas kernels: none -> 25.6 us  [the longest x1 8.8 us: body(): pl.pallas_call(weight_kernel, grid=(groups,), in_specs=[whole(n, width),...]
    reduce_scatter x1, waiting for transfers between devices: 0.01 us -> 24.2 us  [body(): lax.psum_scatter(partials, 'head', scatter_dimension=0, tiled=False)]
    dot_general x11 -> x0, matrix products: 9.79 us -> none  [the longest x1 6.31 us: body(): lax.dot_general(weight_local, grad_value, (((1,), (1,)), ((), ())), prefe...]
    slice x15 -> x0, local copies, waits for them, and re-layouts: 9.54 us -> none  [the longest x6 3.78 us: join_forward(): first_id = jnp.where(tags_in[..., 0] < 0, tags_out[..., 0], tags_in[..., 0])]
    all_to_all x0 -> x1, waiting for transfers between devices: none -> 3.76 us  [exchange(): return lax.all_to_all(array, 'line', 0, 0, tiled=True)]
  transfers between devices with their start and end apart: 42 -> 5, of which waited for: 13 -> 4; matrix products, arithmetic and copies ran while one was open for 7% -> 0% of each run, Pallas kernels for 0% -> 8%
where the time goes in v1:
time: 131 us; the launch traced here: 130 us
  blocking collectives  39.7 us (30%)
  waiting for transfers between devices  34.4 us (26%)
  Pallas kernels  25.6 us (20%)
  between operations  14.1 us (11%)
  starting transfers between devices  14 us (11%)
  local copies, waits for them, and re-layouts  2.62 us (2%)
    all_to_all x3, blocking collectives, exchange(): return lax.all_to_all(array, 'line', 0, 0, tiled=True)  39.7 us
    reduce_scatter x1, waiting for transfers between devices, body(): lax.psum_scatter(partials, 'head', scatter_dimension=0, tiled=False)  24.2 us
    pallas_call x1, Pallas kernels, body(): pl.pallas_call(weight_kernel, grid=(groups,), in_specs=[whole(n, width),...  8.8 us
    ppermute x2, waiting for transfers between devices, relay(): return lax.ppermute(own, 'plane', pairs)  6.37 us
    ppermute x2, starting transfers between devices, relay(): return lax.ppermute(own, 'plane', pairs)  5.76 us
    ppermute x1, starting transfers between devices, body(): lax.ppermute(summed, 'pipe', [((i + 1) % sections, i) for i in range(sect...  4.84 us
    pallas_call x1, Pallas kernels, body(): call(forward_local_kernel, (message, jax.ShapeDtypeStruct((n, width), f32...  4.03 us
    all_to_all x1, waiting for transfers between devices, exchange(): return lax.all_to_all(array, 'line', 0, 0, tiled=True)  3.76 us
  transfers between devices with their start and end apart: 5, of which 4 were waited for; matrix products, arithmetic and copies ran while one was open for 0% of the time, Pallas kernels for 8%

profile of v1, /device:TPU:1, one launch (start us, length us, event | category | flops | bytes accessed | tf_op | source)
XLA Modules:
  0.0 130.3 jit_solution(10470460827392196314)
XLA Ops:
  7.2 2.6 %backward_local.1 = bf16[8,80,128]{2,1,0:T(8,128)(2,1)} custom-call(bf16[1,256,512]{2,1,0:T(8,128)(2,1)} %q.5, bf16[1,256,512]{2,1,0:T(8,128)(2,1)} %o.5, f32[1,4,256]{2,1,0:T(4,128)} %rates.5, s32[1,256]{1,0:T(1,128)} %seg_row.5), custom_call_target="tpu_custom_call" | custom-call | tf_op jit(solution)/shard_map/backward_local/pallas_call | solution.py:209
  9.8 16.5 %all_to_all.20.refs_0_ = bf16[8,80,128]{2,1,0:T(8,128)(2,1)} all-to-all(bf16[8,80,128]{2,1,0:T(8,128)(2,1)} %backward_local.1), channel_id=1, replica_groups=mesh['plane'=8,'line'=8,'head'=8,'pipe'=2] {'line'}, dimensions={0} | all-to-all | bytes 327680 | tf_op jit(solution)/shard_map/all_to_all | solution.py:198
  26.2 1.6 %total_backward.1 = bf16[80,128]{1,0:T(8,128)(2,1)} custom-call(bf16[8,80,128]{2,1,0:T(8,128)(2,1)} %all_to_all.20.refs_0_), custom_call_target="tpu_custom_call" | custom-call | tf_op jit(solution)/shard_map/total_backward/pallas_call | solution.py:201
  27.8 1.3 collective-permute-start
  29.1 5.3 %collective-permute-done.refs_1_ = bf16[80,128]{1,0:T(8,128)(2,1)S(1)} collective-permute-done((bf16[80,128]{1,0:T(8,128)(2,1)}, bf16[80,128]{1,0:T(8,128)(2,1)S(1)}, u32[]{:S(2)}, u32[]{:S(2)}) %collective-permute-start) | collective-permute-done | bytes 20512 | tf_op jit(solution)/shard_map/ppermute | solution.py:203
  34.4 0.6 copy-done.2
  35.0 1.6 %scan_backward.1 = bf16[8,64,128]{2,1,0:T(8,128)(2,1)} custom-call(bf16[8,80,128]{2,1,0:T(8,128)(2,1)} %all_to_all.20.refs_0_, bf16[80,128]{1,0:T(8,128)(2,1)} %copy-done.2), custom_call_target="tpu_custom_call" | custom-call | tf_op jit(solution)/shard_map/scan_backward/pallas_call | solution.py:206
  36.6 3.4 %all-to-all-start.1 = ((bf16[8,64,128]{2,1,0:T(8,128)(2,1)}), bf16[8,64,128]{2,1,0:T(8,128)(2,1)S(1)}, u32[]{:S(2)}, u32[]{:S(2)}) async-start(bf16[8,64,128]{2,1,0:T(8,128)(2,1)} %scan_backward.1), calls=%async_computation.1 | async-start | bytes 262144 | tf_op jit(solution)/shard_map/all_to_all | solution.py:198
  40.0 0.0 reduce-scatter.2.cloned.1.call-start
  40.0 4.0 %forward_local.1 = (bf16[8,80,128]{2,1,0:T(8,128)(2,1)}, f32[256,512]{1,0:T(8,128)}, f32[256,512]{1,0:T(8,128)}) custom-call(bf16[1,256,512]{2,1,0:T(8,128)(2,1)} %q.5, bf16[1,256,512]{2,1,0:T(8,128)(2,1)} %k.5, bf16[1,256,512]{2,1,0:T(8,128)(2,1)} %v.3, bf16[1,256,512]{2,1,0:T(8,128)(2,1)} %o.5, f32[1,4,256]{2,1,0:T(4,128)} %rates.5, s32[1,256]{1,0:T(1,128)} %seg_row.5), custom_call_target="tpu_custom_call" | custom-call | tf_op jit(solution)/shard_map/forward_local/pallas_call | solution.py:212
  44.1 3.8 %all-to-all-done.1 = bf16[8,64,128]{2,1,0:T(8,128)(2,1)S(1)} async-done(((bf16[8,64,128]{2,1,0:T(8,128)(2,1)}), bf16[8,64,128]{2,1,0:T(8,128)(2,1)S(1)}, u32[]{:S(2)}, u32[]{:S(2)}) %all-to-all-start.1) | async-done | bytes 131104 | tf_op jit(solution)/shard_map/all_to_all | solution.py:198
  47.8 0.7 copy-done
  48.5 8.8 %weight.1 = (bf16[256,512]{1,0:T(8,128)(2,1)}, bf16[8,256,768]{2,1,0:T(8,128)(2,1)}) custom-call(f32[256,512]{1,0:T(8,128)} %get-tuple-element.16.local, f32[256,512]{1,0:T(8,128)} %get-tuple-element.17.gain, bf16[1,256,512]{2,1,0:T(8,128)(2,1)} %k.5, bf16[512,128]{1,0:T(8,128)(2,1)} %bitcast.9, bf16[8,768,512]{2,1,0:T(8,128)(2,1)} %bitcast.8), custom_call_target="tpu_custom_call" | custom-call | tf_op jit(solution)/shard_map/weight/pallas_call | solution.py:221
  57.3 11.3 %all_to_all.21.refs_0_ = bf16[8,80,128]{2,1,0:T(8,128)(2,1)} all-to-all(bf16[8,80,128]{2,1,0:T(8,128)(2,1)S(1)} %copy-done.1), channel_id=1, replica_groups=mesh['plane'=8,'line'=8,'head'=8,'pipe'=2] {'line'}, dimensions={0} | all-to-all | bytes 327680 | tf_op jit(solution)/shard_map/all_to_all | solution.py:198
  68.6 1.6 %total_forward.1 = bf16[80,128]{1,0:T(8,128)(2,1)} custom-call(bf16[8,80,128]{2,1,0:T(8,128)(2,1)} %all_to_all.21.refs_0_), custom_call_target="tpu_custom_call" | custom-call | tf_op jit(solution)/shard_map/total_forward/pallas_call | solution.py:201
  70.2 4.5 %collective-permute-start.1 = (bf16[80,128]{1,0:T(8,128)(2,1)}, bf16[80,128]{1,0:T(8,128)(2,1)S(1)}, u32[]{:S(2)}, u32[]{:S(2)}) collective-permute-start(bf16[80,128]{1,0:T(8,128)(2,1)} %total_forward.1), channel_id=1, source_target_pairs={{0,128},{128,256},{256,384},{384,512},{512,640},{640,768},{768,896... | collective-permute-start | bytes 61448 | tf_op jit(solution)/shard_map/ppermute | solution.py:203
  74.7 1.1 collective-permute-done.1.refs_1_
  75.8 0.6 copy-done.3
  76.4 1.6 %scan_forward.1 = bf16[8,64,128]{2,1,0:T(8,128)(2,1)} custom-call(bf16[8,80,128]{2,1,0:T(8,128)(2,1)} %all_to_all.21.refs_0_, bf16[80,128]{1,0:T(8,128)(2,1)} %copy-done.3), custom_call_target="tpu_custom_call" | custom-call | tf_op jit(solution)/shard_map/scan_forward/pallas_call | solution.py:206
  78.0 11.9 %all_to_all.22 = bf16[8,64,128]{2,1,0:T(8,128)(2,1)} all-to-all(bf16[8,64,128]{2,1,0:T(8,128)(2,1)} %scan_forward.1), channel_id=1, replica_groups=mesh['plane'=8,'line'=8,'head'=8,'pipe'=2] {'line'}, dimensions={0} | all-to-all | bytes 262144 | tf_op jit(solution)/shard_map/all_to_all | solution.py:198
  89.9 24.2 %reduce-scatter.2.cloned.1.call-done = bf16[1,256,768]{2,1,0:T(8,128)(2,1)} async-done(((bf16[8,256,768]{2,1,0:T(8,128)(2,1)}), bf16[1,256,768]{2,1,0:T(8,128)(2,1)}) %reduce-scatter.2.cloned.1.call-update) | async-done | bytes 393232 | tf_op jit(solution)/shard_map/reduce_scatter | solution.py:240
  114.1 4.8 %collective-permute-start.2 = (bf16[256,768]{1,0:T(8,128)(2,1)}, bf16[256,768]{1,0:T(8,128)(2,1)S(1)}, u32[]{:S(2)}, u32[]{:S(2)}) collective-permute-start(bf16[256,768]{1,0:T(8,128)(2,1)} %bitcast.13), channel_id=1, source_target_pairs={{1,0},{0,1},{3,2},{2,3},{5,4},{4,5},{7,6},{6,7},{9,8},{8,9},{11,10... | collective-permute-start | bytes 1179656 | tf_op jit(solution)/shard_map/ppermute | solution.py:252
  119.0 3.8 %query_key.1 = (bf16[256,512]{1,0:T(8,128)(2,1)}, bf16[256,512]{1,0:T(8,128)(2,1)}) custom-call(bf16[1,256,512]{2,1,0:T(8,128)(2,1)} %q.5, bf16[1,256,512]{2,1,0:T(8,128)(2,1)} %k.5, bf16[1,256,512]{2,1,0:T(8,128)(2,1)} %v.3, bf16[1,256,512]{2,1,0:T(8,128)(2,1)} %o.5, f32[1,4,256]{2,1,0:T(4,128)} %rates.5, s32[1,256]{1,0:T(1,128)} %seg_row.5, ...), custom_call_target="tpu_custom_call" | custom-call | tf_op jit(solution)/shard_map/query_key/pallas_call | solution.py:245
  122.7 0.7 copy.12
  (7 shorter events, 0.0 us)
Async XLA Ops:
  27.8 6.6 %collective-permute-start = (bf16[80,128]{1,0:T(8,128)(2,1)}, bf16[80,128]{1,0:T(8,128)(2,1)S(1)}, u32[]{:S(2)}, u32[]{:S(2)}) collective-permute-start(bf16[80,128]{1,0:T(8,128)(2,1)} %total_backward.1), channel_id=1, source_target_pairs={{128,0},{256,128},{384,256},{512,384},{640,512},{768,640},{896,768... | collective-permute-start | bytes 61448 | tf_op jit(solution)/shard_map/ppermute | solution.py:203
  34.4 0.6 copy-start.2
  36.6 11.2 %all-to-all-start.1 = ((bf16[8,64,128]{2,1,0:T(8,128)(2,1)}), bf16[8,64,128]{2,1,0:T(8,128)(2,1)S(1)}, u32[]{:S(2)}, u32[]{:S(2)}) async-start(bf16[8,64,128]{2,1,0:T(8,128)(2,1)} %scan_backward.1), calls=%async_computation.1 | async-start | bytes 262144 | tf_op jit(solution)/shard_map/all_to_all | solution.py:198
  40.0 74.2 %reduce-scatter.2.cloned.1.call-start = ((), (), s32[]{:S(2)}) async-start(), calls=%async_computation.5 | async-start | bytes 3538944 | tf_op jit(solution)/shard_map/reduce_scatter | solution.py:240
  44.1 13.2 %copy-start.1 = (bf16[8,80,128]{2,1,0:T(8,128)(2,1)S(1)}, bf16[8,80,128]{2,1,0:T(8,128)(2,1)}, u32[]{:S(2)}) copy-start(bf16[8,80,128]{2,1,0:T(8,128)(2,1)} %get-tuple-element.20) | copy-start | bytes 491524
  47.8 0.7 copy-start
  70.2 5.6 %collective-permute-start.1 = (bf16[80,128]{1,0:T(8,128)(2,1)}, bf16[80,128]{1,0:T(8,128)(2,1)S(1)}, u32[]{:S(2)}, u32[]{:S(2)}) collective-permute-start(bf16[80,128]{1,0:T(8,128)(2,1)} %total_forward.1), channel_id=1, source_target_pairs={{0,128},{128,256},{256,384},{384,512},{512,640},{640,768},{768,896... | collective-permute-start | bytes 61448 | tf_op jit(solution)/shard_map/ppermute | solution.py:203
  75.8 0.6 copy-start.3
  114.1 8.6 %collective-permute-start.2 = (bf16[256,768]{1,0:T(8,128)(2,1)}, bf16[256,768]{1,0:T(8,128)(2,1)S(1)}, u32[]{:S(2)}, u32[]{:S(2)}) collective-permute-start(bf16[256,768]{1,0:T(8,128)(2,1)} %bitcast.13), channel_id=1, source_target_pairs={{1,0},{0,1},{3,2},{2,3},{5,4},{4,5},{7,6},{6,7},{9,8},{8,9},{11,10... | collective-permute-start | bytes 1179656 | tf_op jit(solution)/shard_map/ppermute | solution.py:252
Sparse Core Ops, SparseCore 0:
  57.4 56.6 reduce-scatter.1

commit v2 on v1

--- a/solution.py
+++ b/solution.py
@@ -58,14 +58,26 @@
     return seg[0:1, :], seg[n - 1 : n, :]
 
 
-def backward_local_kernel(q, o, rates, seg_row, out):
+def fetch(sources, targets, sems):
+    copies = [pltpu.make_async_copy(src, dst, sems.at[i]) for i, (src, dst) in enumerate(zip(sources, targets))]
+    for copy in copies:
+        copy.start()
+    return copies
+
+
+def backward_local_kernel(rates_in, seg_in, q_in, o_in, out, rates, seg_row, q, o, sems):
+    rates_copy, seg_copy, q_copy, o_copy = fetch((rates_in, seg_in, q_in, o_in), (rates, seg_row, q, o), sems)
+    rates_copy.wait()
     cum = cumulative_columns(rates[0])
     heads = rates.shape[1]
     n = cum.shape[0]
     dh = q.shape[2] // heads
+    seg_copy.wait()
     seg = ids_column(seg_row)
     first, last = block_ids(seg)
     scale = jnp.where(seg == seg[0:1, :], jnp.exp(cum), 0.0)
+    q_copy.wait()
+    o_copy.wait()
     for h in range(heads):
         cols = slice(h * dh, (h + 1) * dh)
         scaled = (q[0, :, cols].astype(f32) * scale[:, h : h + 1]).astype(bf16)
@@ -81,16 +93,24 @@
     return jnp.exp(jnp.where(keep, cum_col - cum_row, NEVER))
 
 
-def forward_local_kernel(q, k, v, o, rates, seg_row, out, gv, gain):
+def forward_local_kernel(
+    rates_in, seg_in, k_in, v_in, q_in, o_in, out, gv, gain, k, rates, seg_row, v, q, o, sems
+):
+    sources = (rates_in, seg_in, k_in, v_in, q_in, o_in)
+    rates_copy, seg_copy, *others = fetch(sources, (rates, seg_row, k, v, q, o), sems)
+    rates_copy.wait()
     cum = cumulative_columns(rates[0])
     cum_t = cumulative_rows(rates[0])
     heads = rates.shape[1]
     n = cum.shape[0]
     dh = q.shape[2] // heads
+    seg_copy.wait()
     seg = ids_column(seg_row)
     first, last = block_ids(seg)
     keep = (iota2(n, 1) <= iota2(n, 0)) & (seg == seg_row[...].astype(f32))
     scale = jnp.where(seg == seg[n - 1 : n, :], jnp.exp(cum[n - 1 : n, :] - cum), 0.0)
+    for copy in others:
+        copy.wait()
     for h in range(heads):
         cols = slice(h * dh, (h + 1) * dh)
         kh = k[0, :, cols]
@@ -100,7 +120,7 @@
         weight = decay_weight(cum[:, h : h + 1], cum_t[h : h + 1, :], keep)
         ks = scores(q[0, :, cols], kh, weight)
         gv[:, cols] = dot(ks, o[0, :, cols], ((0,), (0,)))
-        gain[:, h * dh : (h + 1) * dh] = jnp.broadcast_to(scale[:, h : h + 1], (n, dh))
+        gain[:, cols] = jnp.broadcast_to(scale[:, h : h + 1], (n, dh))
 
 
 def unpack(msg, y):
@@ -142,23 +162,42 @@
         tag = first if reverse else last
 
 
-def weight_kernel(local, gain, k, state, w, gv, out, kept):
+LOADS = 4
+
+
+def weight_kernel(local, gain, k, state, w_in, gv, out, kept, w, made, in_sems, out_sems):
+    pieces = w.shape[0]
+    loads = fetch([w_in.at[0, i] for i in range(pieces)], [w.at[i] for i in range(pieces)], in_sems)
     heads = gv.shape[1] // state.shape[1]
     dh = state.shape[1]
-
-    @pl.when(pl.program_id(0) == 0)
-    def _():
-        for h in range(heads):
-            cols = slice(h * dh, (h + 1) * dh)
-            b = state[h * dh : (h + 1) * dh, :]
-            far = dot(k[0, :, cols], b, ((1,), (0,)))
-            kept[:, cols] = (local[:, cols] + gain[:, cols] * far).astype(bf16)
-        gv[...] = kept[...]
-
-    out[0] = dot(kept[...], w[0], ((1,), (1,))).astype(bf16)
-
-
-def query_key_kernel(q, k, v, o, rates, seg_row, fwd, bwd, gain, dq, dk):
+    for h in range(heads):
+        cols = slice(h * dh, (h + 1) * dh)
+        b = state[h * dh : (h + 1) * dh, :]
+        far = dot(k[0, :, cols], b, ((1,), (0,)))
+        kept[:, cols] = (local[:, cols] + gain[:, cols] * far).astype(bf16)
+    gv[...] = kept[...]
+    step = out.shape[2]
+    each = out.shape[0] // pieces
+    copies = []
+    for i in range(pieces):
+        loads[i].wait()
+        for j in range(each):
+            rows = w[i, j * step : (j + 1) * step, :]
+            made[i * each + j] = dot(kept[...], rows, ((1,), (1,))).astype(bf16)
+        span = pl.ds(i * each, each)
+        copy = pltpu.make_async_copy(made.at[span], out.at[span], out_sems.at[i])
+        copy.start()
+        copies.append(copy)
+    for copy in copies:
+        copy.wait()
+
+
+def query_key_kernel(
+    rates_in, seg_in, q_in, k_in, v_in, o_in, fwd, bwd, gain, dq, dk, rates, seg_row, q, k, v, o, sems
+):
+    sources = (rates_in, seg_in, q_in, k_in, v_in, o_in)
+    for copy in fetch(sources, (rates, seg_row, q, k, v, o), sems):
+        copy.wait()
     cum = cumulative_columns(rates[0])
     cum_t = cumulative_rows(rates[0])
     heads = rates.shape[1]
@@ -179,8 +218,25 @@
         dk[:, cols] = (dot(vs, q[0, :, cols], ((0,), (0,))) + gain[:, cols] * far_k).astype(bf16)
 
 
-def call(kernel, shapes, name):
-    return pl.pallas_call(kernel, out_shape=shapes, name=name)
+IN_VMEM = pl.BlockSpec(memory_space=pltpu.VMEM)
+IN_HBM = pl.BlockSpec(memory_space=pltpu.HBM)
+
+
+def call(kernel, shapes, name, mib=4, in_specs=None, out_specs=IN_VMEM, scratch=()):
+    def run(*args):
+        specs = in_specs or [IN_VMEM] * len(args)
+        args = [pltpu.with_memory_space_constraint(a, pltpu.HBM) if spec is IN_HBM else a for a, spec in zip(args, specs)]
+        return pl.pallas_call(
+            kernel,
+            in_specs=specs,
+            out_specs=jax.tree.map(lambda _: IN_VMEM, shapes) if out_specs is IN_VMEM else out_specs,
+            out_shape=shapes,
+            scratch_shapes=scratch,
+            compiler_params=pltpu.CompilerParams(vmem_limit_bytes=mib << 20),
+            name=name,
+        )(*args)
+
+    return run
 
 
 def body(queries, keys, values, out_grad, log_decay, segment_ids, w_value):
@@ -192,7 +248,7 @@
     share = heads * dh // ROW
     message = jax.ShapeDtypeStruct((ROW, share + META, dh), bf16)
     total = jax.ShapeDtypeStruct((share + META, dh), bf16)
-    states = jax.ShapeDtypeStruct((ROW, share, dh), bf16)
+    states = pltpu.VMEM((ROW, share, dh), bf16)
 
     def exchange(array):
         return lax.all_to_all(array, "line", 0, 0, tiled=True)
@@ -206,48 +262,69 @@
         out = call(lambda *refs: row_scan_kernel(reverse, *refs), states, "scan_" + tag)(msg, carried)
         return exchange(out).reshape(heads * dh, dh)
 
-    sent = call(backward_local_kernel, message, "backward_local")(queries, out_grad, log_decay, segment_ids)
+    block = pltpu.VMEM((1, n, width), bf16)
+    small = [pltpu.VMEM(log_decay.shape, f32), pltpu.VMEM(segment_ids.shape, jnp.int32)]
+    sent = call(
+        backward_local_kernel,
+        message,
+        "backward_local",
+        mib=12,
+        in_specs=[IN_HBM] * 4,
+        scratch=[*small, block, block, pltpu.SemaphoreType.DMA((4,))],
+    )(log_decay, segment_ids, queries, out_grad)
     got = exchange(sent)
     carried = relay(got, True, "backward")
-    fwd_sent, gv_local, gain = call(
+    fwd_sent, gv_local, gain, keys_near = call(
         forward_local_kernel,
-        (message, jax.ShapeDtypeStruct((n, width), f32), jax.ShapeDtypeStruct((n, width), f32)),
+        (
+            message,
+            pltpu.VMEM((n, width), f32),
+            pltpu.VMEM((n, width), f32),
+            block,
+        ),
         "forward_local",
-    )(queries, keys, values, out_grad, log_decay, segment_ids)
+        mib=12,
+        in_specs=[IN_HBM] * 6,
+        scratch=[*small, block, block, block, pltpu.SemaphoreType.DMA((6,))],
+    )(log_decay, segment_ids, keys, values, queries, out_grad)
     bwd = scan(got, carried, True, "backward")
 
-    slice_rows = w_value.shape[1] // groups
-    whole = lambda *shape: pl.BlockSpec(shape, lambda i: (0,) * len(shape))
-    grad_value, partials = pl.pallas_call(
+    step = w_value.shape[1] // groups
+    pieces = LOADS if groups % LOADS == 0 else 1
+    piece_rows = w_value.shape[1] // pieces
+    grad_value, partials = call(
         weight_kernel,
-        grid=(groups,),
-        in_specs=[
-            whole(n, width),
-            whole(n, width),
-            whole(1, n, width),
-            whole(heads * dh, dh),
-            pl.BlockSpec((1, slice_rows, width), lambda i: (i, 0, 0)),
+        (
+            jax.ShapeDtypeStruct((n, width), bf16),
+            jax.ShapeDtypeStruct((groups, n, step), bf16),
+        ),
+        "weight",
+        mib=18,
+        in_specs=[IN_VMEM] * 4 + [IN_HBM],
+        out_specs=(IN_VMEM, IN_HBM),
+        scratch=[
+            pltpu.VMEM((n, width), bf16),
+            pltpu.VMEM((pieces, piece_rows, width), bf16),
+            pltpu.VMEM((groups, n, step), bf16),
+            pltpu.SemaphoreType.DMA((pieces,)),
+            pltpu.SemaphoreType.DMA((pieces,)),
         ],
-        out_specs=[whole(n, width), pl.BlockSpec((1, n, slice_rows), lambda i: (i, 0, 0))],
-        out_shape=(
-            jax.ShapeDtypeStruct((n, width), bf16),
-            jax.ShapeDtypeStruct((groups, n, slice_rows), bf16),
-        ),
-        scratch_shapes=[pltpu.VMEM((n, width), bf16)],
-        name="weight",
-    )(gv_local, gain, keys, bwd, w_value.reshape(groups, slice_rows, width))
+    )(gv_local, gain, keys_near, bwd, w_value.reshape(1, pieces, piece_rows, width))
     fwd_sent, partials = lax.optimization_barrier((fwd_sent, partials))
     summed = lax.psum_scatter(partials, "head", scatter_dimension=0, tiled=False)
 
     fwd_got = exchange(fwd_sent)
     fwd = scan(fwd_got, relay(fwd_got, False, "forward"), False, "forward")
-    summed, fwd = lax.optimization_barrier((summed, fwd))
     grad_query, grad_key = call(
         query_key_kernel,
         (jax.ShapeDtypeStruct((n, width), bf16), jax.ShapeDtypeStruct((n, width), bf16)),
         "query_key",
-    )(queries, keys, values, out_grad, log_decay, segment_ids, fwd, bwd, gain)
-
+        mib=12,
+        in_specs=[IN_HBM] * 6 + [IN_VMEM] * 3,
+        scratch=[*small, block, block, block, block, pltpu.SemaphoreType.DMA((6,))],
+    )(log_decay, segment_ids, queries, keys, values, out_grad, fwd, bwd, gain)
+
+    summed, grad_query, grad_key = lax.optimization_barrier((summed, grad_query, grad_key))
     sections = lax.axis_size("pipe")
     shifted = lax.ppermute(summed, "pipe", [((i + 1) % sections, i) for i in range(sections)])
     return (grad_query[None], grad_key[None], grad_value[None], shifted[None])

time: 131 us -> 120 us (0.916)
  Pallas kernels: 25.6 us -> 14.5 us
  waiting for transfers between devices: 34.4 us -> 38.9 us
  blocking collectives: 39.7 us -> 37.2 us
  local copies, waits for them, and re-layouts: 2.62 us -> 0.75 us
    pallas_call x8, Pallas kernels: 25.6 us -> 14.5 us  [run(): pl.pallas_call(kernel, in_specs=specs, out_specs=jax.tree.map(lambda _: I...]
    all_to_all x3, blocking collectives: 39.7 us -> 37.2 us  [exchange(): return lax.all_to_all(array, 'line', 0, 0, tiled=True)]
    reduce_scatter x1, waiting for transfers between devices: 24.2 us -> 26.4 us  [body(): lax.psum_scatter(partials, 'head', scatter_dimension=0, tiled=False)]
    unnamed x9 -> x1, local copies, waits for them, and re-layouts: 2.62 us -> 0.75 us
    ppermute x1, waiting for transfers between devices: 0.01 us -> 1.54 us  [body(): lax.ppermute(summed, 'pipe', [((i + 1) % sections, i) for i in range(sect...]
    all_to_all x1, waiting for transfers between devices: 3.76 us -> 5.08 us  [exchange(): return lax.all_to_all(array, 'line', 0, 0, tiled=True)]
  transfers between devices with their start and end apart: 5 -> 5, of which waited for: 4 -> 5; matrix products, arithmetic and copies ran while one was open for 0% -> 0% of each run, Pallas kernels for 8% -> 5%
where the time goes in v2:
time: 120 us
  waiting for transfers between devices  38.9 us (32%)
  blocking collectives  37.2 us (31%)
  Pallas kernels  14.5 us (12%)
  starting transfers between devices  14.2 us (12%)
  between operations  14.1 us (12%)
    all_to_all x3, blocking collectives, exchange(): return lax.all_to_all(array, 'line', 0, 0, tiled=True)  37.2 us
    reduce_scatter x1, waiting for transfers between devices, body(): lax.psum_scatter(partials, 'head', scatter_dimension=0, tiled=False)  26.4 us
    pallas_call x8, Pallas kernels, run(): pl.pallas_call(kernel, in_specs=specs, out_specs=jax.tree.map(lambda _: I...  14.5 us
    ppermute x2, starting transfers between devices, relay(): return lax.ppermute(own, 'plane', pairs)  5.9 us
    ppermute x2, waiting for transfers between devices, relay(): return lax.ppermute(own, 'plane', pairs)  5.82 us
    all_to_all x1, waiting for transfers between devices, exchange(): return lax.all_to_all(array, 'line', 0, 0, tiled=True)  5.08 us
    ppermute x1, starting transfers between devices, body(): lax.ppermute(summed, 'pipe', [((i + 1) % sections, i) for i in range(sect...  4.86 us
    all_to_all x1, starting transfers between devices, exchange(): return lax.all_to_all(array, 'line', 0, 0, tiled=True)  3.37 us
  transfers between devices with their start and end apart: 5, of which 5 were waited for; matrix products, arithmetic and copies ran while one was open for 0% of the time, Pallas kernels for 5%

profile of v2, /device:TPU:1, one launch (start us, length us, event | category | flops | bytes accessed | tf_op | source)
XLA Modules:
  0.0 119.5 jit_solution(15879577691500652207)
XLA Ops:
  7.2 1.8 %backward_local.1 = bf16[8,80,128]{2,1,0:T(8,128)(2,1)S(1)} custom-call(f32[1,4,256]{2,1,0:T(4,128)} %rates_in.5, s32[1,256]{1,0:T(1,128)} %seg_in.5, bf16[1,256,512]{2,1,0:T(8,128)(2,1)} %q_in.5, bf16[1,256,512]{2,1,0:T(8,128)(2,1)} %o_in.5), custom_call_target="tpu_custom_call" | custom-call | tf_op jit(solution)/shard_map/backward_local/pallas_call | solution.py:229
  9.0 16.2 %all_to_all.20.refs_0_ = bf16[8,80,128]{2,1,0:T(8,128)(2,1)S(1)} all-to-all(bf16[8,80,128]{2,1,0:T(8,128)(2,1)S(1)} %backward_local.1), channel_id=1, replica_groups=mesh['plane'=8,'line'=8,'head'=8,'pipe'=2] {'line'}, dimensions={0} | all-to-all | bytes 327680 | tf_op jit(solution)/shard_map/all_to_all | solution.py:254
  25.2 1.3 %collective-permute-start = (bf16[80,128]{1,0:T(8,128)(2,1)S(1)}, bf16[80,128]{1,0:T(8,128)(2,1)S(1)}, u32[]{:S(2)}, u32[]{:S(2)}) collective-permute-start(bf16[80,128]{1,0:T(8,128)(2,1)S(1)} %total_backward.1), channel_id=1, source_target_pairs={{128,0},{256,128},{384,256},{512,384},{640,512},{768,640},{896,768... | collective-permute-start | bytes 61448 | tf_op jit(solution)/shard_map/ppermute | solution.py:259
  26.5 4.9 %collective-permute-done.refs_1_ = bf16[80,128]{1,0:T(8,128)(2,1)S(1)} collective-permute-done((bf16[80,128]{1,0:T(8,128)(2,1)S(1)}, bf16[80,128]{1,0:T(8,128)(2,1)S(1)}, u32[]{:S(2)}, u32[]{:S(2)}) %collective-permute-start) | collective-permute-done | bytes 20512 | tf_op jit(solution)/shard_map/ppermute | solution.py:259
  31.5 0.7 scan_backward.1
  32.2 3.4 %all-to-all-start.1 = ((bf16[8,64,128]{2,1,0:T(8,128)(2,1)}), bf16[8,64,128]{2,1,0:T(8,128)(2,1)S(1)}, u32[]{:S(2)}, u32[]{:S(2)}) async-start(bf16[8,64,128]{2,1,0:T(8,128)(2,1)} %scan_backward.1), calls=%async_computation.1 | async-start | bytes 262144 | tf_op jit(solution)/shard_map/all_to_all | solution.py:254
  35.6 0.0 reduce-scatter.2.cloned.1.call-start
  35.6 2.7 %forward_local.1 = (bf16[8,80,128]{2,1,0:T(8,128)(2,1)S(1)}, f32[256,512]{1,0:T(8,128)S(1)}, f32[256,512]{1,0:T(8,128)S(1)}, bf16[1,256,512]{2,1,0:T(8,128)(2,1)S(1)}) custom-call(f32[1,4,256]{2,1,0:T(4,128)} %rates_in.5, s32[1,256]{1,0:T(1,128)} %seg_in.5, bf16[1,256,512]{2,1,0:T(8,128)(2,1)} %k_in.3, bf16[1,256,512]{2,1,0:T(8,128)(2,1)} %v_in.3, ...), custom_call_target="tpu_custom_call" | custom-call | tf_op jit(solution)/shard_map/forward_local/pallas_call | solution.py:229
  38.3 5.1 %all-to-all-done.1 = bf16[8,64,128]{2,1,0:T(8,128)(2,1)S(1)} async-done(((bf16[8,64,128]{2,1,0:T(8,128)(2,1)}), bf16[8,64,128]{2,1,0:T(8,128)(2,1)S(1)}, u32[]{:S(2)}, u32[]{:S(2)}) %all-to-all-start.1) | async-done | bytes 131104 | tf_op jit(solution)/shard_map/all_to_all | solution.py:254
  43.4 5.6 %weight.1 = (bf16[256,512]{1,0:T(8,128)(2,1)}, bf16[8,256,768]{2,1,0:T(8,128)(2,1)}) custom-call(f32[256,512]{1,0:T(8,128)S(1)} %get-tuple-element.18.local, f32[256,512]{1,0:T(8,128)S(1)} %get-tuple-element.19.gain, bf16[1,256,512]{2,1,0:T(8,128)(2,1)S(1)} %get-tuple-element.20.k, bf16[512,128]{1,0:T(8,128)(2,1)S(1)} %bitcast.8, ...), custom_call_target="tpu_custom_call" | custom-call | tf_op jit(solution)/shard_map/weight/pallas_call | solution.py:229
  49.0 0.0 reduce-scatter.2.cloned.1.call-update
  49.0 10.7 %all_to_all.21.refs_0_ = bf16[8,80,128]{2,1,0:T(8,128)(2,1)S(1)} all-to-all(bf16[8,80,128]{2,1,0:T(8,128)(2,1)S(1)} %get-tuple-element.23), channel_id=1, replica_groups=mesh['plane'=8,'line'=8,'head'=8,'pipe'=2] {'line'}, dimensions={0} | all-to-all | bytes 327680 | tf_op jit(solution)/shard_map/all_to_all | solution.py:254
  59.7 4.6 %collective-permute-start.1 = (bf16[80,128]{1,0:T(8,128)(2,1)S(1)}, bf16[80,128]{1,0:T(8,128)(2,1)S(1)}, u32[]{:S(2)}, u32[]{:S(2)}) collective-permute-start(bf16[80,128]{1,0:T(8,128)(2,1)S(1)} %total_forward.1), channel_id=1, source_target_pairs={{0,128},{128,256},{256,384},{384,512},{512,640},{640,768},{768,896... | collective-permute-start | bytes 61448 | tf_op jit(solution)/shard_map/ppermute | solution.py:259
  64.3 0.9 collective-permute-done.1.refs_1_
  65.2 0.1 scan_forward.1
  65.3 10.3 %all_to_all.22 = bf16[8,64,128]{2,1,0:T(8,128)(2,1)S(1)} all-to-all(bf16[8,64,128]{2,1,0:T(8,128)(2,1)S(1)} %scan_forward.1), channel_id=1, replica_groups=mesh['plane'=8,'line'=8,'head'=8,'pipe'=2] {'line'}, dimensions={0} | all-to-all | bytes 262144 | tf_op jit(solution)/shard_map/all_to_all | solution.py:254
  75.6 3.5 %query_key.1 = (bf16[256,512]{1,0:T(8,128)(2,1)}, bf16[256,512]{1,0:T(8,128)(2,1)}) custom-call(f32[1,4,256]{2,1,0:T(4,128)} %rates_in.5, s32[1,256]{1,0:T(1,128)} %seg_in.5, bf16[1,256,512]{2,1,0:T(8,128)(2,1)} %q_in.5, bf16[1,256,512]{2,1,0:T(8,128)(2,1)} %k_in.3, bf16[1,256,512]{2,1,0:T(8,128)(2,1)} %v_in.3, bf16[1,256,512]{2,1,0:T(8,128)(2,1)} %o_in.5, ...), custom_call_target="tpu_custom_call" | custom-call | tf_op jit(solution)/shard_map/query_key/pallas_call | solution.py:229
  79.1 26.4 %reduce-scatter.2.cloned.1.call-done = bf16[1,256,768]{2,1,0:T(8,128)(2,1)} async-done(((bf16[8,256,768]{2,1,0:T(8,128)(2,1)}), bf16[1,256,768]{2,1,0:T(8,128)(2,1)}) %reduce-scatter.2.cloned.1.call-update) | async-done | bytes 393232 | tf_op jit(solution)/shard_map/reduce_scatter | solution.py:314
  105.6 4.9 %collective-permute-start.2 = (bf16[256,768]{1,0:T(8,128)(2,1)}, bf16[256,768]{1,0:T(8,128)(2,1)S(1)}, u32[]{:S(2)}, u32[]{:S(2)}) collective-permute-start(bf16[256,768]{1,0:T(8,128)(2,1)} %bitcast.13), channel_id=1, source_target_pairs={{1,0},{0,1},{3,2},{2,3},{5,4},{4,5},{7,6},{6,7},{9,8},{8,9},{11,10... | collective-permute-start | bytes 1179656 | tf_op jit(solution)/shard_map/ppermute | solution.py:329
  110.4 1.5 %collective-permute-done.2 = bf16[256,768]{1,0:T(8,128)(2,1)S(1)} collective-permute-done((bf16[256,768]{1,0:T(8,128)(2,1)}, bf16[256,768]{1,0:T(8,128)(2,1)S(1)}, u32[]{:S(2)}, u32[]{:S(2)}) %collective-permute-start.2) | collective-permute-done | bytes 393248 | tf_op jit(solution)/shard_map/ppermute | solution.py:329
  112.0 0.7 copy.12
  (2 shorter events, 0.1 us)
Async XLA Ops:
  25.2 6.2 %collective-permute-start = (bf16[80,128]{1,0:T(8,128)(2,1)S(1)}, bf16[80,128]{1,0:T(8,128)(2,1)S(1)}, u32[]{:S(2)}, u32[]{:S(2)}) collective-permute-start(bf16[80,128]{1,0:T(8,128)(2,1)S(1)} %total_backward.1), channel_id=1, source_target_pairs={{128,0},{256,128},{384,256},{512,384},{640,512},{768,640},{896,768... | collective-permute-start | bytes 61448 | tf_op jit(solution)/shard_map/ppermute | solution.py:259
  32.2 11.2 %all-to-all-start.1 = ((bf16[8,64,128]{2,1,0:T(8,128)(2,1)}), bf16[8,64,128]{2,1,0:T(8,128)(2,1)S(1)}, u32[]{:S(2)}, u32[]{:S(2)}) async-start(bf16[8,64,128]{2,1,0:T(8,128)(2,1)} %scan_backward.1), calls=%async_computation.1 | async-start | bytes 262144 | tf_op jit(solution)/shard_map/all_to_all | solution.py:254
  35.6 70.0 %reduce-scatter.2.cloned.1.call-start = ((), (), s32[]{:S(2)}) async-start(), calls=%async_computation.5 | async-start | bytes 3538944 | tf_op jit(solution)/shard_map/reduce_scatter | solution.py:314
  59.7 5.5 %collective-permute-start.1 = (bf16[80,128]{1,0:T(8,128)(2,1)S(1)}, bf16[80,128]{1,0:T(8,128)(2,1)S(1)}, u32[]{:S(2)}, u32[]{:S(2)}) collective-permute-start(bf16[80,128]{1,0:T(8,128)(2,1)S(1)} %total_forward.1), channel_id=1, source_target_pairs={{0,128},{128,256},{256,384},{384,512},{512,640},{640,768},{768,896... | collective-permute-start | bytes 61448 | tf_op jit(solution)/shard_map/ppermute | solution.py:259
  105.6 6.4 %collective-permute-start.2 = (bf16[256,768]{1,0:T(8,128)(2,1)}, bf16[256,768]{1,0:T(8,128)(2,1)S(1)}, u32[]{:S(2)}, u32[]{:S(2)}) collective-permute-start(bf16[256,768]{1,0:T(8,128)(2,1)} %bitcast.13), channel_id=1, source_target_pairs={{1,0},{0,1},{3,2},{2,3},{5,4},{4,5},{7,6},{6,7},{9,8},{8,9},{11,10... | collective-permute-start | bytes 1179656 | tf_op jit(solution)/shard_map/ppermute | solution.py:329
Sparse Core Ops, SparseCore 0:
  49.1 56.3 reduce-scatter.1

commit v3 on v2

v3 whole, which is shorter than its diff:
```python
import jax
import jax.numpy as jnp
import numpy as np
from jax import lax
from jax.experimental import pallas as pl
from jax.experimental.pallas import tpu as pltpu
from jax.sharding import Mesh
from jax.sharding import PartitionSpec as P

f32, bf16 = jnp.float32, jnp.bfloat16
HIGHEST = lax.Precision.HIGHEST
ROW = 8
META = 16
NEVER = -1e30


def dot(a, b, dims):
    return lax.dot_general(a, b, (dims, ((), ())), preferred_element_type=f32)


def iota2(n, axis):
    return lax.broadcasted_iota(jnp.int32, (n, n), axis)


def cumulative_columns(rates):
    n = rates.shape[1]
    lower = (iota2(n, 1) <= iota2(n, 0)).astype(f32)
    return lax.dot_general(lower, rates, (((1,), (1,)), ((), ())), precision=HIGHEST, preferred_element_type=f32)


def cumulative_rows(rates):
    n = rates.shape[1]
    upper = (iota2(n, 0) <= iota2(n, 1)).astype(f32)
    return lax.dot_general(rates, upper, (((1,), (0,)), ((), ())), precision=HIGHEST, preferred_element_type=f32)


def write_message(out, h, states, first, last, through, width):
    share = states[0].shape[0] // 2
    high = through.astype(bf16)
    low = (through - high.astype(f32)).astype(bf16)
    row = lax.broadcasted_iota(jnp.int32, (META, width), 0)
    meta = jnp.where(row == 0, first, jnp.where(row == 1, last, 0.0))
    meta = jnp.where(row == 2, high.astype(f32), jnp.where(row == 3, low.astype(f32), meta)).astype(bf16)
    for half in range(2):
        p = 2 * h + half
        for i, state in enumerate(states):
            out[p, i * share : (i + 1) * share, :] = state[half * share : (half + 1) * share].astype(bf16)
        out[p, 2 * share : 2 * share + META, :] = meta


def ids_column(seg_row):
    n = seg_row.shape[1]
    on_diagonal = iota2(n, 0) == iota2(n, 1)
    return jnp.sum(jnp.where(on_diagonal, seg_row[...].astype(f32), 0.0), axis=1, keepdims=True)


def block_ids(seg):
    n = seg.shape[0]
    return seg[0:1, :], seg[n - 1 : n, :]


def fetch(sources, targets, sems):
    copies = [pltpu.make_async_copy(src, dst, sems.at[i]) for i, (src, dst) in enumerate(zip(sources, targets))]
    for copy in copies:
        copy.start()
    return copies


def local_kernel(rates_in, seg_in, q_in, o_in, k_in, v_in, out, rates, seg_row, q, o, k, v, sems):
    sources = (rates_in, seg_in, q_in, o_in, k_in, v_in)
    rates_copy, seg_copy, *others = fetch(sources, (rates, seg_row, q, o, k, v), sems)
    rates_copy.wait()
    cum = cumulative_columns(rates[0])
    heads = rates.shape[1]
    n = cum.shape[0]
    dh = q.shape[2] // heads
    seg_copy.wait()
    seg = ids_column(seg_row)
    first, last = block_ids(seg)
    ahead = jnp.where(seg == seg[0:1, :], jnp.exp(cum), 0.0)
    behind = jnp.where(seg == seg[n - 1 : n, :], jnp.exp(cum[n - 1 : n, :] - cum), 0.0)
    for copy in others:
        copy.wait()
    for h in range(heads):
        cols = slice(h * dh, (h + 1) * dh)
        scaled_q = (q[0, :, cols].astype(f32) * ahead[:, h : h + 1]).astype(bf16)
        scaled_k = (k[0, :, cols].astype(f32) * behind[:, h : h + 1]).astype(bf16)
        states = (dot(scaled_q, o[0, :, cols], ((0,), (0,))), dot(scaled_k, v[0, :, cols], ((0,), (0,))))
        write_message(out, h, states, first, last, jnp.exp(cum[n - 1 : n, h : h + 1]), dh)


def scores(a, b, weight):
    return (dot(a, b, ((1,), (1,))) * weight).astype(bf16)


def decay_weight(cum_col, cum_row, keep):
    return jnp.exp(jnp.where(keep, cum_col - cum_row, NEVER))


def near_kernel(rates_in, seg_in, k_in, q_in, o_in, gv, gain, k, rates, seg_row, q, o, sems):
    sources = (rates_in, seg_in, k_in, q_in, o_in)
    rates_copy, seg_copy, *others = fetch(sources, (rates, seg_row, k, q, o), sems)
    rates_copy.wait()
    cum = cumulative_columns(rates[0])
    cum_t = cumulative_rows(rates[0])
    heads = rates.shape[1]
    n = cum.shape[0]
    dh = q.shape[2] // heads
    seg_copy.wait()
    seg = ids_column(seg_row)
    keep = (iota2(n, 1) <= iota2(n, 0)) & (seg == seg_row[...].astype(f32))
    behind = jnp.where(seg == seg[n - 1 : n, :], jnp.exp(cum[n - 1 : n, :] - cum), 0.0)
    for copy in others:
        copy.wait()
    for h in range(heads):
        cols = slice(h * dh, (h + 1) * dh)
        weight = decay_weight(cum[:, h : h + 1], cum_t[h : h + 1, :], keep)
        ks = scores(q[0, :, cols], k[0, :, cols], weight)
        gv[:, cols] = dot(ks, o[0, :, cols], ((0,), (0,)))
        gain[:, cols] = jnp.broadcast_to(behind[:, h : h + 1], (n, dh))


def unpack(msg, y, reverse):
    share = (msg.shape[1] - META) // 2
    start = 0 if reverse else share
    meta = msg[y, 2 * share : 2 * share + META, :].astype(f32)
    state = msg[y, start : start + share, :].astype(f32)
    return state, meta[0:1], meta[1:2], meta[2:3] + meta[3:4]


def order(reverse):
    return range(ROW - 1, -1, -1) if reverse else range(ROW)


def row_total_kernel(msg, out_backward, out_forward):
    for out, reverse in ((out_backward, True), (out_forward, False)):
        share = out.shape[0] - META
        tag, total = None, None
        for y in order(reverse):
            state, first, last, through = unpack(msg, y, reverse)
            if total is None:
                total = state
            else:
                same = jnp.where((first == last) & (tag == last), through, 0.0)
                total = same * total + state
            tag = first if reverse else last
        out[0:share, :] = total.astype(bf16)
        out[share:, :] = jnp.broadcast_to(tag, (META, tag.shape[1])).astype(bf16)


def row_scan_kernel(msg, carried_backward, carried_forward, out):
    for carried, reverse in ((carried_backward, True), (carried_forward, False)):
        share = carried.shape[0] - META
        start = 0 if reverse else share
        running = carried[0:share, :].astype(f32)
        tag = carried[share : share + META, :].astype(f32)[0:1]
        for y in order(reverse):
            state, first, last, through = unpack(msg, y, reverse)
            edge = last if reverse else first
            out[y, start : start + share, :] = jnp.where(edge == tag, running, 0.0).astype(bf16)
            same = jnp.where((first == last) & (tag == last), through, 0.0)
            running = same * running + state
            tag = first if reverse else last


def head_state(states, h, reverse):
    share = states.shape[1] // 2
    start = 0 if reverse else share
    return jnp.concatenate([states[2 * h + half, start : start + share, :] for half in range(2)], axis=0)


def far_kernel(me, local, gain, k, states, w_in, gv, low, high, w, sem):
    groups = w_in.shape[0]
    copy = pltpu.make_async_copy(w_in.at[lax.rem(me[0] + groups // 2, groups)], w, sem)
    copy.start()
    dh = states.shape[2]
    for h in range(gv.shape[1] // dh):
        cols = slice(h * dh, (h + 1) * dh)
        far = dot(k[0, :, cols], head_state(states, h, True), ((1,), (0,)))
        gv[:, cols] = (local[:, cols] + gain[:, cols] * far).astype(bf16)
    copy.wait()
    rows = low.shape[0]
    low[...] = dot(gv[0:rows, :], w[...], ((1,), (1,))).astype(bf16)
    high[...] = dot(gv[rows:, :], w[...], ((1,), (1,))).astype(bf16)


def offsets(groups):
    return [sign * far for far in range(groups // 2 - 1, 0, -1) for sign in (-1, 1)] + [0]


def partial_kernel(me, gv, w_in, out, w, sems):
    groups = w_in.shape[0]
    wanted = offsets(groups)
    sources = [w_in.at[lax.rem(me[0] + groups + offset, groups)] for offset in wanted]
    copies = fetch(sources, [w.at[i] for i in range(len(wanted))], sems)
    for i, copy in enumerate(copies):
        copy.wait()
        out[i] = dot(gv[...], w[i], ((1,), (1,))).astype(bf16)


def add_kernel(index, partials, *refs):
    *arrived, out = refs
    total = partials[index].astype(f32)
    for first, ref in arrived:
        rows = ref.shape[0]
        if rows == total.shape[0]:
            total = total + ref[...].astype(f32)
        else:
            kept = [total[0:first], total[first : first + rows] + ref[...].astype(f32), total[first + rows :]]
            total = jnp.concatenate([part for part in kept if part.shape[0]], axis=0)
    out[...] = total.astype(bf16)


def query_key_kernel(
    rates_in, seg_in, q_in, k_in, v_in, o_in, states, gain, dq, dk, rates, seg_row, q, k, v, o, sems
):
    sources = (rates_in, seg_in, q_in, k_in, v_in, o_in)
    for copy in fetch(sources, (rates, seg_row, q, k, v, o), sems):
        copy.wait()
    cum = cumulative_columns(rates[0])
    cum_t = cumulative_rows(rates[0])
    heads = rates.shape[1]
    n = cum.shape[0]
    dh = q.shape[2] // heads
    seg = ids_column(seg_row)
    keep = (iota2(n, 1) <= iota2(n, 0)) & (seg == seg_row[...].astype(f32))
    reach = jnp.where(seg == seg[0:1, :], jnp.exp(cum), 0.0)
    for h in range(heads):
        cols = slice(h * dh, (h + 1) * dh)
        weight = decay_weight(cum[:, h : h + 1], cum_t[h : h + 1, :], keep)
        vs = scores(o[0, :, cols], v[0, :, cols], weight)
        f = head_state(states, h, False)
        b = head_state(states, h, True)
        far_q = dot(o[0, :, cols], f, ((1,), (1,)))
        far_k = dot(v[0, :, cols], b, ((1,), (1,)))
        dq[:, cols] = (dot(vs, k[0, :, cols], ((1,), (0,))) + reach[:, h : h + 1] * far_q).astype(bf16)
        dk[:, cols] = (dot(vs, q[0, :, cols], ((0,), (0,))) + gain[:, cols] * far_k).astype(bf16)


IN_VMEM = pl.BlockSpec(memory_space=pltpu.VMEM)
IN_SMEM = pl.BlockSpec(memory_space=pltpu.SMEM)
IN_HBM = pl.BlockSpec(memory_space=pltpu.HBM)


def call(kernel, shapes, name, mib=4, in_specs=None, out_specs=IN_VMEM, scratch=()):
    def run(*args):
        specs = in_specs or [IN_VMEM] * len(args)
        args = [pltpu.with_memory_space_constraint(a, pltpu.HBM) if spec is IN_HBM else a for a, spec in zip(args, specs)]
        return pl.pallas_call(
            kernel,
            in_specs=specs,
            out_specs=jax.tree.map(lambda _: IN_VMEM, shapes) if out_specs is IN_VMEM else out_specs,
            out_shape=shapes,
            scratch_shapes=scratch,
            compiler_params=pltpu.CompilerParams(vmem_limit_bytes=mib << 20),
            name=name,
        )(*args)

    return run


def body(queries, keys, values, out_grad, log_decay, segment_ids, w_value):
    n, width = queries.shape[1:]
    heads = log_decay.shape[1]
    dh = width // heads
    planes = lax.axis_size("plane")
    groups = lax.axis_size("head")
    share = heads * dh // ROW
    step = w_value.shape[1] // groups
    half = groups // 2
    block = pltpu.VMEM((1, n, width), bf16)
    small = [pltpu.VMEM(log_decay.shape, f32), pltpu.VMEM(segment_ids.shape, jnp.int32)]
    dma = pltpu.SemaphoreType.DMA

    def exchange(array):
        return lax.all_to_all(array, "line", 0, 0, tiled=True)

    sent = call(
        local_kernel,
        pltpu.VMEM((ROW, 2 * share + META, dh), bf16),
        "local",
        mib=12,
        in_specs=[IN_HBM] * 6,
        scratch=[*small, block, block, block, block, dma((6,))],
    )(log_decay, segment_ids, queries, out_grad, keys, values)
    got = exchange(sent)
    total = pltpu.VMEM((share + META, dh), bf16)
    total_backward, total_forward = call(row_total_kernel, (total, total), "row_total")(got)
    up = [(z - 1, z) for z in range(1, planes)]
    down = [(z, z - 1) for z in range(1, planes)]
    carried_backward = lax.ppermute(total_backward, "plane", down)
    carried_forward = lax.ppermute(total_forward, "plane", up)
    scanned = call(row_scan_kernel, pltpu.VMEM((ROW, 2 * share, dh), bf16), "row_scan")(
        got, carried_backward, carried_forward
    )
    states = exchange(scanned)
    gv_local, gain, keys_near = call(
        near_kernel,
        (pltpu.VMEM((n, width), f32), pltpu.VMEM((n, width), f32), block),
        "near",
        mib=12,
        in_specs=[IN_HBM] * 5,
        scratch=[*small, block, block, dma((5,))],
    )(log_decay, segment_ids, keys, queries, out_grad)

    me = lax.axis_index("head").astype(jnp.int32).reshape(1)
    weights = w_value.reshape(groups, step, width)
    piece = pltpu.VMEM((n // 2, step), bf16)
    grad_value, low, high = call(
        far_kernel,
        (pltpu.VMEM((n, width), bf16), piece, piece),
        "far",
        mib=12,
        in_specs=[IN_SMEM] + [IN_VMEM] * 4 + [IN_HBM],
        scratch=[pltpu.VMEM((step, width), bf16), dma],
    )(me, gv_local, gain, keys_near, states, weights)
    partials = call(
        partial_kernel,
        pltpu.VMEM((groups - 1, n, step), bf16),
        "partial",
        mib=16,
        in_specs=[IN_SMEM, IN_VMEM, IN_HBM],
        scratch=[pltpu.VMEM((groups - 1, step, width), bf16), dma((groups - 1,))],
    )(me, grad_value, weights)
    grad_query, grad_key = call(
        query_key_kernel,
        (jax.ShapeDtypeStruct((n, width), bf16), jax.ShapeDtypeStruct((n, width), bf16)),
        "query_key",
        mib=12,
        in_specs=[IN_HBM] * 6 + [IN_VMEM] * 2,
        scratch=[*small, block, block, block, block, dma((6,))],
    )(log_decay, segment_ids, queries, keys, values, out_grad, states, gain)

    before = [(i, (i - 1) % groups) for i in range(groups)]
    after = [(i, (i + 1) % groups) for i in range(groups)]
    firsts = (0, n // 2)

    def add(index, arrived, starts, name):
        def kernel(partials_ref, *refs):
            add_kernel(index, partials_ref, *zip(starts, refs[:-1]), refs[-1])

        return call(kernel, pltpu.VMEM((n, step), bf16), name)(partials, *arrived)

    for i in range(half):
        low = lax.ppermute(low, "head", before)
        high = lax.ppermute(high, "head", after)
        starts = firsts if i == 0 else (0, 0)
        if i == half - 1:
            summed = add(groups - 2, (low, high), starts, "add_last")
        else:
            low = add(2 * i, (low,), starts[:1], "add_low")
            high = add(2 * i + 1, (high,), starts[1:], "add_high")
        if i == 1:
            low, high, grad_query, grad_key = lax.optimization_barrier((low, high, grad_query, grad_key))

    sections = lax.axis_size("pipe")
    shifted = lax.ppermute(summed, "pipe", [((i + 1) % sections, i) for i in range(sections)])
    return (grad_query[None], grad_key[None], grad_value[None], shifted[None])


def solution(mesh):
    ctx, head, pipe = (mesh.shape[name] for name in ("ctx", "head", "pipe"))
    grid = Mesh(np.asarray(mesh.devices).reshape(ctx // ROW, ROW, head, pipe), ("plane", "line", "head", "pipe"))
    seq = ("plane", "line")
    tokens = P("pipe", seq, "head")
    return jax.shard_map(
        body,
        mesh=grid,
        in_specs=(tokens, tokens, tokens, tokens, P("pipe", "head", seq), P("pipe", seq), P("pipe", None, "head")),
        out_specs=(tokens, tokens, tokens, tokens),
        check_vma=False,
    )
```

time: 120 us -> 110 us (0.917)
  starting transfers between devices: 14.2 us -> 47.5 us
  blocking collectives: 37.2 us -> 17.6 us
  between operations: 14.1 us -> 0.86 us
  waiting for transfers between devices: 38.9 us -> 26.4 us
  Pallas kernels: 14.5 us -> 15.8 us
    reduce_scatter x1 -> x0, waiting for transfers between devices: 26.4 us -> none  [body(): lax.psum_scatter(partials, 'head', scatter_dimension=0, tiled=False)]
    ppermute x2 -> x10, starting transfers between devices: 5.9 us -> 31.7 us  [the longest x4 14.3 us: body(): low = lax.ppermute(low, 'head', before)]
    all_to_all x3 -> x1, blocking collectives: 37.2 us -> 17.6 us  [exchange(): return lax.all_to_all(array, 'line', 0, 0, tiled=True)]
    ppermute x2 -> x10, waiting for transfers between devices: 5.82 us -> 18.8 us  [the longest x4 10.7 us: body(): low = lax.ppermute(low, 'head', before)]
    ppermute x1, starting transfers between devices: 4.86 us -> 12.4 us  [body(): lax.ppermute(summed, 'pipe', [((i + 1) % sections, i) for i in range(sect...]
    all_to_all x1, waiting for transfers between devices: 5.08 us -> 6.94 us  [exchange(): return lax.all_to_all(array, 'line', 0, 0, tiled=True)]
    pallas_call x8 -> x14, Pallas kernels: 14.5 us -> 15.8 us  [run(): pl.pallas_call(kernel, in_specs=specs, out_specs=jax.tree.map(lambda _: I...]
  transfers between devices with their start and end apart: 5 -> 12, of which waited for: 5 -> 7; matrix products, arithmetic and copies ran while one was open for 0% -> 1% of each run, Pallas kernels for 5% -> 10%
where the time goes in v3:
time: 110 us
  starting transfers between devices  47.5 us (43%)
  waiting for transfers between devices  26.4 us (24%)
  blocking collectives  17.6 us (16%)
  Pallas kernels  15.8 us (14%)
  local copies, waits for them, and re-layouts  1.45 us (1%)
    all_to_all x1, blocking collectives, exchange(): return lax.all_to_all(array, 'line', 0, 0, tiled=True)  17.6 us
    pallas_call x14, Pallas kernels, run(): pl.pallas_call(kernel, in_specs=specs, out_specs=jax.tree.map(lambda _: I...  15.8 us
    ppermute x4, starting transfers between devices, body(): low = lax.ppermute(low, 'head', before)  14.3 us
    ppermute x1, starting transfers between devices, body(): lax.ppermute(summed, 'pipe', [((i + 1) % sections, i) for i in range(sect...  12.4 us
    ppermute x4, waiting for transfers between devices, body(): low = lax.ppermute(low, 'head', before)  10.7 us
    ppermute x4, starting transfers between devices, body(): high = lax.ppermute(high, 'head', after)  9.35 us
    ppermute x4, waiting for transfers between devices, body(): high = lax.ppermute(high, 'head', after)  7.19 us
    all_to_all x1, waiting for transfers between devices, exchange(): return lax.all_to_all(array, 'line', 0, 0, tiled=True)  6.94 us
  transfers between devices with their start and end apart: 12, of which 7 were waited for; matrix products, arithmetic and copies ran while one was open for 1% of the time, Pallas kernels for 10%

profile of v3, /device:TPU:1, one launch (start us, length us, event | category | flops | bytes accessed | tf_op | source)
XLA Modules:
  0.0 109.5 jit_solution(13026328469013019122)
XLA Ops:
  0.6 2.2 %local.1 = bf16[8,144,128]{2,1,0:T(8,128)(2,1)S(1)} custom-call(f32[1,4,256]{2,1,0:T(4,128)} %rates_in.5, s32[1,256]{1,0:T(1,128)} %seg_in.5, bf16[1,256,512]{2,1,0:T(8,128)(2,1)} %q_in.5, bf16[1,256,512]{2,1,0:T(8,128)(2,1)} %o_in.5, bf16[1,256,512]{2,1,0:T(8,128)(2,1)} %k_in.5, bf16[1,256,512]{2,1,0:T(8,128)(2,1)} %v_in.3), custom_call_target="tpu_custom_call" | custom-call | tf_op jit(solution)/shard_map/local/pallas_call | solution.py:249
  2.8 17.6 %all_to_all.10.msg = bf16[8,144,128]{2,1,0:T(8,128)(2,1)S(1)} all-to-all(bf16[8,144,128]{2,1,0:T(8,128)(2,1)S(1)} %local.1), channel_id=1, replica_groups=mesh['plane'=8,'line'=8,'head'=8,'pipe'=2] {'line'}, dimensions={0} | all-to-all | bytes 589824 | tf_op jit(solution)/shard_map/all_to_all | solution.py:276
  20.5 1.3 %collective-permute-start = (bf16[80,128]{1,0:T(8,128)(2,1)S(1)}, bf16[80,128]{1,0:T(8,128)(2,1)S(1)}, u32[]{:S(2)}, u32[]{:S(2)}) collective-permute-start(bf16[80,128]{1,0:T(8,128)(2,1)S(1)} %get-tuple-element.21), channel_id=1, source_target_pairs={{128,0},{256,128},{384,256},{512,384},{640,512},{768,640},{896,768... | collective-permute-start | bytes 61448 | tf_op jit(solution)/shard_map/ppermute | solution.py:291
  21.8 6.7 %collective-permute-start.1 = (bf16[80,128]{1,0:T(8,128)(2,1)S(1)}, bf16[80,128]{1,0:T(8,128)(2,1)S(1)}, u32[]{:S(2)}, u32[]{:S(2)}) collective-permute-start(bf16[80,128]{1,0:T(8,128)(2,1)S(1)} %get-tuple-element.22), channel_id=1, source_target_pairs={{0,128},{128,256},{256,384},{384,512},{512,640},{640,768},{768,896... | collective-permute-start | bytes 61448 | tf_op jit(solution)/shard_map/ppermute | solution.py:292
  28.5 0.9 collective-permute-done.1.carried_forward
  30.2 3.4 %all-to-all-start.1 = ((bf16[8,128,128]{2,1,0:T(8,128)(2,1)}), bf16[8,128,128]{2,1,0:T(8,128)(2,1)S(1)}, u32[]{:S(2)}, u32[]{:S(2)}) async-start(bf16[8,128,128]{2,1,0:T(8,128)(2,1)} %row_scan.1), calls=%async_computation.1 | async-start | bytes 524288 | tf_op jit(solution)/shard_map/all_to_all | solution.py:276
  33.6 2.3 %near.1 = (f32[256,512]{1,0:T(8,128)S(1)}, f32[256,512]{1,0:T(8,128)S(1)}, bf16[1,256,512]{2,1,0:T(8,128)(2,1)S(1)}) custom-call(f32[1,4,256]{2,1,0:T(4,128)} %rates_in.5, s32[1,256]{1,0:T(1,128)} %seg_in.5, bf16[1,256,512]{2,1,0:T(8,128)(2,1)} %k_in.5, bf16[1,256,512]{2,1,0:T(8,128)(2,1)} %q_in.5, bf16[1,256,512]{2,1,0:T(8,128)(2,1)} %o_in.5), custom_call_target="tpu_custom_call" | custom-call | tf_op jit(solution)/shard_map/near/pallas_call | solution.py:249
  35.9 6.9 %all-to-all-done.1.states = bf16[8,128,128]{2,1,0:T(8,128)(2,1)S(1)} async-done(((bf16[8,128,128]{2,1,0:T(8,128)(2,1)}), bf16[8,128,128]{2,1,0:T(8,128)(2,1)S(1)}, u32[]{:S(2)}, u32[]{:S(2)}) %all-to-all-start.1) | async-done | bytes 262176 | tf_op jit(solution)/shard_map/all_to_all | solution.py:276
  42.9 1.8 %far.1 = (bf16[256,512]{1,0:T(8,128)(2,1)S(1)}, bf16[128,768]{1,0:T(8,128)(2,1)S(1)}, bf16[128,768]{1,0:T(8,128)(2,1)S(1)}) custom-call(s32[1]{0:T(128)} %bitcast.me, f32[256,512]{1,0:T(8,128)S(1)} %get-tuple-element.18.local, f32[256,512]{1,0:T(8,128)S(1)} %get-tuple-element.19.gain, bf16[1,256,512]{2,1,0:T(8,128)(2,1)S(1)} %get-tuple-element.20.k, ...), custom_call_target="tpu_custom_call" | custom-call | tf_op jit(solution)/shard_map/far/pallas_call | solution.py:249
  44.7 4.7 %collective-permute-start.2 = (bf16[128,768]{1,0:T(8,128)(2,1)S(1)}, bf16[128,768]{1,0:T(8,128)(2,1)S(1)}, u32[]{:S(2)}, u32[]{:S(2)}) collective-permute-start(bf16[128,768]{1,0:T(8,128)(2,1)S(1)} %get-tuple-element.24), channel_id=1, source_target_pairs={{0,14},{2,0},{4,2},{6,4},{8,6},{10,8},{12,10},{14,12},{1,15},{3,1}... | collective-permute-start | bytes 589832 | tf_op jit(solution)/shard_map/ppermute | solution.py:345
  49.4 1.9 %collective-permute-start.4 = (bf16[128,768]{1,0:T(8,128)(2,1)S(1)}, bf16[128,768]{1,0:T(8,128)(2,1)S(1)}, u32[]{:S(2)}, u32[]{:S(2)}) collective-permute-start(bf16[128,768]{1,0:T(8,128)(2,1)S(1)} %get-tuple-element.25), channel_id=1, source_target_pairs={{0,2},{2,4},{4,6},{6,8},{8,10},{10,12},{12,14},{14,0},{1,3},{3,5},... | collective-permute-start | bytes 589832 | tf_op jit(solution)/shard_map/ppermute | solution.py:346
  51.3 4.5 %partial.1.partials_ref = bf16[7,256,768]{2,1,0:T(8,128)(2,1)S(1)} custom-call(s32[1]{0:T(128)} %bitcast.me, bf16[256,512]{1,0:T(8,128)(2,1)S(1)} %get-tuple-element.23.gv, bf16[8,768,512]{2,1,0:T(8,128)(2,1)} %bitcast.8), custom_call_target="tpu_custom_call" | custom-call | tf_op jit(solution)/shard_map/partial/pallas_call | solution.py:249
  55.8 4.6 %collective-permute-start.3 = (bf16[256,768]{1,0:T(8,128)(2,1)S(1)}, bf16[256,768]{1,0:T(8,128)(2,1)S(1)}, u32[]{:S(2)}, u32[]{:S(2)}) collective-permute-start(bf16[256,768]{1,0:T(8,128)(2,1)S(1)} %add_low.3), channel_id=1, source_target_pairs={{0,14},{2,0},{4,2},{6,4},{8,6},{10,8},{12,10},{14,12},{1,15},{3,1}... | collective-permute-start | bytes 1179656 | tf_op jit(solution)/shard_map/ppermute | solution.py:345
  60.5 1.9 %collective-permute-start.5 = (bf16[256,768]{1,0:T(8,128)(2,1)S(1)}, bf16[256,768]{1,0:T(8,128)(2,1)S(1)}, u32[]{:S(2)}, u32[]{:S(2)}) collective-permute-start(bf16[256,768]{1,0:T(8,128)(2,1)S(1)} %add_high.3), channel_id=1, source_target_pairs={{0,2},{2,4},{4,6},{6,8},{8,10},{10,12},{12,14},{14,0},{1,3},{3,5},... | collective-permute-start | bytes 1179656 | tf_op jit(solution)/shard_map/ppermute | solution.py:346
  62.4 3.5 %query_key.1 = (bf16[256,512]{1,0:T(8,128)(2,1)}, bf16[256,512]{1,0:T(8,128)(2,1)}) custom-call(f32[1,4,256]{2,1,0:T(4,128)} %rates_in.5, s32[1,256]{1,0:T(1,128)} %seg_in.5, bf16[1,256,512]{2,1,0:T(8,128)(2,1)} %q_in.5, bf16[1,256,512]{2,1,0:T(8,128)(2,1)} %k_in.5, bf16[1,256,512]{2,1,0:T(8,128)(2,1)} %v_in.3, bf16[1,256,512]{2,1,0:T(8,128)(2,1)} %o_in.5, ...), custom_call_target="tpu_custom_call" | custom-call | tf_op jit(solution)/shard_map/query_key/pallas_call | solution.py:249
  66.1 4.1 %collective-permute-done.5.refs_0_ = bf16[256,768]{1,0:T(8,128)(2,1)S(1)} collective-permute-done((bf16[256,768]{1,0:T(8,128)(2,1)S(1)}, bf16[256,768]{1,0:T(8,128)(2,1)S(1)}, u32[]{:S(2)}, u32[]{:S(2)}) %collective-permute-start.5) | collective-permute-done | bytes 393248 | tf_op jit(solution)/shard_map/ppermute | solution.py:346
  70.3 1.9 %collective-permute-start.6 = (bf16[256,768]{1,0:T(8,128)(2,1)S(1)}, bf16[256,768]{1,0:T(8,128)(2,1)S(1)}, u32[]{:S(2)}, u32[]{:S(2)}) collective-permute-start(bf16[256,768]{1,0:T(8,128)(2,1)S(1)} %add_low.4), channel_id=1, source_target_pairs={{0,14},{2,0},{4,2},{6,4},{8,6},{10,8},{12,10},{14,12},{1,15},{3,1}... | collective-permute-start | bytes 1179656 | tf_op jit(solution)/shard_map/ppermute | solution.py:345
  72.3 3.4 %collective-permute-start.8 = (bf16[256,768]{1,0:T(8,128)(2,1)S(1)}, bf16[256,768]{1,0:T(8,128)(2,1)S(1)}, u32[]{:S(2)}, u32[]{:S(2)}) collective-permute-start(bf16[256,768]{1,0:T(8,128)(2,1)S(1)} %add_high.4), channel_id=1, source_target_pairs={{0,2},{2,4},{4,6},{6,8},{8,10},{10,12},{12,14},{14,0},{1,3},{3,5},... | collective-permute-start | bytes 1179656 | tf_op jit(solution)/shard_map/ppermute | solution.py:346
  75.6 3.2 %collective-permute-done.6.refs_0_ = bf16[256,768]{1,0:T(8,128)(2,1)S(1)} collective-permute-done((bf16[256,768]{1,0:T(8,128)(2,1)S(1)}, bf16[256,768]{1,0:T(8,128)(2,1)S(1)}, u32[]{:S(2)}, u32[]{:S(2)}) %collective-permute-start.6) | collective-permute-done | bytes 393248 | tf_op jit(solution)/shard_map/ppermute | solution.py:345
  78.9 3.1 %collective-permute-start.7 = (bf16[256,768]{1,0:T(8,128)(2,1)S(1)}, bf16[256,768]{1,0:T(8,128)(2,1)S(1)}, u32[]{:S(2)}, u32[]{:S(2)}) collective-permute-start(bf16[256,768]{1,0:T(8,128)(2,1)S(1)} %add_low.5), channel_id=1, source_target_pairs={{0,14},{2,0},{4,2},{6,4},{8,6},{10,8},{12,10},{14,12},{1,15},{3,1}... | collective-permute-start | bytes 1179656 | tf_op jit(solution)/shard_map/ppermute | solution.py:345
  82.2 2.2 %collective-permute-start.9 = (bf16[256,768]{1,0:T(8,128)(2,1)S(1)}, bf16[256,768]{1,0:T(8,128)(2,1)S(1)}, u32[]{:S(2)}, u32[]{:S(2)}) collective-permute-start(bf16[256,768]{1,0:T(8,128)(2,1)S(1)} %add_high.5), channel_id=1, source_target_pairs={{0,2},{2,4},{4,6},{6,8},{8,10},{10,12},{12,14},{14,0},{1,3},{3,5},... | collective-permute-start | bytes 1179656 | tf_op jit(solution)/shard_map/ppermute | solution.py:346
  84.3 7.5 %collective-permute-done.7.refs_0_ = bf16[256,768]{1,0:T(8,128)(2,1)S(1)} collective-permute-done((bf16[256,768]{1,0:T(8,128)(2,1)S(1)}, bf16[256,768]{1,0:T(8,128)(2,1)S(1)}, u32[]{:S(2)}, u32[]{:S(2)}) %collective-permute-start.7) | collective-permute-done | bytes 393248 | tf_op jit(solution)/shard_map/ppermute | solution.py:345
  91.9 3.0 %collective-permute-done.9.refs_1_ = bf16[256,768]{1,0:T(8,128)(2,1)S(1)} collective-permute-done((bf16[256,768]{1,0:T(8,128)(2,1)S(1)}, bf16[256,768]{1,0:T(8,128)(2,1)S(1)}, u32[]{:S(2)}, u32[]{:S(2)}) %collective-permute-start.9) | collective-permute-done | bytes 393248 | tf_op jit(solution)/shard_map/ppermute | solution.py:346
  95.1 12.4 %collective-permute-start.10 = (bf16[256,768]{1,0:T(8,128)(2,1)S(1)}, bf16[256,768]{1,0:T(8,128)(2,1)S(1)}, u32[]{:S(2)}, u32[]{:S(2)}) collective-permute-start(bf16[256,768]{1,0:T(8,128)(2,1)S(1)} %add_last.1), channel_id=1, source_target_pairs={{1,0},{0,1},{3,2},{2,3},{5,4},{4,5},{7,6},{6,7},{9,8},{8,9},{11,10... | collective-permute-start | bytes 1179656 | tf_op jit(solution)/shard_map/ppermute | solution.py:357
  (17 shorter events, 3.6 us)
Async XLA Ops:
  20.5 8.0 %collective-permute-start = (bf16[80,128]{1,0:T(8,128)(2,1)S(1)}, bf16[80,128]{1,0:T(8,128)(2,1)S(1)}, u32[]{:S(2)}, u32[]{:S(2)}) collective-permute-start(bf16[80,128]{1,0:T(8,128)(2,1)S(1)} %get-tuple-element.21), channel_id=1, source_target_pairs={{128,0},{256,128},{384,256},{512,384},{640,512},{768,640},{896,768... | collective-permute-start | bytes 61448 | tf_op jit(solution)/shard_map/ppermute | solution.py:291
  21.8 7.6 %collective-permute-start.1 = (bf16[80,128]{1,0:T(8,128)(2,1)S(1)}, bf16[80,128]{1,0:T(8,128)(2,1)S(1)}, u32[]{:S(2)}, u32[]{:S(2)}) collective-permute-start(bf16[80,128]{1,0:T(8,128)(2,1)S(1)} %get-tuple-element.22), channel_id=1, source_target_pairs={{0,128},{128,256},{256,384},{384,512},{512,640},{640,768},{768,896... | collective-permute-start | bytes 61448 | tf_op jit(solution)/shard_map/ppermute | solution.py:292
  30.2 12.7 %all-to-all-start.1 = ((bf16[8,128,128]{2,1,0:T(8,128)(2,1)}), bf16[8,128,128]{2,1,0:T(8,128)(2,1)S(1)}, u32[]{:S(2)}, u32[]{:S(2)}) async-start(bf16[8,128,128]{2,1,0:T(8,128)(2,1)} %row_scan.1), calls=%async_computation.1 | async-start | bytes 524288 | tf_op jit(solution)/shard_map/all_to_all | solution.py:276
  44.7 11.1 %collective-permute-start.2 = (bf16[128,768]{1,0:T(8,128)(2,1)S(1)}, bf16[128,768]{1,0:T(8,128)(2,1)S(1)}, u32[]{:S(2)}, u32[]{:S(2)}) collective-permute-start(bf16[128,768]{1,0:T(8,128)(2,1)S(1)} %get-tuple-element.24), channel_id=1, source_target_pairs={{0,14},{2,0},{4,2},{6,4},{8,6},{10,8},{12,10},{14,12},{1,15},{3,1}... | collective-permute-start | bytes 589832 | tf_op jit(solution)/shard_map/ppermute | solution.py:345
  49.4 11.0 %collective-permute-start.4 = (bf16[128,768]{1,0:T(8,128)(2,1)S(1)}, bf16[128,768]{1,0:T(8,128)(2,1)S(1)}, u32[]{:S(2)}, u32[]{:S(2)}) collective-permute-start(bf16[128,768]{1,0:T(8,128)(2,1)S(1)} %get-tuple-element.25), channel_id=1, source_target_pairs={{0,2},{2,4},{4,6},{6,8},{8,10},{10,12},{12,14},{14,0},{1,3},{3,5},... | collective-permute-start | bytes 589832 | tf_op jit(solution)/shard_map/ppermute | solution.py:346
  55.8 10.1 %collective-permute-start.3 = (bf16[256,768]{1,0:T(8,128)(2,1)S(1)}, bf16[256,768]{1,0:T(8,128)(2,1)S(1)}, u32[]{:S(2)}, u32[]{:S(2)}) collective-permute-start(bf16[256,768]{1,0:T(8,128)(2,1)S(1)} %add_low.3), channel_id=1, source_target_pairs={{0,14},{2,0},{4,2},{6,4},{8,6},{10,8},{12,10},{14,12},{1,15},{3,1}... | collective-permute-start | bytes 1179656 | tf_op jit(solution)/shard_map/ppermute | solution.py:345
  60.5 9.7 %collective-permute-start.5 = (bf16[256,768]{1,0:T(8,128)(2,1)S(1)}, bf16[256,768]{1,0:T(8,128)(2,1)S(1)}, u32[]{:S(2)}, u32[]{:S(2)}) collective-permute-start(bf16[256,768]{1,0:T(8,128)(2,1)S(1)} %add_high.3), channel_id=1, source_target_pairs={{0,2},{2,4},{4,6},{6,8},{8,10},{10,12},{12,14},{14,0},{1,3},{3,5},... | collective-permute-start | bytes 1179656 | tf_op jit(solution)/shard_map/ppermute | solution.py:346
  70.3 8.5 %collective-permute-start.6 = (bf16[256,768]{1,0:T(8,128)(2,1)S(1)}, bf16[256,768]{1,0:T(8,128)(2,1)S(1)}, u32[]{:S(2)}, u32[]{:S(2)}) collective-permute-start(bf16[256,768]{1,0:T(8,128)(2,1)S(1)} %add_low.4), channel_id=1, source_target_pairs={{0,14},{2,0},{4,2},{6,4},{8,6},{10,8},{12,10},{14,12},{1,15},{3,1}... | collective-permute-start | bytes 1179656 | tf_op jit(solution)/shard_map/ppermute | solution.py:345
  72.3 9.8 %collective-permute-start.8 = (bf16[256,768]{1,0:T(8,128)(2,1)S(1)}, bf16[256,768]{1,0:T(8,128)(2,1)S(1)}, u32[]{:S(2)}, u32[]{:S(2)}) collective-permute-start(bf16[256,768]{1,0:T(8,128)(2,1)S(1)} %add_high.4), channel_id=1, source_target_pairs={{0,2},{2,4},{4,6},{6,8},{8,10},{10,12},{12,14},{14,0},{1,3},{3,5},... | collective-permute-start | bytes 1179656 | tf_op jit(solution)/shard_map/ppermute | solution.py:346
  78.9 12.9 %collective-permute-start.7 = (bf16[256,768]{1,0:T(8,128)(2,1)S(1)}, bf16[256,768]{1,0:T(8,128)(2,1)S(1)}, u32[]{:S(2)}, u32[]{:S(2)}) collective-permute-start(bf16[256,768]{1,0:T(8,128)(2,1)S(1)} %add_low.5), channel_id=1, source_target_pairs={{0,14},{2,0},{4,2},{6,4},{8,6},{10,8},{12,10},{14,12},{1,15},{3,1}... | collective-permute-start | bytes 1179656 | tf_op jit(solution)/shard_map/ppermute | solution.py:345
  82.2 12.7 %collective-permute-start.9 = (bf16[256,768]{1,0:T(8,128)(2,1)S(1)}, bf16[256,768]{1,0:T(8,128)(2,1)S(1)}, u32[]{:S(2)}, u32[]{:S(2)}) collective-permute-start(bf16[256,768]{1,0:T(8,128)(2,1)S(1)} %add_high.5), channel_id=1, source_target_pairs={{0,2},{2,4},{4,6},{6,8},{8,10},{10,12},{12,14},{14,0},{1,3},{3,5},... | collective-permute-start | bytes 1179656 | tf_op jit(solution)/shard_map/ppermute | solution.py:346
  95.1 13.7 %collective-permute-start.10 = (bf16[256,768]{1,0:T(8,128)(2,1)S(1)}, bf16[256,768]{1,0:T(8,128)(2,1)S(1)}, u32[]{:S(2)}, u32[]{:S(2)}) collective-permute-start(bf16[256,768]{1,0:T(8,128)(2,1)S(1)} %add_last.1), channel_id=1, source_target_pairs={{1,0},{0,1},{3,2},{2,3},{5,4},{4,5},{7,6},{6,7},{9,8},{8,9},{11,10... | collective-permute-start | bytes 1179656 | tf_op jit(solution)/shard_map/ppermute | solution.py:357

commit v4 on v3

--- a/solution.py
+++ b/solution.py
@@ -97,9 +97,11 @@
     return jnp.exp(jnp.where(keep, cum_col - cum_row, NEVER))
 
 
-def near_kernel(rates_in, seg_in, k_in, q_in, o_in, gv, gain, k, rates, seg_row, q, o, sems):
-    sources = (rates_in, seg_in, k_in, q_in, o_in)
-    rates_copy, seg_copy, *others = fetch(sources, (rates, seg_row, k, q, o), sems)
+def near_kernel(place, rates_in, seg_in, k_in, q_in, o_in, w_in, gv, gain, k, w, rates, seg_row, q, o, sems):
+    groups = w_in.shape[0]
+    w_far = w_in.at[destination(place, groups // 2, groups)]
+    sources = (rates_in, seg_in, k_in, q_in, o_in, w_far)
+    rates_copy, seg_copy, *others, w_copy = fetch(sources, (rates, seg_row, k, q, o, w), sems)
     rates_copy.wait()
     cum = cumulative_columns(rates[0])
     cum_t = cumulative_rows(rates[0])
@@ -118,6 +120,7 @@
         ks = scores(q[0, :, cols], k[0, :, cols], weight)
         gv[:, cols] = dot(ks, o[0, :, cols], ((0,), (0,)))
         gain[:, cols] = jnp.broadcast_to(behind[:, h : h + 1], (n, dh))
+    w_copy.wait()
 
 
 def unpack(msg, y, reverse):
@@ -169,16 +172,16 @@
     return jnp.concatenate([states[2 * h + half, start : start + share, :] for half in range(2)], axis=0)
 
 
-def far_kernel(me, local, gain, k, states, w_in, gv, low, high, w, sem):
-    groups = w_in.shape[0]
-    copy = pltpu.make_async_copy(w_in.at[lax.rem(me[0] + groups // 2, groups)], w, sem)
-    copy.start()
+def destination(place, offset, groups):
+    return lax.rem(place[0] + groups + place[1] * offset, groups)
+
+
+def far_kernel(place, local, gain, k, states, w, gv, low, high):
     dh = states.shape[2]
     for h in range(gv.shape[1] // dh):
         cols = slice(h * dh, (h + 1) * dh)
         far = dot(k[0, :, cols], head_state(states, h, True), ((1,), (0,)))
         gv[:, cols] = (local[:, cols] + gain[:, cols] * far).astype(bf16)
-    copy.wait()
     rows = low.shape[0]
     low[...] = dot(gv[0:rows, :], w[...], ((1,), (1,))).astype(bf16)
     high[...] = dot(gv[rows:, :], w[...], ((1,), (1,))).astype(bf16)
@@ -188,14 +191,19 @@
     return [sign * far for far in range(groups // 2 - 1, 0, -1) for sign in (-1, 1)] + [0]
 
 
-def partial_kernel(me, gv, w_in, out, w, sems):
+def partial_kernel(wanted, place, gv, w_in, out, *rest):
+    *gv_out, w, sems = rest
     groups = w_in.shape[0]
-    wanted = offsets(groups)
-    sources = [w_in.at[lax.rem(me[0] + groups + offset, groups)] for offset in wanted]
+    sources = [w_in.at[destination(place, offset, groups)] for offset in wanted]
     copies = fetch(sources, [w.at[i] for i in range(len(wanted))], sems)
-    for i, copy in enumerate(copies):
+    for target in gv_out:
+        copies.append(pltpu.make_async_copy(gv, target, sems.at[len(wanted)]))
+        copies[-1].start()
+    for i in range(len(wanted)):
+        copies[i].wait()
+        out[i] = dot(gv[...], w[i], ((1,), (1,))).astype(bf16)
+    for copy in copies[len(wanted) :]:
         copy.wait()
-        out[i] = dot(gv[...], w[i], ((1,), (1,))).astype(bf16)
 
 
 def add_kernel(index, partials, *refs):
@@ -294,34 +302,39 @@
         got, carried_backward, carried_forward
     )
     states = exchange(scanned)
-    gv_local, gain, keys_near = call(
+    place = jnp.stack([lax.axis_index("head"), 1 - 2 * (lax.axis_index("pipe") & 1)]).astype(jnp.int32)
+    weights = w_value.reshape(groups, step, width)
+    gv_local, gain, keys_near, w_far = call(
         near_kernel,
-        (pltpu.VMEM((n, width), f32), pltpu.VMEM((n, width), f32), block),
+        (pltpu.VMEM((n, width), f32), pltpu.VMEM((n, width), f32), block, pltpu.VMEM((step, width), bf16)),
         "near",
         mib=12,
-        in_specs=[IN_HBM] * 5,
-        scratch=[*small, block, block, dma((5,))],
-    )(log_decay, segment_ids, keys, queries, out_grad)
-
-    me = lax.axis_index("head").astype(jnp.int32).reshape(1)
-    weights = w_value.reshape(groups, step, width)
+        in_specs=[IN_SMEM] + [IN_HBM] * 6,
+        scratch=[*small, block, block, dma((6,))],
+    )(place, log_decay, segment_ids, keys, queries, out_grad, weights)
+
     piece = pltpu.VMEM((n // 2, step), bf16)
-    grad_value, low, high = call(
+    near_gv, low, high = call(
         far_kernel,
         (pltpu.VMEM((n, width), bf16), piece, piece),
         "far",
-        mib=12,
-        in_specs=[IN_SMEM] + [IN_VMEM] * 4 + [IN_HBM],
-        scratch=[pltpu.VMEM((step, width), bf16), dma],
-    )(me, gv_local, gain, keys_near, states, weights)
-    partials = call(
-        partial_kernel,
-        pltpu.VMEM((groups - 1, n, step), bf16),
-        "partial",
-        mib=16,
-        in_specs=[IN_SMEM, IN_VMEM, IN_HBM],
-        scratch=[pltpu.VMEM((groups - 1, step, width), bf16), dma((groups - 1,))],
-    )(me, grad_value, weights)
+        in_specs=[IN_SMEM] + [IN_VMEM] * 5,
+    )(place, gv_local, gain, keys_near, states, w_far)
+    def products(wanted, gv, name, writes):
+        count = len(wanted)
+        extra = (jax.ShapeDtypeStruct((n, width), bf16),) if writes else ()
+        return call(
+            lambda *refs: partial_kernel(wanted, *refs),
+            (pltpu.VMEM((count, n, step), bf16), *extra),
+            name,
+            mib=4 * count,
+            in_specs=[IN_SMEM, IN_VMEM, IN_HBM],
+            out_specs=(IN_VMEM, *(IN_HBM for _ in extra)),
+            scratch=[pltpu.VMEM((count, step, width), bf16), dma((count + 1,))],
+        )(place, gv, weights)
+
+    wanted = offsets(groups)
+    (soon,) = products(wanted[:2], near_gv, "partial_soon", False)
     grad_query, grad_key = call(
         query_key_kernel,
         (jax.ShapeDtypeStruct((n, width), bf16), jax.ShapeDtypeStruct((n, width), bf16)),
@@ -331,29 +344,42 @@
         scratch=[*small, block, block, block, block, dma((6,))],
     )(log_decay, segment_ids, queries, keys, values, out_grad, states, gain)
 
-    before = [(i, (i - 1) % groups) for i in range(groups)]
-    after = [(i, (i + 1) % groups) for i in range(groups)]
+    sections = lax.axis_size("pipe")
+
+    def ring(direction):
+        pairs = []
+        for i in range(groups):
+            for c in range(sections):
+                to = (i + (direction if c % 2 == 0 else -direction)) % groups
+                pairs.append((i * sections + c, to * sections + c))
+        return lambda array: lax.ppermute(array, ("head", "pipe"), pairs)
+
+    before, after = ring(-1), ring(1)
     firsts = (0, n // 2)
 
     def add(index, arrived, starts, name):
+        source, index = (soon, index) if index < 2 else (later, index - 2)
+
         def kernel(partials_ref, *refs):
             add_kernel(index, partials_ref, *zip(starts, refs[:-1]), refs[-1])
 
-        return call(kernel, pltpu.VMEM((n, step), bf16), name)(partials, *arrived)
+        return call(kernel, pltpu.VMEM((n, step), bf16), name)(source, *arrived)
 
     for i in range(half):
-        low = lax.ppermute(low, "head", before)
-        high = lax.ppermute(high, "head", after)
+        low = before(low)
+        high = after(high)
         starts = firsts if i == 0 else (0, 0)
         if i == half - 1:
             summed = add(groups - 2, (low, high), starts, "add_last")
         else:
             low = add(2 * i, (low,), starts[:1], "add_low")
             high = add(2 * i + 1, (high,), starts[1:], "add_high")
-        if i == 1:
+        if i == 0:
+            near_gv, low, high = lax.optimization_barrier((near_gv, low, high))
+            later, grad_value = products(wanted[2:], near_gv, "partial_later", True)
+        if i == min(2, half - 1):
             low, high, grad_query, grad_key = lax.optimization_barrier((low, high, grad_query, grad_key))
 
-    sections = lax.axis_size("pipe")
     shifted = lax.ppermute(summed, "pipe", [((i + 1) % sections, i) for i in range(sections)])
     return (grad_query[None], grad_key[None], grad_value[None], shifted[None])
 

time: 110 us -> 113 us (1.027)
  starting transfers between devices: 47.5 us -> 57.3 us
  waiting for transfers between devices: 26.4 us -> 17.7 us
  Pallas kernels: 15.8 us -> 18.2 us
    ppermute x8, waiting for transfers between devices: 17.9 us -> 9.15 us  [ring(): return lambda array: lax.ppermute(array, ('head', 'pipe'), pairs)]
    ppermute x1, starting transfers between devices: 12.4 us -> 19.8 us  [body(): lax.ppermute(summed, 'pipe', [((i + 1) % sections, i) for i in range(sect...]
    ppermute x8, starting transfers between devices: 23.7 us -> 26.1 us  [ring(): return lambda array: lax.ppermute(array, ('head', 'pipe'), pairs)]
    pallas_call x14 -> x15, Pallas kernels: 15.8 us -> 18.2 us  [run(): pl.pallas_call(kernel, in_specs=specs, out_specs=jax.tree.map(lambda _: I...]
  transfers between devices with their start and end apart: 12 -> 12, of which waited for: 7 -> 7; matrix products, arithmetic and copies ran while one was open for 1% -> 0% of each run, Pallas kernels for 10% -> 12%
where the time goes in v4:
time: 113 us; the launch traced here: 112 us
  starting transfers between devices  57.3 us (51%)
  Pallas kernels  18.2 us (16%)
  waiting for transfers between devices  17.7 us (16%)
  blocking collectives  17.6 us (16%)
    ppermute x8, starting transfers between devices, ring(): return lambda array: lax.ppermute(array, ('head', 'pipe'), pairs)  26.1 us
    ppermute x1, starting transfers between devices, body(): lax.ppermute(summed, 'pipe', [((i + 1) % sections, i) for i in range(sect...  19.8 us
    pallas_call x15, Pallas kernels, run(): pl.pallas_call(kernel, in_specs=specs, out_specs=jax.tree.map(lambda _: I...  18.2 us
    all_to_all x1, blocking collectives, exchange(): return lax.all_to_all(array, 'line', 0, 0, tiled=True)  17.6 us
    ppermute x8, waiting for transfers between devices, ring(): return lambda array: lax.ppermute(array, ('head', 'pipe'), pairs)  9.15 us
    ppermute x1, starting transfers between devices, body(): carried_forward = lax.ppermute(total_forward, 'plane', up)  6.69 us
    all_to_all x1, waiting for transfers between devices, exchange(): return lax.all_to_all(array, 'line', 0, 0, tiled=True)  6.32 us
    all_to_all x1, starting transfers between devices, exchange(): return lax.all_to_all(array, 'line', 0, 0, tiled=True)  3.41 us
  transfers between devices with their start and end apart: 12, of which 7 were waited for; matrix products, arithmetic and copies ran while one was open for 0% of the time, Pallas kernels for 12%

profile of v4, /device:TPU:1, one launch (start us, length us, event | category | flops | bytes accessed | tf_op | source)
XLA Modules:
  0.0 112.4 jit_solution(380885012338447202)
XLA Ops:
  0.6 2.2 %local.1 = bf16[8,144,128]{2,1,0:T(8,128)(2,1)S(1)} custom-call(f32[1,4,256]{2,1,0:T(4,128)} %rates_in.5, s32[1,256]{1,0:T(1,128)} %seg_in.5, bf16[1,256,512]{2,1,0:T(8,128)(2,1)} %q_in.5, bf16[1,256,512]{2,1,0:T(8,128)(2,1)} %o_in.5, bf16[1,256,512]{2,1,0:T(8,128)(2,1)} %k_in.5, bf16[1,256,512]{2,1,0:T(8,128)(2,1)} %v_in.3), custom_call_target="tpu_custom_call" | custom-call | tf_op jit(solution)/shard_map/local/pallas_call | solution.py:257
  2.8 17.6 %all_to_all.10.msg = bf16[8,144,128]{2,1,0:T(8,128)(2,1)S(1)} all-to-all(bf16[8,144,128]{2,1,0:T(8,128)(2,1)S(1)} %local.1), channel_id=1, replica_groups=mesh['plane'=8,'line'=8,'head'=8,'pipe'=2] {'line'}, dimensions={0} | all-to-all | bytes 589824 | tf_op jit(solution)/shard_map/all_to_all | solution.py:284
  20.5 1.3 %collective-permute-start = (bf16[80,128]{1,0:T(8,128)(2,1)S(1)}, bf16[80,128]{1,0:T(8,128)(2,1)S(1)}, u32[]{:S(2)}, u32[]{:S(2)}) collective-permute-start(bf16[80,128]{1,0:T(8,128)(2,1)S(1)} %get-tuple-element.27), channel_id=1, source_target_pairs={{128,0},{256,128},{384,256},{512,384},{640,512},{768,640},{896,768... | collective-permute-start | bytes 61448 | tf_op jit(solution)/shard_map/ppermute | solution.py:299
  21.8 6.7 %collective-permute-start.1 = (bf16[80,128]{1,0:T(8,128)(2,1)S(1)}, bf16[80,128]{1,0:T(8,128)(2,1)S(1)}, u32[]{:S(2)}, u32[]{:S(2)}) collective-permute-start(bf16[80,128]{1,0:T(8,128)(2,1)S(1)} %get-tuple-element.28), channel_id=1, source_target_pairs={{0,128},{128,256},{256,384},{384,512},{512,640},{640,768},{768,896... | collective-permute-start | bytes 61448 | tf_op jit(solution)/shard_map/ppermute | solution.py:300
  30.2 3.4 %all-to-all-start.1 = ((bf16[8,128,128]{2,1,0:T(8,128)(2,1)}), bf16[8,128,128]{2,1,0:T(8,128)(2,1)S(1)}, u32[]{:S(2)}, u32[]{:S(2)}) async-start(bf16[8,128,128]{2,1,0:T(8,128)(2,1)} %row_scan.1), calls=%async_computation.1 | async-start | bytes 524288 | tf_op jit(solution)/shard_map/all_to_all | solution.py:284
  33.7 2.8 %near.1 = (f32[256,512]{1,0:T(8,128)S(1)}, f32[256,512]{1,0:T(8,128)S(1)}, bf16[1,256,512]{2,1,0:T(8,128)(2,1)S(1)}, bf16[768,512]{1,0:T(8,128)(2,1)S(1)}) custom-call(s32[2]{0:T(128)S(1)} %pad_add_fusion.place.refs_0_, f32[1,4,256]{2,1,0:T(4,128)} %rates_in.5, s32[1,256]{1,0:T(1,128)} %seg_in.5, bf16[1,256,512]{2,1,0:T(8,128)(2,1)} %k_in.5, ...), custom_call_target="tpu_custom_call" | custom-call | tf_op jit(solution)/shard_map/near/pallas_call | solution.py:257
  36.5 6.3 %all-to-all-done.1.states = bf16[8,128,128]{2,1,0:T(8,128)(2,1)S(1)} async-done(((bf16[8,128,128]{2,1,0:T(8,128)(2,1)}), bf16[8,128,128]{2,1,0:T(8,128)(2,1)S(1)}, u32[]{:S(2)}, u32[]{:S(2)}) %all-to-all-start.1) | async-done | bytes 262176 | tf_op jit(solution)/shard_map/all_to_all | solution.py:284
  42.9 1.3 %far.1 = (bf16[256,512]{1,0:T(8,128)(2,1)S(1)}, bf16[128,768]{1,0:T(8,128)(2,1)S(1)}, bf16[128,768]{1,0:T(8,128)(2,1)S(1)}) custom-call(s32[2]{0:T(128)S(1)} %pad_add_fusion.place.refs_0_, f32[256,512]{1,0:T(8,128)S(1)} %get-tuple-element.24.local, f32[256,512]{1,0:T(8,128)S(1)} %get-tuple-element.25.gain, bf16[1,256,512]{2,1,0:T(8,128)(2,1)S(1)} %get-tuple-element.26.k, ...), custom_call_target="tpu_custom_call" | custom-call | tf_op jit(solution)/shard_map/far/pallas_call | solution.py:257
  44.1 4.7 %collective-permute-start.3 = (bf16[128,768]{1,0:T(8,128)(2,1)S(1)}, bf16[128,768]{1,0:T(8,128)(2,1)S(1)}, u32[]{:S(2)}, u32[]{:S(2)}) collective-permute-start(bf16[128,768]{1,0:T(8,128)(2,1)S(1)} %get-tuple-element.32), channel_id=1, source_target_pairs={{0,2},{1,15},{2,4},{3,1},{4,6},{5,3},{6,8},{7,5},{8,10},{9,7},{10,... | collective-permute-start | bytes 589832 | tf_op jit(solution)/shard_map/ppermute | solution.py:355
  48.9 1.9 %collective-permute-start.2 = (bf16[128,768]{1,0:T(8,128)(2,1)S(1)}, bf16[128,768]{1,0:T(8,128)(2,1)S(1)}, u32[]{:S(2)}, u32[]{:S(2)}) collective-permute-start(bf16[128,768]{1,0:T(8,128)(2,1)S(1)} %get-tuple-element.31), channel_id=1, source_target_pairs={{0,14},{1,3},{2,0},{3,5},{4,2},{5,7},{6,4},{7,9},{8,6},{9,11},{10,... | collective-permute-start | bytes 589832 | tf_op jit(solution)/shard_map/ppermute | solution.py:355
  50.8 2.7 %partial_soon.1.partials_ref = bf16[2,256,768]{2,1,0:T(8,128)(2,1)S(1)} custom-call(s32[2]{0:T(128)S(1)} %pad_add_fusion.place.refs_0_, bf16[256,512]{1,0:T(8,128)(2,1)S(1)} %get-tuple-element.33.refs_1_, bf16[8,768,512]{2,1,0:T(8,128)(2,1)} %bitcast.8), custom_call_target="tpu_custom_call" | custom-call | tf_op jit(solution)/shard_map/partial_soon/pallas_call | solution.py:257
  53.5 3.0 %collective-permute-done.2.refs_0_ = bf16[128,768]{1,0:T(8,128)(2,1)S(1)} collective-permute-done((bf16[128,768]{1,0:T(8,128)(2,1)S(1)}, bf16[128,768]{1,0:T(8,128)(2,1)S(1)}, u32[]{:S(2)}, u32[]{:S(2)}) %collective-permute-start.2) | collective-permute-done | bytes 196640 | tf_op jit(solution)/shard_map/ppermute | solution.py:355
  56.5 1.9 %collective-permute-start.4 = (bf16[256,768]{1,0:T(8,128)(2,1)S(1)}, bf16[256,768]{1,0:T(8,128)(2,1)S(1)}, u32[]{:S(2)}, u32[]{:S(2)}) collective-permute-start(bf16[256,768]{1,0:T(8,128)(2,1)S(1)} %add_low.3), channel_id=1, source_target_pairs={{0,14},{1,3},{2,0},{3,5},{4,2},{5,7},{6,4},{7,9},{8,6},{9,11},{10,... | collective-permute-start | bytes 1179656 | tf_op jit(solution)/shard_map/ppermute | solution.py:355
  58.5 4.6 %collective-permute-start.6 = (bf16[256,768]{1,0:T(8,128)(2,1)S(1)}, bf16[256,768]{1,0:T(8,128)(2,1)S(1)}, u32[]{:S(2)}, u32[]{:S(2)}) collective-permute-start(bf16[256,768]{1,0:T(8,128)(2,1)S(1)} %add_high.3), channel_id=1, source_target_pairs={{0,2},{1,15},{2,4},{3,1},{4,6},{5,3},{6,8},{7,5},{8,10},{9,7},{10,... | collective-permute-start | bytes 1179656 | tf_op jit(solution)/shard_map/ppermute | solution.py:355
  63.0 4.2 %partial_later.1 = (bf16[5,256,768]{2,1,0:T(8,128)(2,1)S(1)}, bf16[256,512]{1,0:T(8,128)(2,1)}) custom-call(s32[2]{0:T(128)S(1)} %pad_add_fusion.place.refs_0_, bf16[256,512]{1,0:T(8,128)(2,1)S(1)} %get-tuple-element.33.refs_1_, bf16[8,768,512]{2,1,0:T(8,128)(2,1)} %bitcast.9), custom_call_target="tpu_custom_call" | custom-call | tf_op jit(solution)/shard_map/partial_later/pallas_call | solution.py:257
  67.3 1.9 %collective-permute-start.5 = (bf16[256,768]{1,0:T(8,128)(2,1)S(1)}, bf16[256,768]{1,0:T(8,128)(2,1)S(1)}, u32[]{:S(2)}, u32[]{:S(2)}) collective-permute-start(bf16[256,768]{1,0:T(8,128)(2,1)S(1)} %add_low.4), channel_id=1, source_target_pairs={{0,14},{1,3},{2,0},{3,5},{4,2},{5,7},{6,4},{7,9},{8,6},{9,11},{10,... | collective-permute-start | bytes 1179656 | tf_op jit(solution)/shard_map/ppermute | solution.py:355
  69.4 4.6 %collective-permute-start.7 = (bf16[256,768]{1,0:T(8,128)(2,1)S(1)}, bf16[256,768]{1,0:T(8,128)(2,1)S(1)}, u32[]{:S(2)}, u32[]{:S(2)}) collective-permute-start(bf16[256,768]{1,0:T(8,128)(2,1)S(1)} %add_high.4), channel_id=1, source_target_pairs={{0,2},{1,15},{2,4},{3,1},{4,6},{5,3},{6,8},{7,5},{8,10},{9,7},{10,... | collective-permute-start | bytes 1179656 | tf_op jit(solution)/shard_map/ppermute | solution.py:355
  73.9 3.5 %query_key.1 = (bf16[256,512]{1,0:T(8,128)(2,1)}, bf16[256,512]{1,0:T(8,128)(2,1)}) custom-call(f32[1,4,256]{2,1,0:T(4,128)} %rates_in.5, s32[1,256]{1,0:T(1,128)} %seg_in.5, bf16[1,256,512]{2,1,0:T(8,128)(2,1)} %q_in.5, bf16[1,256,512]{2,1,0:T(8,128)(2,1)} %k_in.5, bf16[1,256,512]{2,1,0:T(8,128)(2,1)} %v_in.3, bf16[1,256,512]{2,1,0:T(8,128)(2,1)} %o_in.5, ...), custom_call_target="tpu_custom_call" | custom-call | tf_op jit(solution)/shard_map/query_key/pallas_call | solution.py:257
  77.5 1.5 %collective-permute-done.5.refs_0_ = bf16[256,768]{1,0:T(8,128)(2,1)S(1)} collective-permute-done((bf16[256,768]{1,0:T(8,128)(2,1)S(1)}, bf16[256,768]{1,0:T(8,128)(2,1)S(1)}, u32[]{:S(2)}, u32[]{:S(2)}) %collective-permute-start.5) | collective-permute-done | bytes 393248 | tf_op jit(solution)/shard_map/ppermute | solution.py:355
  79.2 1.9 %collective-permute-start.8 = (bf16[256,768]{1,0:T(8,128)(2,1)S(1)}, bf16[256,768]{1,0:T(8,128)(2,1)S(1)}, u32[]{:S(2)}, u32[]{:S(2)}) collective-permute-start(bf16[256,768]{1,0:T(8,128)(2,1)S(1)} %add_low.5), channel_id=1, source_target_pairs={{0,14},{1,3},{2,0},{3,5},{4,2},{5,7},{6,4},{7,9},{8,6},{9,11},{10,... | collective-permute-start | bytes 1179656 | tf_op jit(solution)/shard_map/ppermute | solution.py:355
  81.1 4.6 %collective-permute-start.9 = (bf16[256,768]{1,0:T(8,128)(2,1)S(1)}, bf16[256,768]{1,0:T(8,128)(2,1)S(1)}, u32[]{:S(2)}, u32[]{:S(2)}) collective-permute-start(bf16[256,768]{1,0:T(8,128)(2,1)S(1)} %add_high.5), channel_id=1, source_target_pairs={{0,2},{1,15},{2,4},{3,1},{4,6},{5,3},{6,8},{7,5},{8,10},{9,7},{10,... | collective-permute-start | bytes 1179656 | tf_op jit(solution)/shard_map/ppermute | solution.py:355
  85.7 4.3 %collective-permute-done.8.refs_0_ = bf16[256,768]{1,0:T(8,128)(2,1)S(1)} collective-permute-done((bf16[256,768]{1,0:T(8,128)(2,1)S(1)}, bf16[256,768]{1,0:T(8,128)(2,1)S(1)}, u32[]{:S(2)}, u32[]{:S(2)}) %collective-permute-start.8) | collective-permute-done | bytes 393248 | tf_op jit(solution)/shard_map/ppermute | solution.py:355
  90.5 19.8 %collective-permute-start.10 = (bf16[256,768]{1,0:T(8,128)(2,1)S(1)}, bf16[256,768]{1,0:T(8,128)(2,1)S(1)}, u32[]{:S(2)}, u32[]{:S(2)}) collective-permute-start(bf16[256,768]{1,0:T(8,128)(2,1)S(1)} %add_last.1), channel_id=1, source_target_pairs={{1,0},{0,1},{3,2},{2,3},{5,4},{4,5},{7,6},{6,7},{9,8},{8,9},{11,10... | collective-permute-start | bytes 1179656 | tf_op jit(solution)/shard_map/ppermute | solution.py:383
  110.4 1.3 %collective-permute-done.10 = bf16[256,768]{1,0:T(8,128)(2,1)S(1)} collective-permute-done((bf16[256,768]{1,0:T(8,128)(2,1)S(1)}, bf16[256,768]{1,0:T(8,128)(2,1)S(1)}, u32[]{:S(2)}, u32[]{:S(2)}) %collective-permute-start.10) | collective-permute-done | bytes 393248 | tf_op jit(solution)/shard_map/ppermute | solution.py:383
  (18 shorter events, 3.6 us)
Async XLA Ops:
  20.5 8.0 %collective-permute-start = (bf16[80,128]{1,0:T(8,128)(2,1)S(1)}, bf16[80,128]{1,0:T(8,128)(2,1)S(1)}, u32[]{:S(2)}, u32[]{:S(2)}) collective-permute-start(bf16[80,128]{1,0:T(8,128)(2,1)S(1)} %get-tuple-element.27), channel_id=1, source_target_pairs={{128,0},{256,128},{384,256},{512,384},{640,512},{768,640},{896,768... | collective-permute-start | bytes 61448 | tf_op jit(solution)/shard_map/ppermute | solution.py:299
  21.8 7.6 %collective-permute-start.1 = (bf16[80,128]{1,0:T(8,128)(2,1)S(1)}, bf16[80,128]{1,0:T(8,128)(2,1)S(1)}, u32[]{:S(2)}, u32[]{:S(2)}) collective-permute-start(bf16[80,128]{1,0:T(8,128)(2,1)S(1)} %get-tuple-element.28), channel_id=1, source_target_pairs={{0,128},{128,256},{256,384},{384,512},{512,640},{640,768},{768,896... | collective-permute-start | bytes 61448 | tf_op jit(solution)/shard_map/ppermute | solution.py:300
  30.2 12.7 %all-to-all-start.1 = ((bf16[8,128,128]{2,1,0:T(8,128)(2,1)}), bf16[8,128,128]{2,1,0:T(8,128)(2,1)S(1)}, u32[]{:S(2)}, u32[]{:S(2)}) async-start(bf16[8,128,128]{2,1,0:T(8,128)(2,1)} %row_scan.1), calls=%async_computation.1 | async-start | bytes 524288 | tf_op jit(solution)/shard_map/all_to_all | solution.py:284
  44.1 9.3 %collective-permute-start.3 = (bf16[128,768]{1,0:T(8,128)(2,1)S(1)}, bf16[128,768]{1,0:T(8,128)(2,1)S(1)}, u32[]{:S(2)}, u32[]{:S(2)}) collective-permute-start(bf16[128,768]{1,0:T(8,128)(2,1)S(1)} %get-tuple-element.32), channel_id=1, source_target_pairs={{0,2},{1,15},{2,4},{3,1},{4,6},{5,3},{6,8},{7,5},{8,10},{9,7},{10,... | collective-permute-start | bytes 589832 | tf_op jit(solution)/shard_map/ppermute | solution.py:355
  48.9 7.6 %collective-permute-start.2 = (bf16[128,768]{1,0:T(8,128)(2,1)S(1)}, bf16[128,768]{1,0:T(8,128)(2,1)S(1)}, u32[]{:S(2)}, u32[]{:S(2)}) collective-permute-start(bf16[128,768]{1,0:T(8,128)(2,1)S(1)} %get-tuple-element.31), channel_id=1, source_target_pairs={{0,14},{1,3},{2,0},{3,5},{4,2},{5,7},{6,4},{7,9},{8,6},{9,11},{10,... | collective-permute-start | bytes 589832 | tf_op jit(solution)/shard_map/ppermute | solution.py:355
  56.5 10.7 %collective-permute-start.4 = (bf16[256,768]{1,0:T(8,128)(2,1)S(1)}, bf16[256,768]{1,0:T(8,128)(2,1)S(1)}, u32[]{:S(2)}, u32[]{:S(2)}) collective-permute-start(bf16[256,768]{1,0:T(8,128)(2,1)S(1)} %add_low.3), channel_id=1, source_target_pairs={{0,14},{1,3},{2,0},{3,5},{4,2},{5,7},{6,4},{7,9},{8,6},{9,11},{10,... | collective-permute-start | bytes 1179656 | tf_op jit(solution)/shard_map/ppermute | solution.py:355
  58.5 10.8 %collective-permute-start.6 = (bf16[256,768]{1,0:T(8,128)(2,1)S(1)}, bf16[256,768]{1,0:T(8,128)(2,1)S(1)}, u32[]{:S(2)}, u32[]{:S(2)}) collective-permute-start(bf16[256,768]{1,0:T(8,128)(2,1)S(1)} %add_high.3), channel_id=1, source_target_pairs={{0,2},{1,15},{2,4},{3,1},{4,6},{5,3},{6,8},{7,5},{8,10},{9,7},{10,... | collective-permute-start | bytes 1179656 | tf_op jit(solution)/shard_map/ppermute | solution.py:355
  67.3 11.7 %collective-permute-start.5 = (bf16[256,768]{1,0:T(8,128)(2,1)S(1)}, bf16[256,768]{1,0:T(8,128)(2,1)S(1)}, u32[]{:S(2)}, u32[]{:S(2)}) collective-permute-start(bf16[256,768]{1,0:T(8,128)(2,1)S(1)} %add_low.4), channel_id=1, source_target_pairs={{0,14},{1,3},{2,0},{3,5},{4,2},{5,7},{6,4},{7,9},{8,6},{9,11},{10,... | collective-permute-start | bytes 1179656 | tf_op jit(solution)/shard_map/ppermute | solution.py:355
  69.4 9.7 %collective-permute-start.7 = (bf16[256,768]{1,0:T(8,128)(2,1)S(1)}, bf16[256,768]{1,0:T(8,128)(2,1)S(1)}, u32[]{:S(2)}, u32[]{:S(2)}) collective-permute-start(bf16[256,768]{1,0:T(8,128)(2,1)S(1)} %add_high.4), channel_id=1, source_target_pairs={{0,2},{1,15},{2,4},{3,1},{4,6},{5,3},{6,8},{7,5},{8,10},{9,7},{10,... | collective-permute-start | bytes 1179656 | tf_op jit(solution)/shard_map/ppermute | solution.py:355
  79.2 10.9 %collective-permute-start.8 = (bf16[256,768]{1,0:T(8,128)(2,1)S(1)}, bf16[256,768]{1,0:T(8,128)(2,1)S(1)}, u32[]{:S(2)}, u32[]{:S(2)}) collective-permute-start(bf16[256,768]{1,0:T(8,128)(2,1)S(1)} %add_low.5), channel_id=1, source_target_pairs={{0,14},{1,3},{2,0},{3,5},{4,2},{5,7},{6,4},{7,9},{8,6},{9,11},{10,... | collective-permute-start | bytes 1179656 | tf_op jit(solution)/shard_map/ppermute | solution.py:355
  81.1 9.3 %collective-permute-start.9 = (bf16[256,768]{1,0:T(8,128)(2,1)S(1)}, bf16[256,768]{1,0:T(8,128)(2,1)S(1)}, u32[]{:S(2)}, u32[]{:S(2)}) collective-permute-start(bf16[256,768]{1,0:T(8,128)(2,1)S(1)} %add_high.5), channel_id=1, source_target_pairs={{0,2},{1,15},{2,4},{3,1},{4,6},{5,3},{6,8},{7,5},{8,10},{9,7},{10,... | collective-permute-start | bytes 1179656 | tf_op jit(solution)/shard_map/ppermute | solution.py:355
  90.5 21.1 %collective-permute-start.10 = (bf16[256,768]{1,0:T(8,128)(2,1)S(1)}, bf16[256,768]{1,0:T(8,128)(2,1)S(1)}, u32[]{:S(2)}, u32[]{:S(2)}) collective-permute-start(bf16[256,768]{1,0:T(8,128)(2,1)S(1)} %add_last.1), channel_id=1, source_target_pairs={{1,0},{0,1},{3,2},{2,3},{5,4},{4,5},{7,6},{6,7},{9,8},{8,9},{11,10... | collective-permute-start | bytes 1179656 | tf_op jit(solution)/shard_map/ppermute | solution.py:383

commit v5 on v4

--- a/solution.py
+++ b/solution.py
@@ -99,7 +99,7 @@
 
 def near_kernel(place, rates_in, seg_in, k_in, q_in, o_in, w_in, gv, gain, k, w, rates, seg_row, q, o, sems):
     groups = w_in.shape[0]
-    w_far = w_in.at[destination(place, groups // 2, groups)]
+    w_far = w_in.at[destination(place, FIRST[0], groups)]
     sources = (rates_in, seg_in, k_in, q_in, o_in, w_far)
     rates_copy, seg_copy, *others, w_copy = fetch(sources, (rates, seg_row, k, q, o, w), sems)
     rates_copy.wait()
@@ -176,19 +176,25 @@
     return lax.rem(place[0] + groups + place[1] * offset, groups)
 
 
-def far_kernel(place, local, gain, k, states, w, gv, low, high):
+FIRST = (-4, -2, 3)
+SOON = (-3, 2)
+LATER = (-1, 1, 0)
+
+
+def far_kernel(place, local, gain, k, states, w_first, w_in, gv, pair, single, w, sems):
+    groups = w_in.shape[0]
+    sources = [w_in.at[destination(place, offset, groups)] for offset in FIRST[1:]]
+    copies = fetch(sources, [w.at[i] for i in range(len(sources))], sems)
     dh = states.shape[2]
     for h in range(gv.shape[1] // dh):
         cols = slice(h * dh, (h + 1) * dh)
         far = dot(k[0, :, cols], head_state(states, h, True), ((1,), (0,)))
         gv[:, cols] = (local[:, cols] + gain[:, cols] * far).astype(bf16)
-    rows = low.shape[0]
-    low[...] = dot(gv[0:rows, :], w[...], ((1,), (1,))).astype(bf16)
-    high[...] = dot(gv[rows:, :], w[...], ((1,), (1,))).astype(bf16)
-
-
-def offsets(groups):
-    return [sign * far for far in range(groups // 2 - 1, 0, -1) for sign in (-1, 1)] + [0]
+    pair[0] = dot(gv[...], w_first[...], ((1,), (1,))).astype(bf16)
+    copies[0].wait()
+    pair[1] = dot(gv[...], w[0], ((1,), (1,))).astype(bf16)
+    copies[1].wait()
+    single[...] = dot(gv[...], w[1], ((1,), (1,))).astype(bf16)
 
 
 def partial_kernel(wanted, place, gv, w_in, out, *rest):
@@ -206,16 +212,11 @@
         copy.wait()
 
 
-def add_kernel(index, partials, *refs):
-    *arrived, out = refs
-    total = partials[index].astype(f32)
-    for first, ref in arrived:
-        rows = ref.shape[0]
-        if rows == total.shape[0]:
-            total = total + ref[...].astype(f32)
-        else:
-            kept = [total[0:first], total[first : first + rows] + ref[...].astype(f32), total[first + rows :]]
-            total = jnp.concatenate([part for part in kept if part.shape[0]], axis=0)
+def add_kernel(own, picks, *refs):
+    partials, *arrived, out = refs
+    total = partials[own].astype(f32)
+    for ref, pick in zip(arrived, picks):
+        total = total + (ref[...] if pick is None else ref[pick]).astype(f32)
     out[...] = total.astype(bf16)
 
 
@@ -313,13 +314,16 @@
         scratch=[*small, block, block, dma((6,))],
     )(place, log_decay, segment_ids, keys, queries, out_grad, weights)
 
-    piece = pltpu.VMEM((n // 2, step), bf16)
-    near_gv, low, high = call(
+    part = pltpu.VMEM((n, step), bf16)
+    near_gv, pair, single = call(
         far_kernel,
-        (pltpu.VMEM((n, width), bf16), piece, piece),
+        (pltpu.VMEM((n, width), bf16), pltpu.VMEM((2, n, step), bf16), part),
         "far",
-        in_specs=[IN_SMEM] + [IN_VMEM] * 5,
-    )(place, gv_local, gain, keys_near, states, w_far)
+        mib=8,
+        in_specs=[IN_SMEM] + [IN_VMEM] * 5 + [IN_HBM],
+        scratch=[pltpu.VMEM((2, step, width), bf16), dma((2,))],
+    )(place, gv_local, gain, keys_near, states, w_far, weights)
+
     def products(wanted, gv, name, writes):
         count = len(wanted)
         extra = (jax.ShapeDtypeStruct((n, width), bf16),) if writes else ()
@@ -333,8 +337,7 @@
             scratch=[pltpu.VMEM((count, step, width), bf16), dma((count + 1,))],
         )(place, gv, weights)
 
-    wanted = offsets(groups)
-    (soon,) = products(wanted[:2], near_gv, "partial_soon", False)
+    (soon,) = products(SOON, near_gv, "partial_soon", False)
     grad_query, grad_key = call(
         query_key_kernel,
         (jax.ShapeDtypeStruct((n, width), bf16), jax.ShapeDtypeStruct((n, width), bf16)),
@@ -346,40 +349,31 @@
 
     sections = lax.axis_size("pipe")
 
-    def ring(direction):
+    def hop(array, distance):
         pairs = []
         for i in range(groups):
             for c in range(sections):
-                to = (i + (direction if c % 2 == 0 else -direction)) % groups
+                to = (i + (distance if c % 2 == 0 else -distance)) % groups
                 pairs.append((i * sections + c, to * sections + c))
-        return lambda array: lax.ppermute(array, ("head", "pipe"), pairs)
-
-    before, after = ring(-1), ring(1)
-    firsts = (0, n // 2)
-
-    def add(index, arrived, starts, name):
-        source, index = (soon, index) if index < 2 else (later, index - 2)
-
-        def kernel(partials_ref, *refs):
-            add_kernel(index, partials_ref, *zip(starts, refs[:-1]), refs[-1])
-
-        return call(kernel, pltpu.VMEM((n, step), bf16), name)(source, *arrived)
-
-    for i in range(half):
-        low = before(low)
-        high = after(high)
-        starts = firsts if i == 0 else (0, 0)
-        if i == half - 1:
-            summed = add(groups - 2, (low, high), starts, "add_last")
-        else:
-            low = add(2 * i, (low,), starts[:1], "add_low")
-            high = add(2 * i + 1, (high,), starts[1:], "add_high")
-        if i == 0:
-            near_gv, low, high = lax.optimization_barrier((near_gv, low, high))
-            later, grad_value = products(wanted[2:], near_gv, "partial_later", True)
-        if i == min(2, half - 1):
-            low, high, grad_query, grad_key = lax.optimization_barrier((low, high, grad_query, grad_key))
-
+        return lax.ppermute(array, ("head", "pipe"), pairs)
+
+    def add(partials, own, picks, name, *arrived):
+        return call(lambda *refs: add_kernel(own, picks, *refs), part, name)(partials, *arrived)
+
+    pair_got = hop(pair, -1)
+    single_got = hop(single, 1)
+    long = add(soon, 0, (0,), "add_long", pair_got)
+    short = add(soon, 1, (None,), "add_short", single_got)
+    long, short, near_gv = lax.optimization_barrier((long, short, near_gv))
+    later, grad_value = products(LATER, near_gv, "partial_later", True)
+    long_got = hop(long, -2)
+    short_got = hop(short, 1)
+    long = add(later, 0, (1, None), "add_long_last", pair_got, long_got)
+    short = add(later, 1, (None,), "add_short_last", short_got)
+    long, short, grad_query, grad_key = lax.optimization_barrier((long, short, grad_query, grad_key))
+    long_got = hop(long, -1)
+    short_got = hop(short, 1)
+    summed = add(later, 2, (None, None), "add_last", long_got, short_got)
     shifted = lax.ppermute(summed, "pipe", [((i + 1) % sections, i) for i in range(sections)])
     return (grad_query[None], grad_key[None], grad_value[None], shifted[None])
 

time: 113 us -> 106 us (0.938)
  the two profiles are of different devices: /device:TPU:1 before, /device:TPU:385 now
where the time goes in v5:
time: 106 us
  starting transfers between devices  36 us (34%)
  waiting for transfers between devices  31.5 us (30%)
  Pallas kernels  18.8 us (18%)
  blocking collectives  17.9 us (17%)
    ppermute x6, waiting for transfers between devices, hop(): return lax.ppermute(array, ('head', 'pipe'), pairs)  22.7 us
    ppermute x6, starting transfers between devices, hop(): return lax.ppermute(array, ('head', 'pipe'), pairs)  21 us
    pallas_call x13, Pallas kernels, run(): pl.pallas_call(kernel, in_specs=specs, out_specs=jax.tree.map(lambda _: I...  18.8 us
    all_to_all x1, blocking collectives, exchange(): return lax.all_to_all(array, 'line', 0, 0, tiled=True)  17.9 us
    all_to_all x1, waiting for transfers between devices, exchange(): return lax.all_to_all(array, 'line', 0, 0, tiled=True)  6.52 us
    ppermute x1, starting transfers between devices, body(): carried_forward = lax.ppermute(total_forward, 'plane', up)  6.13 us
    ppermute x1, starting transfers between devices, body(): lax.ppermute(summed, 'pipe', [((i + 1) % sections, i) for i in range(sect...  3.6 us
    all_to_all x1, starting transfers between devices, exchange(): return lax.all_to_all(array, 'line', 0, 0, tiled=True)  3.41 us
  transfers between devices with their start and end apart: 10, of which 7 were waited for; matrix products, arithmetic and copies ran while one was open for 0% of the time, Pallas kernels for 12%

profile of v5, /device:TPU:385, one launch (start us, length us, event | category | flops | bytes accessed | tf_op | source)
XLA Modules:
  0.0 105.9 jit_solution(17190521449613793383)
XLA Ops:
  0.6 2.2 %local.1 = bf16[8,144,128]{2,1,0:T(8,128)(2,1)S(1)} custom-call(f32[1,4,256]{2,1,0:T(4,128)} %rates_in.5, s32[1,256]{1,0:T(1,128)} %seg_in.5, bf16[1,256,512]{2,1,0:T(8,128)(2,1)} %q_in.5, bf16[1,256,512]{2,1,0:T(8,128)(2,1)} %o_in.5, bf16[1,256,512]{2,1,0:T(8,128)(2,1)} %k_in.5, bf16[1,256,512]{2,1,0:T(8,128)(2,1)} %v_in.3), custom_call_target="tpu_custom_call" | custom-call | tf_op jit(solution)/shard_map/local/pallas_call | solution.py:258
  2.8 17.9 %all_to_all.10.msg = bf16[8,144,128]{2,1,0:T(8,128)(2,1)S(1)} all-to-all(bf16[8,144,128]{2,1,0:T(8,128)(2,1)S(1)} %local.1), channel_id=1, replica_groups=mesh['plane'=8,'line'=8,'head'=8,'pipe'=2] {'line'}, dimensions={0} | all-to-all | bytes 589824 | tf_op jit(solution)/shard_map/all_to_all | solution.py:285
  20.8 1.9 %collective-permute-start = (bf16[80,128]{1,0:T(8,128)(2,1)S(1)}, bf16[80,128]{1,0:T(8,128)(2,1)S(1)}, u32[]{:S(2)}, u32[]{:S(2)}) collective-permute-start(bf16[80,128]{1,0:T(8,128)(2,1)S(1)} %get-tuple-element.27), channel_id=1, source_target_pairs={{128,0},{256,128},{384,256},{512,384},{640,512},{768,640},{896,768... | collective-permute-start | bytes 61448 | tf_op jit(solution)/shard_map/ppermute | solution.py:300
  22.7 6.1 %collective-permute-start.1 = (bf16[80,128]{1,0:T(8,128)(2,1)S(1)}, bf16[80,128]{1,0:T(8,128)(2,1)S(1)}, u32[]{:S(2)}, u32[]{:S(2)}) collective-permute-start(bf16[80,128]{1,0:T(8,128)(2,1)S(1)} %get-tuple-element.28), channel_id=1, source_target_pairs={{0,128},{128,256},{256,384},{384,512},{512,640},{640,768},{768,896... | collective-permute-start | bytes 61448 | tf_op jit(solution)/shard_map/ppermute | solution.py:301
  28.9 0.9 collective-permute-done.1.carried_forward
  30.6 3.4 %all-to-all-start.1 = ((bf16[8,128,128]{2,1,0:T(8,128)(2,1)}), bf16[8,128,128]{2,1,0:T(8,128)(2,1)S(1)}, u32[]{:S(2)}, u32[]{:S(2)}) async-start(bf16[8,128,128]{2,1,0:T(8,128)(2,1)} %row_scan.1), calls=%async_computation.1 | async-start | bytes 524288 | tf_op jit(solution)/shard_map/all_to_all | solution.py:285
  34.1 2.8 %near.1 = (f32[256,512]{1,0:T(8,128)S(1)}, f32[256,512]{1,0:T(8,128)S(1)}, bf16[1,256,512]{2,1,0:T(8,128)(2,1)S(1)}, bf16[768,512]{1,0:T(8,128)(2,1)S(1)}) custom-call(s32[2]{0:T(128)S(1)} %pad_add_fusion.place.refs_0_, f32[1,4,256]{2,1,0:T(4,128)} %rates_in.5, s32[1,256]{1,0:T(1,128)} %seg_in.5, bf16[1,256,512]{2,1,0:T(8,128)(2,1)} %k_in.5, ...), custom_call_target="tpu_custom_call" | custom-call | tf_op jit(solution)/shard_map/near/pallas_call | solution.py:258
  36.9 6.5 %all-to-all-done.1.states = bf16[8,128,128]{2,1,0:T(8,128)(2,1)S(1)} async-done(((bf16[8,128,128]{2,1,0:T(8,128)(2,1)}), bf16[8,128,128]{2,1,0:T(8,128)(2,1)S(1)}, u32[]{:S(2)}, u32[]{:S(2)}) %all-to-all-start.1) | async-done | bytes 262176 | tf_op jit(solution)/shard_map/all_to_all | solution.py:285
  43.4 3.0 %far.1 = (bf16[256,512]{1,0:T(8,128)(2,1)S(1)}, bf16[2,256,768]{2,1,0:T(8,128)(2,1)S(1)}, bf16[256,768]{1,0:T(8,128)(2,1)S(1)}) custom-call(s32[2]{0:T(128)S(1)} %pad_add_fusion.place.refs_0_, f32[256,512]{1,0:T(8,128)S(1)} %get-tuple-element.24.local, f32[256,512]{1,0:T(8,128)S(1)} %get-tuple-element.25.gain, bf16[1,256,512]{2,1,0:T(8,128)(2,1)S(1)} %get-tuple-element.26.k, ...), custom_call_target="tpu_custom_call" | custom-call | tf_op jit(solution)/shard_map/far/pallas_call | solution.py:258
  46.4 3.1 %collective-permute-start.2 = (bf16[2,256,768]{2,1,0:T(8,128)(2,1)S(1)}, bf16[2,256,768]{2,1,0:T(8,128)(2,1)S(1)}, u32[]{:S(2)}, u32[]{:S(2)}) collective-permute-start(bf16[2,256,768]{2,1,0:T(8,128)(2,1)S(1)} %get-tuple-element.31), channel_id=1, source_target_pairs={{0,14},{1,3},{2,0},{3,5},{4,2},{5,7},{6,4},{7,9},{8,6},{9,11},{10,... | collective-permute-start | bytes 2359304 | tf_op jit(solution)/shard_map/ppermute | solution.py:358
  49.5 3.4 %collective-permute-start.3 = (bf16[256,768]{1,0:T(8,128)(2,1)S(1)}, bf16[256,768]{1,0:T(8,128)(2,1)S(1)}, u32[]{:S(2)}, u32[]{:S(2)}) collective-permute-start(bf16[256,768]{1,0:T(8,128)(2,1)S(1)} %get-tuple-element.32), channel_id=1, source_target_pairs={{0,2},{1,15},{2,4},{3,1},{4,6},{5,3},{6,8},{7,5},{8,10},{9,7},{10,... | collective-permute-start | bytes 1179656 | tf_op jit(solution)/shard_map/ppermute | solution.py:358
  52.9 2.7 %partial_soon.1.refs_0_ = bf16[2,256,768]{2,1,0:T(8,128)(2,1)S(1)} custom-call(s32[2]{0:T(128)S(1)} %pad_add_fusion.place.refs_0_, bf16[256,512]{1,0:T(8,128)(2,1)S(1)} %get-tuple-element.33.refs_1_, bf16[8,768,512]{2,1,0:T(8,128)(2,1)} %bitcast.9), custom_call_target="tpu_custom_call" | custom-call | tf_op jit(solution)/shard_map/partial_soon/pallas_call | solution.py:258
  55.6 5.0 %collective-permute-done.3.refs_1_ = bf16[256,768]{1,0:T(8,128)(2,1)S(1)} collective-permute-done((bf16[256,768]{1,0:T(8,128)(2,1)S(1)}, bf16[256,768]{1,0:T(8,128)(2,1)S(1)}, u32[]{:S(2)}, u32[]{:S(2)}) %collective-permute-start.3) | collective-permute-done | bytes 393248 | tf_op jit(solution)/shard_map/ppermute | solution.py:358
  60.9 6.1 %collective-permute-start.4 = (bf16[256,768]{1,0:T(8,128)(2,1)S(1)}, bf16[256,768]{1,0:T(8,128)(2,1)S(1)}, u32[]{:S(2)}, u32[]{:S(2)}) collective-permute-start(bf16[256,768]{1,0:T(8,128)(2,1)S(1)} %add_long.1), channel_id=1, source_target_pairs={{0,12},{1,5},{2,14},{3,7},{4,0},{5,9},{6,2},{7,11},{8,4},{9,13},{1... | collective-permute-start | bytes 1179656 | tf_op jit(solution)/shard_map/ppermute | solution.py:358
  66.9 1.9 %collective-permute-start.5 = (bf16[256,768]{1,0:T(8,128)(2,1)S(1)}, bf16[256,768]{1,0:T(8,128)(2,1)S(1)}, u32[]{:S(2)}, u32[]{:S(2)}) collective-permute-start(bf16[256,768]{1,0:T(8,128)(2,1)S(1)} %add_short.1), channel_id=1, source_target_pairs={{0,2},{1,15},{2,4},{3,1},{4,6},{5,3},{6,8},{7,5},{8,10},{9,7},{10,... | collective-permute-start | bytes 1179656 | tf_op jit(solution)/shard_map/ppermute | solution.py:358
  68.9 3.5 %query_key.1 = (bf16[256,512]{1,0:T(8,128)(2,1)}, bf16[256,512]{1,0:T(8,128)(2,1)}) custom-call(f32[1,4,256]{2,1,0:T(4,128)} %rates_in.5, s32[1,256]{1,0:T(1,128)} %seg_in.5, bf16[1,256,512]{2,1,0:T(8,128)(2,1)} %q_in.5, bf16[1,256,512]{2,1,0:T(8,128)(2,1)} %k_in.5, bf16[1,256,512]{2,1,0:T(8,128)(2,1)} %v_in.3, bf16[1,256,512]{2,1,0:T(8,128)(2,1)} %o_in.5, ...), custom_call_target="tpu_custom_call" | custom-call | tf_op jit(solution)/shard_map/query_key/pallas_call | solution.py:258
  72.4 3.2 %partial_later.1 = (bf16[3,256,768]{2,1,0:T(8,128)(2,1)S(1)}, bf16[256,512]{1,0:T(8,128)(2,1)}) custom-call(s32[2]{0:T(128)S(1)} %pad_add_fusion.place.refs_0_, bf16[256,512]{1,0:T(8,128)(2,1)S(1)} %get-tuple-element.33.refs_1_, bf16[8,768,512]{2,1,0:T(8,128)(2,1)} %bitcast.10), custom_call_target="tpu_custom_call" | custom-call | tf_op jit(solution)/shard_map/partial_later/pallas_call | solution.py:258
  75.8 8.4 %collective-permute-done.5.refs_1_ = bf16[256,768]{1,0:T(8,128)(2,1)S(1)} collective-permute-done((bf16[256,768]{1,0:T(8,128)(2,1)S(1)}, bf16[256,768]{1,0:T(8,128)(2,1)S(1)}, u32[]{:S(2)}, u32[]{:S(2)}) %collective-permute-start.5) | collective-permute-done | bytes 393248 | tf_op jit(solution)/shard_map/ppermute | solution.py:358
  84.2 4.1 %collective-permute-start.6 = (bf16[256,768]{1,0:T(8,128)(2,1)S(1)}, bf16[256,768]{1,0:T(8,128)(2,1)S(1)}, u32[]{:S(2)}, u32[]{:S(2)}) collective-permute-start(bf16[256,768]{1,0:T(8,128)(2,1)S(1)} %add_long_last.1), channel_id=1, source_target_pairs={{0,14},{1,3},{2,0},{3,5},{4,2},{5,7},{6,4},{7,9},{8,6},{9,11},{10,... | collective-permute-start | bytes 1179656 | tf_op jit(solution)/shard_map/ppermute | solution.py:358
  88.3 2.4 %collective-permute-start.7 = (bf16[256,768]{1,0:T(8,128)(2,1)S(1)}, bf16[256,768]{1,0:T(8,128)(2,1)S(1)}, u32[]{:S(2)}, u32[]{:S(2)}) collective-permute-start(bf16[256,768]{1,0:T(8,128)(2,1)S(1)} %add_short_last.1), channel_id=1, source_target_pairs={{0,2},{1,15},{2,4},{3,1},{4,6},{5,3},{6,8},{7,5},{8,10},{9,7},{10,... | collective-permute-start | bytes 1179656 | tf_op jit(solution)/shard_map/ppermute | solution.py:358
  90.8 3.2 %collective-permute-done.6.refs_1_ = bf16[256,768]{1,0:T(8,128)(2,1)S(1)} collective-permute-done((bf16[256,768]{1,0:T(8,128)(2,1)S(1)}, bf16[256,768]{1,0:T(8,128)(2,1)S(1)}, u32[]{:S(2)}, u32[]{:S(2)}) %collective-permute-start.6) | collective-permute-done | bytes 393248 | tf_op jit(solution)/shard_map/ppermute | solution.py:358
  94.0 6.1 %collective-permute-done.7.refs_2_ = bf16[256,768]{1,0:T(8,128)(2,1)S(1)} collective-permute-done((bf16[256,768]{1,0:T(8,128)(2,1)S(1)}, bf16[256,768]{1,0:T(8,128)(2,1)S(1)}, u32[]{:S(2)}, u32[]{:S(2)}) %collective-permute-start.7) | collective-permute-done | bytes 393248 | tf_op jit(solution)/shard_map/ppermute | solution.py:358
  100.2 3.6 %collective-permute-start.8 = (bf16[256,768]{1,0:T(8,128)(2,1)S(1)}, bf16[256,768]{1,0:T(8,128)(2,1)S(1)}, u32[]{:S(2)}, u32[]{:S(2)}) collective-permute-start(bf16[256,768]{1,0:T(8,128)(2,1)S(1)} %add_last.1), channel_id=1, source_target_pairs={{1,0},{0,1},{3,2},{2,3},{5,4},{4,5},{7,6},{6,7},{9,8},{8,9},{11,10... | collective-permute-start | bytes 1179656 | tf_op jit(solution)/shard_map/ppermute | solution.py:377
  103.8 1.3 %collective-permute-done.8 = bf16[256,768]{1,0:T(8,128)(2,1)S(1)} collective-permute-done((bf16[256,768]{1,0:T(8,128)(2,1)S(1)}, bf16[256,768]{1,0:T(8,128)(2,1)S(1)}, u32[]{:S(2)}, u32[]{:S(2)}) %collective-permute-start.8) | collective-permute-done | bytes 393248 | tf_op jit(solution)/shard_map/ppermute | solution.py:377
  (12 shorter events, 2.3 us)
Async XLA Ops:
  20.8 8.1 %collective-permute-start = (bf16[80,128]{1,0:T(8,128)(2,1)S(1)}, bf16[80,128]{1,0:T(8,128)(2,1)S(1)}, u32[]{:S(2)}, u32[]{:S(2)}) collective-permute-start(bf16[80,128]{1,0:T(8,128)(2,1)S(1)} %get-tuple-element.27), channel_id=1, source_target_pairs={{128,0},{256,128},{384,256},{512,384},{640,512},{768,640},{896,768... | collective-permute-start | bytes 61448 | tf_op jit(solution)/shard_map/ppermute | solution.py:300
  22.7 7.0 %collective-permute-start.1 = (bf16[80,128]{1,0:T(8,128)(2,1)S(1)}, bf16[80,128]{1,0:T(8,128)(2,1)S(1)}, u32[]{:S(2)}, u32[]{:S(2)}) collective-permute-start(bf16[80,128]{1,0:T(8,128)(2,1)S(1)} %get-tuple-element.28), channel_id=1, source_target_pairs={{0,128},{128,256},{256,384},{384,512},{512,640},{640,768},{768,896... | collective-permute-start | bytes 61448 | tf_op jit(solution)/shard_map/ppermute | solution.py:301
  30.6 12.9 %all-to-all-start.1 = ((bf16[8,128,128]{2,1,0:T(8,128)(2,1)}), bf16[8,128,128]{2,1,0:T(8,128)(2,1)S(1)}, u32[]{:S(2)}, u32[]{:S(2)}) async-start(bf16[8,128,128]{2,1,0:T(8,128)(2,1)} %row_scan.1), calls=%async_computation.1 | async-start | bytes 524288 | tf_op jit(solution)/shard_map/all_to_all | solution.py:285
  46.4 14.3 %collective-permute-start.2 = (bf16[2,256,768]{2,1,0:T(8,128)(2,1)S(1)}, bf16[2,256,768]{2,1,0:T(8,128)(2,1)S(1)}, u32[]{:S(2)}, u32[]{:S(2)}) collective-permute-start(bf16[2,256,768]{2,1,0:T(8,128)(2,1)S(1)} %get-tuple-element.31), channel_id=1, source_target_pairs={{0,14},{1,3},{2,0},{3,5},{4,2},{5,7},{6,4},{7,9},{8,6},{9,11},{10,... | collective-permute-start | bytes 2359304 | tf_op jit(solution)/shard_map/ppermute | solution.py:358
  49.5 11.1 %collective-permute-start.3 = (bf16[256,768]{1,0:T(8,128)(2,1)S(1)}, bf16[256,768]{1,0:T(8,128)(2,1)S(1)}, u32[]{:S(2)}, u32[]{:S(2)}) collective-permute-start(bf16[256,768]{1,0:T(8,128)(2,1)S(1)} %get-tuple-element.32), channel_id=1, source_target_pairs={{0,2},{1,15},{2,4},{3,1},{4,6},{5,3},{6,8},{7,5},{8,10},{9,7},{10,... | collective-permute-start | bytes 1179656 | tf_op jit(solution)/shard_map/ppermute | solution.py:358
  60.9 14.7 %collective-permute-start.4 = (bf16[256,768]{1,0:T(8,128)(2,1)S(1)}, bf16[256,768]{1,0:T(8,128)(2,1)S(1)}, u32[]{:S(2)}, u32[]{:S(2)}) collective-permute-start(bf16[256,768]{1,0:T(8,128)(2,1)S(1)} %add_long.1), channel_id=1, source_target_pairs={{0,12},{1,5},{2,14},{3,7},{4,0},{5,9},{6,2},{7,11},{8,4},{9,13},{1... | collective-permute-start | bytes 1179656 | tf_op jit(solution)/shard_map/ppermute | solution.py:358
  66.9 17.2 %collective-permute-start.5 = (bf16[256,768]{1,0:T(8,128)(2,1)S(1)}, bf16[256,768]{1,0:T(8,128)(2,1)S(1)}, u32[]{:S(2)}, u32[]{:S(2)}) collective-permute-start(bf16[256,768]{1,0:T(8,128)(2,1)S(1)} %add_short.1), channel_id=1, source_target_pairs={{0,2},{1,15},{2,4},{3,1},{4,6},{5,3},{6,8},{7,5},{8,10},{9,7},{10,... | collective-permute-start | bytes 1179656 | tf_op jit(solution)/shard_map/ppermute | solution.py:358
  84.2 9.7 %collective-permute-start.6 = (bf16[256,768]{1,0:T(8,128)(2,1)S(1)}, bf16[256,768]{1,0:T(8,128)(2,1)S(1)}, u32[]{:S(2)}, u32[]{:S(2)}) collective-permute-start(bf16[256,768]{1,0:T(8,128)(2,1)S(1)} %add_long_last.1), channel_id=1, source_target_pairs={{0,14},{1,3},{2,0},{3,5},{4,2},{5,7},{6,4},{7,9},{8,6},{9,11},{10,... | collective-permute-start | bytes 1179656 | tf_op jit(solution)/shard_map/ppermute | solution.py:358
  88.3 11.7 %collective-permute-start.7 = (bf16[256,768]{1,0:T(8,128)(2,1)S(1)}, bf16[256,768]{1,0:T(8,128)(2,1)S(1)}, u32[]{:S(2)}, u32[]{:S(2)}) collective-permute-start(bf16[256,768]{1,0:T(8,128)(2,1)S(1)} %add_short_last.1), channel_id=1, source_target_pairs={{0,2},{1,15},{2,4},{3,1},{4,6},{5,3},{6,8},{7,5},{8,10},{9,7},{10,... | collective-permute-start | bytes 1179656 | tf_op jit(solution)/shard_map/ppermute | solution.py:358
  100.2 4.9 %collective-permute-start.8 = (bf16[256,768]{1,0:T(8,128)(2,1)S(1)}, bf16[256,768]{1,0:T(8,128)(2,1)S(1)}, u32[]{:S(2)}, u32[]{:S(2)}) collective-permute-start(bf16[256,768]{1,0:T(8,128)(2,1)S(1)} %add_last.1), channel_id=1, source_target_pairs={{1,0},{0,1},{3,2},{2,3},{5,4},{4,5},{7,6},{6,7},{9,8},{8,9},{11,10... | collective-permute-start | bytes 1179656 | tf_op jit(solution)/shard_map/ppermute | solution.py:377

commit v6 on v5

--- a/solution.py
+++ b/solution.py
@@ -98,10 +98,11 @@
 
 
 def near_kernel(place, rates_in, seg_in, k_in, q_in, o_in, w_in, gv, gain, k, w, rates, seg_row, q, o, sems):
-    groups = w_in.shape[0]
-    w_far = w_in.at[destination(place, FIRST[0], groups)]
-    sources = (rates_in, seg_in, k_in, q_in, o_in, w_far)
-    rates_copy, seg_copy, *others, w_copy = fetch(sources, (rates, seg_row, k, q, o, w), sems)
+    w_pair = [w_in.at[destination(place, offset, w_in.shape[0])] for offset in PAIR]
+    sources = (rates_in, seg_in, k_in, q_in, o_in, *w_pair)
+    targets = (rates, seg_row, k, q, o, *(w.at[i] for i in range(len(PAIR))))
+    rates_copy, seg_copy, *others = fetch(sources, targets, sems)
+    others, w_copies = others[:3], others[3:]
     rates_copy.wait()
     cum = cumulative_columns(rates[0])
     cum_t = cumulative_rows(rates[0])
@@ -120,7 +121,8 @@
         ks = scores(q[0, :, cols], k[0, :, cols], weight)
         gv[:, cols] = dot(ks, o[0, :, cols], ((0,), (0,)))
         gain[:, cols] = jnp.broadcast_to(behind[:, h : h + 1], (n, dh))
-    w_copy.wait()
+    for copy in w_copies:
+        copy.wait()
 
 
 def unpack(msg, y, reverse):
@@ -176,25 +178,20 @@
     return lax.rem(place[0] + groups + place[1] * offset, groups)
 
 
-FIRST = (-4, -2, 3)
-SOON = (-3, 2)
-LATER = (-1, 1, 0)
-
-
-def far_kernel(place, local, gain, k, states, w_first, w_in, gv, pair, single, w, sems):
-    groups = w_in.shape[0]
-    sources = [w_in.at[destination(place, offset, groups)] for offset in FIRST[1:]]
-    copies = fetch(sources, [w.at[i] for i in range(len(sources))], sems)
+PAIR = (-4, -2)
+SINGLE = (3,)
+SOON = (-3, 2, 0)
+LATER = (-1, 1)
+
+
+def far_kernel(place, local, gain, k, states, w, gv, pair):
     dh = states.shape[2]
     for h in range(gv.shape[1] // dh):
         cols = slice(h * dh, (h + 1) * dh)
         far = dot(k[0, :, cols], head_state(states, h, True), ((1,), (0,)))
         gv[:, cols] = (local[:, cols] + gain[:, cols] * far).astype(bf16)
-    pair[0] = dot(gv[...], w_first[...], ((1,), (1,))).astype(bf16)
-    copies[0].wait()
-    pair[1] = dot(gv[...], w[0], ((1,), (1,))).astype(bf16)
-    copies[1].wait()
-    single[...] = dot(gv[...], w[1], ((1,), (1,))).astype(bf16)
+    for i in range(len(PAIR)):
+        pair[i] = dot(gv[...], w[i], ((1,), (1,))).astype(bf16)
 
 
 def partial_kernel(wanted, place, gv, w_in, out, *rest):
@@ -276,7 +273,6 @@
     groups = lax.axis_size("head")
     share = heads * dh // ROW
     step = w_value.shape[1] // groups
-    half = groups // 2
     block = pltpu.VMEM((1, n, width), bf16)
     small = [pltpu.VMEM(log_decay.shape, f32), pltpu.VMEM(segment_ids.shape, jnp.int32)]
     dma = pltpu.SemaphoreType.DMA
@@ -305,24 +301,22 @@
     states = exchange(scanned)
     place = jnp.stack([lax.axis_index("head"), 1 - 2 * (lax.axis_index("pipe") & 1)]).astype(jnp.int32)
     weights = w_value.reshape(groups, step, width)
-    gv_local, gain, keys_near, w_far = call(
+    gv_local, gain, keys_near, w_pair = call(
         near_kernel,
-        (pltpu.VMEM((n, width), f32), pltpu.VMEM((n, width), f32), block, pltpu.VMEM((step, width), bf16)),
+        (pltpu.VMEM((n, width), f32), pltpu.VMEM((n, width), f32), block, pltpu.VMEM((len(PAIR), step, width), bf16)),
         "near",
         mib=12,
         in_specs=[IN_SMEM] + [IN_HBM] * 6,
-        scratch=[*small, block, block, dma((6,))],
+        scratch=[*small, block, block, dma((5 + len(PAIR),))],
     )(place, log_decay, segment_ids, keys, queries, out_grad, weights)
 
     part = pltpu.VMEM((n, step), bf16)
-    near_gv, pair, single = call(
+    near_gv, pair = call(
         far_kernel,
-        (pltpu.VMEM((n, width), bf16), pltpu.VMEM((2, n, step), bf16), part),
+        (pltpu.VMEM((n, width), bf16), pltpu.VMEM((2, n, step), bf16)),
         "far",
-        mib=8,
-        in_specs=[IN_SMEM] + [IN_VMEM] * 5 + [IN_HBM],
-        scratch=[pltpu.VMEM((2, step, width), bf16), dma((2,))],
-    )(place, gv_local, gain, keys_near, states, w_far, weights)
+        in_specs=[IN_SMEM] + [IN_VMEM] * 5,
+    )(place, gv_local, gain, keys_near, states, w_pair)
 
     def products(wanted, gv, name, writes):
         count = len(wanted)
@@ -337,7 +331,60 @@
             scratch=[pltpu.VMEM((count, step, width), bf16), dma((count + 1,))],
         )(place, gv, weights)
 
+    sections = lax.axis_size("pipe")
+
+    def hop(array, distance, cross=False):
+        pairs = []
+        for i in range(groups):
+            for c in range(sections):
+                to = (i + (distance if c % 2 == 0 else -distance)) % groups
+                pairs.append((i * sections + c, to * sections + (c - cross) % sections))
+        return lax.ppermute(array, ("head", "pipe"), pairs)
+
+    def add(partials, own, picks, name, *arrived):
+        return call(lambda *refs: add_kernel(own, picks, *refs), part, name)(partials, *arrived)
+
+    pair_got = hop(pair, -1)
+    (single,) = products(SINGLE, near_gv, "partial_single", False)
+    single_got = hop(single, 1)
     (soon,) = products(SOON, near_gv, "partial_soon", False)
+    own_got = hop(soon[2:], 0, True)
+    long = add(soon, 0, (0,), "add_long", pair_got)
+    short = add(soon, 1, (0,), "add_short", single_got)
+    long, short, near_gv, own_got = lax.optimization_barrier((long, short, near_gv, own_got))
+    later, grad_value = products(LATER, near_gv, "partial_later", True)
+    long_got = hop(long, -2)
+    short_got = hop(short, 1)
+    long = add(later, 0, (1, None), "add_long_last", pair_got, long_got)
+    short = add(later, 1, (None,), "add_short_last", short_got)
+    long, short, states, gain = lax.optimization_barrier((long, short, states, gain))
+    sections = lax.axis_size("pipe")
+
+    def hop(array, distance, cross=False):
+        pairs = []
+        for i in range(groups):
+            for c in range(sections):
+                to = (i + (distance if c % 2 == 0 else -distance)) % groups
+                pairs.append((i * sections + c, to * sections + (c - cross) % sections))
+        return lax.ppermute(array, ("head", "pipe"), pairs)
+
+    def add(partials, own, picks, name, *arrived):
+        return call(lambda *refs: add_kernel(own, picks, *refs), part, name)(partials, *arrived)
+
+    pair_got = hop(pair, -1)
+    (single,) = products(SINGLE, near_gv, "partial_single", False)
+    single_got = hop(single, 1)
+    (soon,) = products(SOON, near_gv, "partial_soon", False)
+    own_got = hop(soon[2:], 0, True)
+    long = add(soon, 0, (0,), "add_long", pair_got)
+    short = add(soon, 1, (0,), "add_short", single_got)
+    long, short, near_gv, own_got = lax.optimization_barrier((long, short, near_gv, own_got))
+    later, grad_value = products(LATER, near_gv, "partial_later", True)
+    long_got = hop(long, -2)
+    short_got = hop(short, 1)
+    long = add(later, 0, (1, None), "add_long_last", pair_got, long_got)
+    short = add(later, 1, (None,), "add_short_last", short_got)
+    long, short, states, gain = lax.optimization_barrier((long, short, states, gain))
     grad_query, grad_key = call(
         query_key_kernel,
         (jax.ShapeDtypeStruct((n, width), bf16), jax.ShapeDtypeStruct((n, width), bf16)),
@@ -346,36 +393,13 @@
         in_specs=[IN_HBM] * 6 + [IN_VMEM] * 2,
         scratch=[*small, block, block, block, block, dma((6,))],
     )(log_decay, segment_ids, queries, keys, values, out_grad, states, gain)
-
-    sections = lax.axis_size("pipe")
-
-    def hop(array, distance):
-        pairs = []
-        for i in range(groups):
-            for c in range(sections):
-                to = (i + (distance if c % 2 == 0 else -distance)) % groups
-                pairs.append((i * sections + c, to * sections + c))
-        return lax.ppermute(array, ("head", "pipe"), pairs)
-
-    def add(partials, own, picks, name, *arrived):
-        return call(lambda *refs: add_kernel(own, picks, *refs), part, name)(partials, *arrived)
-
-    pair_got = hop(pair, -1)
-    single_got = hop(single, 1)
-    long = add(soon, 0, (0,), "add_long", pair_got)
-    short = add(soon, 1, (None,), "add_short", single_got)
-    long, short, near_gv = lax.optimization_barrier((long, short, near_gv))
-    later, grad_value = products(LATER, near_gv, "partial_later", True)
-    long_got = hop(long, -2)
-    short_got = hop(short, 1)
-    long = add(later, 0, (1, None), "add_long_last", pair_got, long_got)
-    short = add(later, 1, (None,), "add_short_last", short_got)
-    long, short, grad_query, grad_key = lax.optimization_barrier((long, short, grad_query, grad_key))
-    long_got = hop(long, -1)
-    short_got = hop(short, 1)
-    summed = add(later, 2, (None, None), "add_last", long_got, short_got)
-    shifted = lax.ppermute(summed, "pipe", [((i + 1) % sections, i) for i in range(sections)])
-    return (grad_query[None], grad_key[None], grad_value[None], shifted[None])
+    long_got = hop(long, -1, True)
+    short_got = hop(short, 1, True)
+    long_got, short_got, grad_query, grad_key = lax.optimization_barrier((long_got, short_got, grad_query, grad_key))
+    grad_input = call(
+        lambda *refs: add_kernel(0, (None, None), *refs), jax.ShapeDtypeStruct((n, step), bf16), "add_last"
+    )(own_got, long_got, short_got)
+    return (grad_query[None], grad_key[None], grad_value[None], grad_input[None])
 
 
 def solution(mesh):

time: 106 us -> 103 us (0.972)
  the two profiles are of different devices: /device:TPU:385 before, /device:TPU:1 now
where the time goes in v6:
time: 103 us; the launch traced here: 102 us
  starting transfers between devices  41.5 us (40%)
  waiting for transfers between devices  22.1 us (21%)
  Pallas kernels  20 us (19%)
  blocking collectives  17.6 us (17%)
    ppermute x7, starting transfers between devices, hop(): return lax.ppermute(array, ('head', 'pipe'), pairs)  30.1 us
    pallas_call x14, Pallas kernels, run(): pl.pallas_call(kernel, in_specs=specs, out_specs=jax.tree.map(lambda _: I...  20 us
    all_to_all x1, blocking collectives, exchange(): return lax.all_to_all(array, 'line', 0, 0, tiled=True)  17.6 us
    ppermute x7, waiting for transfers between devices, hop(): return lax.ppermute(array, ('head', 'pipe'), pairs)  14.9 us
    ppermute x1, starting transfers between devices, body(): carried_forward = lax.ppermute(total_forward, 'plane', up)  6.69 us
    all_to_all x1, waiting for transfers between devices, exchange(): return lax.all_to_all(array, 'line', 0, 0, tiled=True)  6.31 us
    all_to_all x1, starting transfers between devices, exchange(): return lax.all_to_all(array, 'line', 0, 0, tiled=True)  3.41 us
  transfers between devices with their start and end apart: 10, of which 6 were waited for; matrix products, arithmetic and copies ran while one was open for 0% of the time, Pallas kernels for 14%

profile of v6, /device:TPU:1, one launch (start us, length us, event | category | flops | bytes accessed | tf_op | source)
XLA Modules:
  0.0 102.1 jit_solution(4053372080866580881)
XLA Ops:
  0.6 2.2 %local.1 = bf16[8,144,128]{2,1,0:T(8,128)(2,1)S(1)} custom-call(f32[1,4,256]{2,1,0:T(4,128)} %rates_in.5, s32[1,256]{1,0:T(1,128)} %seg_in.5, bf16[1,256,512]{2,1,0:T(8,128)(2,1)} %q_in.5, bf16[1,256,512]{2,1,0:T(8,128)(2,1)} %o_in.5, bf16[1,256,512]{2,1,0:T(8,128)(2,1)} %k_in.5, bf16[1,256,512]{2,1,0:T(8,128)(2,1)} %v_in.3), custom_call_target="tpu_custom_call" | custom-call | tf_op jit(solution)/shard_map/local/pallas_call | solution.py:255
  2.8 17.6 %all_to_all.10.msg = bf16[8,144,128]{2,1,0:T(8,128)(2,1)S(1)} all-to-all(bf16[8,144,128]{2,1,0:T(8,128)(2,1)S(1)} %local.1), channel_id=1, replica_groups=mesh['plane'=8,'line'=8,'head'=8,'pipe'=2] {'line'}, dimensions={0} | all-to-all | bytes 589824 | tf_op jit(solution)/shard_map/all_to_all | solution.py:281
  20.5 1.3 %collective-permute-start = (bf16[80,128]{1,0:T(8,128)(2,1)S(1)}, bf16[80,128]{1,0:T(8,128)(2,1)S(1)}, u32[]{:S(2)}, u32[]{:S(2)}) collective-permute-start(bf16[80,128]{1,0:T(8,128)(2,1)S(1)} %get-tuple-element.33), channel_id=1, source_target_pairs={{128,0},{256,128},{384,256},{512,384},{640,512},{768,640},{896,768... | collective-permute-start | bytes 61448 | tf_op jit(solution)/shard_map/ppermute | solution.py:296
  21.8 6.7 %collective-permute-start.1 = (bf16[80,128]{1,0:T(8,128)(2,1)S(1)}, bf16[80,128]{1,0:T(8,128)(2,1)S(1)}, u32[]{:S(2)}, u32[]{:S(2)}) collective-permute-start(bf16[80,128]{1,0:T(8,128)(2,1)S(1)} %get-tuple-element.34), channel_id=1, source_target_pairs={{0,128},{128,256},{256,384},{384,512},{512,640},{640,768},{768,896... | collective-permute-start | bytes 61448 | tf_op jit(solution)/shard_map/ppermute | solution.py:297
  30.2 3.4 %all-to-all-start.1 = ((bf16[8,128,128]{2,1,0:T(8,128)(2,1)}), bf16[8,128,128]{2,1,0:T(8,128)(2,1)S(1)}, u32[]{:S(2)}, u32[]{:S(2)}) async-start(bf16[8,128,128]{2,1,0:T(8,128)(2,1)} %row_scan.1), calls=%async_computation.1 | async-start | bytes 524288 | tf_op jit(solution)/shard_map/all_to_all | solution.py:281
  33.7 2.9 %near.1 = (f32[256,512]{1,0:T(8,128)S(1)}, f32[256,512]{1,0:T(8,128)S(1)}, bf16[1,256,512]{2,1,0:T(8,128)(2,1)S(1)}, bf16[2,768,512]{2,1,0:T(8,128)(2,1)S(1)}) custom-call(s32[2]{0:T(128)S(1)} %pad_add_fusion.place.refs_0_, f32[1,4,256]{2,1,0:T(4,128)} %rates_in.5, s32[1,256]{1,0:T(1,128)} %seg_in.5, bf16[1,256,512]{2,1,0:T(8,128)(2,1)} %k_in.5, ...), custom_call_target="tpu_custom_call" | custom-call | tf_op jit(solution)/shard_map/near/pallas_call | solution.py:255
  36.5 6.3 %all-to-all-done.1.states = bf16[8,128,128]{2,1,0:T(8,128)(2,1)S(1)} async-done(((bf16[8,128,128]{2,1,0:T(8,128)(2,1)}), bf16[8,128,128]{2,1,0:T(8,128)(2,1)S(1)}, u32[]{:S(2)}, u32[]{:S(2)}) %all-to-all-start.1) | async-done | bytes 262176 | tf_op jit(solution)/shard_map/all_to_all | solution.py:281
  42.9 1.3 %far.1 = (bf16[256,512]{1,0:T(8,128)(2,1)S(1)}, bf16[2,256,768]{2,1,0:T(8,128)(2,1)S(1)}) custom-call(s32[2]{0:T(128)S(1)} %pad_add_fusion.place.refs_0_, f32[256,512]{1,0:T(8,128)S(1)} %get-tuple-element.30.local, f32[256,512]{1,0:T(8,128)S(1)} %get-tuple-element.47.gain, bf16[1,256,512]{2,1,0:T(8,128)(2,1)S(1)} %get-tuple-element.32.k, ...), custom_call_target="tpu_custom_call" | custom-call | tf_op jit(solution)/shard_map/far/pallas_call | solution.py:255
  44.1 3.3 %collective-permute-start.2 = (bf16[2,256,768]{2,1,0:T(8,128)(2,1)S(1)}, bf16[2,256,768]{2,1,0:T(8,128)(2,1)S(1)}, u32[]{:S(2)}, u32[]{:S(2)}) collective-permute-start(bf16[2,256,768]{2,1,0:T(8,128)(2,1)S(1)} %get-tuple-element.37), channel_id=1, source_target_pairs={{0,14},{1,3},{2,0},{3,5},{4,2},{5,7},{6,4},{7,9},{8,6},{9,11},{10,... | collective-permute-start | bytes 2359304 | tf_op jit(solution)/shard_map/ppermute | solution.py:342
  47.4 2.1 %partial_single.2 = bf16[1,256,768]{2,1,0:T(8,128)(2,1)S(1)} custom-call(s32[2]{0:T(128)S(1)} %pad_add_fusion.place.refs_0_, bf16[256,512]{1,0:T(8,128)(2,1)S(1)} %get-tuple-element.38.refs_1_, bf16[8,768,512]{2,1,0:T(8,128)(2,1)} %bitcast.8), custom_call_target="tpu_custom_call" | custom-call | tf_op jit(solution)/shard_map/partial_single/pallas_call | solution.py:255
  49.5 3.3 %collective-permute-start.3 = (bf16[1,256,768]{2,1,0:T(8,128)(2,1)S(1)}, bf16[1,256,768]{2,1,0:T(8,128)(2,1)S(1)}, u32[]{:S(2)}, u32[]{:S(2)}) collective-permute-start(bf16[1,256,768]{2,1,0:T(8,128)(2,1)S(1)} %partial_single.2), channel_id=1, source_target_pairs={{0,2},{1,15},{2,4},{3,1},{4,6},{5,3},{6,8},{7,5},{8,10},{9,7},{10,... | collective-permute-start | bytes 1179656 | tf_op jit(solution)/shard_map/ppermute | solution.py:369
  52.9 3.1 %partial_soon.2.refs_0_ = bf16[3,256,768]{2,1,0:T(8,128)(2,1)S(1)} custom-call(s32[2]{0:T(128)S(1)} %pad_add_fusion.place.refs_0_, bf16[256,512]{1,0:T(8,128)(2,1)S(1)} %get-tuple-element.38.refs_1_, bf16[8,768,512]{2,1,0:T(8,128)(2,1)} %bitcast.9), custom_call_target="tpu_custom_call" | custom-call | tf_op jit(solution)/shard_map/partial_soon/pallas_call | solution.py:255
  56.0 10.5 %collective-permute-start.4 = (bf16[1,256,768]{2,1,0:T(8,128)(2,1)S(1)}, bf16[1,256,768]{2,1,0:T(8,128)(2,1)S(1)}, u32[]{:S(2)}, u32[]{:S(2)}) collective-permute-start(bf16[1,256,768]{2,1,0:T(8,128)(2,1)S(1)} %slice.5), channel_id=1, source_target_pairs={{0,1},{1,0},{2,3},{3,2},{4,5},{5,4},{6,7},{7,6},{8,9},{9,8},{10,11... | collective-permute-start | bytes 1179656 | tf_op jit(solution)/shard_map/ppermute | solution.py:369
  66.7 1.1 %collective-permute-done.4.refs_0_ = bf16[1,256,768]{2,1,0:T(8,128)(2,1)S(1)} collective-permute-done((bf16[1,256,768]{2,1,0:T(8,128)(2,1)S(1)}, bf16[1,256,768]{2,1,0:T(8,128)(2,1)S(1)}, u32[]{:S(2)}, u32[]{:S(2)}) %collective-permute-start.4) | collective-permute-done | bytes 393248 | tf_op jit(solution)/shard_map/ppermute | solution.py:369
  67.8 1.9 %collective-permute-start.5 = (bf16[256,768]{1,0:T(8,128)(2,1)S(1)}, bf16[256,768]{1,0:T(8,128)(2,1)S(1)}, u32[]{:S(2)}, u32[]{:S(2)}) collective-permute-start(bf16[256,768]{1,0:T(8,128)(2,1)S(1)} %add_long.2), channel_id=1, source_target_pairs={{0,12},{1,5},{2,14},{3,7},{4,0},{5,9},{6,2},{7,11},{8,4},{9,13},{1... | collective-permute-start | bytes 1179656 | tf_op jit(solution)/shard_map/ppermute | solution.py:369
  69.7 4.0 %collective-permute-start.6 = (bf16[256,768]{1,0:T(8,128)(2,1)S(1)}, bf16[256,768]{1,0:T(8,128)(2,1)S(1)}, u32[]{:S(2)}, u32[]{:S(2)}) collective-permute-start(bf16[256,768]{1,0:T(8,128)(2,1)S(1)} %add_short.2), channel_id=1, source_target_pairs={{0,2},{1,15},{2,4},{3,1},{4,6},{5,3},{6,8},{7,5},{8,10},{9,7},{10,... | collective-permute-start | bytes 1179656 | tf_op jit(solution)/shard_map/ppermute | solution.py:369
  73.8 2.8 %partial_later.2 = (bf16[2,256,768]{2,1,0:T(8,128)(2,1)S(1)}, bf16[256,512]{1,0:T(8,128)(2,1)}) custom-call(s32[2]{0:T(128)S(1)} %pad_add_fusion.place.refs_0_, bf16[256,512]{1,0:T(8,128)(2,1)S(1)} %get-tuple-element.38.refs_1_, bf16[8,768,512]{2,1,0:T(8,128)(2,1)} %bitcast.10), custom_call_target="tpu_custom_call" | custom-call | tf_op jit(solution)/shard_map/partial_later/pallas_call | solution.py:255
  76.5 7.6 %collective-permute-done.5.refs_2_ = bf16[256,768]{1,0:T(8,128)(2,1)S(1)} collective-permute-done((bf16[256,768]{1,0:T(8,128)(2,1)S(1)}, bf16[256,768]{1,0:T(8,128)(2,1)S(1)}, u32[]{:S(2)}, u32[]{:S(2)}) %collective-permute-start.5) | collective-permute-done | bytes 393248 | tf_op jit(solution)/shard_map/ppermute | solution.py:369
  84.3 2.3 %collective-permute-done.6.refs_1_ = bf16[256,768]{1,0:T(8,128)(2,1)S(1)} collective-permute-done((bf16[256,768]{1,0:T(8,128)(2,1)S(1)}, bf16[256,768]{1,0:T(8,128)(2,1)S(1)}, u32[]{:S(2)}, u32[]{:S(2)}) %collective-permute-start.6) | collective-permute-done | bytes 393248 | tf_op jit(solution)/shard_map/ppermute | solution.py:369
  86.7 3.3 %collective-permute-start.7 = (bf16[256,768]{1,0:T(8,128)(2,1)S(1)}, bf16[256,768]{1,0:T(8,128)(2,1)S(1)}, u32[]{:S(2)}, u32[]{:S(2)}) collective-permute-start(bf16[256,768]{1,0:T(8,128)(2,1)S(1)} %add_long_last.2), channel_id=1, source_target_pairs={{0,15},{1,2},{2,1},{3,4},{4,3},{5,6},{6,5},{7,8},{8,7},{9,10},{10,... | collective-permute-start | bytes 1179656 | tf_op jit(solution)/shard_map/ppermute | solution.py:369
  90.0 3.7 %collective-permute-start.8 = (bf16[256,768]{1,0:T(8,128)(2,1)S(1)}, bf16[256,768]{1,0:T(8,128)(2,1)S(1)}, u32[]{:S(2)}, u32[]{:S(2)}) collective-permute-start(bf16[256,768]{1,0:T(8,128)(2,1)S(1)} %add_short_last.2), channel_id=1, source_target_pairs={{0,3},{1,14},{2,5},{3,0},{4,7},{5,2},{6,9},{7,4},{8,11},{9,6},{10,... | collective-permute-start | bytes 1179656 | tf_op jit(solution)/shard_map/ppermute | solution.py:369
  93.7 3.5 %query_key.1 = (bf16[256,512]{1,0:T(8,128)(2,1)}, bf16[256,512]{1,0:T(8,128)(2,1)}) custom-call(f32[1,4,256]{2,1,0:T(4,128)} %rates_in.5, s32[1,256]{1,0:T(1,128)} %seg_in.5, bf16[1,256,512]{2,1,0:T(8,128)(2,1)} %q_in.5, bf16[1,256,512]{2,1,0:T(8,128)(2,1)} %k_in.5, bf16[1,256,512]{2,1,0:T(8,128)(2,1)} %v_in.3, bf16[1,256,512]{2,1,0:T(8,128)(2,1)} %o_in.5, ...), custom_call_target="tpu_custom_call" | custom-call | tf_op jit(solution)/shard_map/query_key/pallas_call | solution.py:255
  97.3 3.9 %collective-permute-done.8.refs_2_ = bf16[256,768]{1,0:T(8,128)(2,1)S(1)} collective-permute-done((bf16[256,768]{1,0:T(8,128)(2,1)S(1)}, bf16[256,768]{1,0:T(8,128)(2,1)S(1)}, u32[]{:S(2)}, u32[]{:S(2)}) %collective-permute-start.8) | collective-permute-done | bytes 393248 | tf_op jit(solution)/shard_map/ppermute | solution.py:369
  101.2 0.9 add_last.1
  (13 shorter events, 2.3 us)
Async XLA Ops:
  20.5 8.0 %collective-permute-start = (bf16[80,128]{1,0:T(8,128)(2,1)S(1)}, bf16[80,128]{1,0:T(8,128)(2,1)S(1)}, u32[]{:S(2)}, u32[]{:S(2)}) collective-permute-start(bf16[80,128]{1,0:T(8,128)(2,1)S(1)} %get-tuple-element.33), channel_id=1, source_target_pairs={{128,0},{256,128},{384,256},{512,384},{640,512},{768,640},{896,768... | collective-permute-start | bytes 61448 | tf_op jit(solution)/shard_map/ppermute | solution.py:296
  21.8 7.6 %collective-permute-start.1 = (bf16[80,128]{1,0:T(8,128)(2,1)S(1)}, bf16[80,128]{1,0:T(8,128)(2,1)S(1)}, u32[]{:S(2)}, u32[]{:S(2)}) collective-permute-start(bf16[80,128]{1,0:T(8,128)(2,1)S(1)} %get-tuple-element.34), channel_id=1, source_target_pairs={{0,128},{128,256},{256,384},{384,512},{512,640},{640,768},{768,896... | collective-permute-start | bytes 61448 | tf_op jit(solution)/shard_map/ppermute | solution.py:297
  30.2 12.7 %all-to-all-start.1 = ((bf16[8,128,128]{2,1,0:T(8,128)(2,1)}), bf16[8,128,128]{2,1,0:T(8,128)(2,1)S(1)}, u32[]{:S(2)}, u32[]{:S(2)}) async-start(bf16[8,128,128]{2,1,0:T(8,128)(2,1)} %row_scan.1), calls=%async_computation.1 | async-start | bytes 524288 | tf_op jit(solution)/shard_map/all_to_all | solution.py:281
  44.1 22.5 %collective-permute-start.2 = (bf16[2,256,768]{2,1,0:T(8,128)(2,1)S(1)}, bf16[2,256,768]{2,1,0:T(8,128)(2,1)S(1)}, u32[]{:S(2)}, u32[]{:S(2)}) collective-permute-start(bf16[2,256,768]{2,1,0:T(8,128)(2,1)S(1)} %get-tuple-element.37), channel_id=1, source_target_pairs={{0,14},{1,3},{2,0},{3,5},{4,2},{5,7},{6,4},{7,9},{8,6},{9,11},{10,... | collective-permute-start | bytes 2359304 | tf_op jit(solution)/shard_map/ppermute | solution.py:342
  49.5 16.9 %collective-permute-start.3 = (bf16[1,256,768]{2,1,0:T(8,128)(2,1)S(1)}, bf16[1,256,768]{2,1,0:T(8,128)(2,1)S(1)}, u32[]{:S(2)}, u32[]{:S(2)}) collective-permute-start(bf16[1,256,768]{2,1,0:T(8,128)(2,1)S(1)} %partial_single.2), channel_id=1, source_target_pairs={{0,2},{1,15},{2,4},{3,1},{4,6},{5,3},{6,8},{7,5},{8,10},{9,7},{10,... | collective-permute-start | bytes 1179656 | tf_op jit(solution)/shard_map/ppermute | solution.py:369
  56.0 11.8 %collective-permute-start.4 = (bf16[1,256,768]{2,1,0:T(8,128)(2,1)S(1)}, bf16[1,256,768]{2,1,0:T(8,128)(2,1)S(1)}, u32[]{:S(2)}, u32[]{:S(2)}) collective-permute-start(bf16[1,256,768]{2,1,0:T(8,128)(2,1)S(1)} %slice.5), channel_id=1, source_target_pairs={{0,1},{1,0},{2,3},{3,2},{4,5},{5,4},{6,7},{7,6},{8,9},{9,8},{10,11... | collective-permute-start | bytes 1179656 | tf_op jit(solution)/shard_map/ppermute | solution.py:369
  67.8 16.4 %collective-permute-start.5 = (bf16[256,768]{1,0:T(8,128)(2,1)S(1)}, bf16[256,768]{1,0:T(8,128)(2,1)S(1)}, u32[]{:S(2)}, u32[]{:S(2)}) collective-permute-start(bf16[256,768]{1,0:T(8,128)(2,1)S(1)} %add_long.2), channel_id=1, source_target_pairs={{0,12},{1,5},{2,14},{3,7},{4,0},{5,9},{6,2},{7,11},{8,4},{9,13},{1... | collective-permute-start | bytes 1179656 | tf_op jit(solution)/shard_map/ppermute | solution.py:369
  69.7 16.8 %collective-permute-start.6 = (bf16[256,768]{1,0:T(8,128)(2,1)S(1)}, bf16[256,768]{1,0:T(8,128)(2,1)S(1)}, u32[]{:S(2)}, u32[]{:S(2)}) collective-permute-start(bf16[256,768]{1,0:T(8,128)(2,1)S(1)} %add_short.2), channel_id=1, source_target_pairs={{0,2},{1,15},{2,4},{3,1},{4,6},{5,3},{6,8},{7,5},{8,10},{9,7},{10,... | collective-permute-start | bytes 1179656 | tf_op jit(solution)/shard_map/ppermute | solution.py:369
  86.7 10.6 %collective-permute-start.7 = (bf16[256,768]{1,0:T(8,128)(2,1)S(1)}, bf16[256,768]{1,0:T(8,128)(2,1)S(1)}, u32[]{:S(2)}, u32[]{:S(2)}) collective-permute-start(bf16[256,768]{1,0:T(8,128)(2,1)S(1)} %add_long_last.2), channel_id=1, source_target_pairs={{0,15},{1,2},{2,1},{3,4},{4,3},{5,6},{6,5},{7,8},{8,7},{9,10},{10,... | collective-permute-start | bytes 1179656 | tf_op jit(solution)/shard_map/ppermute | solution.py:369
  90.0 11.2 %collective-permute-start.8 = (bf16[256,768]{1,0:T(8,128)(2,1)S(1)}, bf16[256,768]{1,0:T(8,128)(2,1)S(1)}, u32[]{:S(2)}, u32[]{:S(2)}) collective-permute-start(bf16[256,768]{1,0:T(8,128)(2,1)S(1)} %add_short_last.2), channel_id=1, source_target_pairs={{0,3},{1,14},{2,5},{3,0},{4,7},{5,2},{6,9},{7,4},{8,11},{9,6},{10,... | collective-permute-start | bytes 1179656 | tf_op jit(solution)/shard_map/ppermute | solution.py:369

commit v7 on v6

--- a/solution.py
+++ b/solution.py
@@ -98,9 +98,9 @@
 
 
 def near_kernel(place, rates_in, seg_in, k_in, q_in, o_in, w_in, gv, gain, k, w, rates, seg_row, q, o, sems):
-    w_pair = [w_in.at[destination(place, offset, w_in.shape[0])] for offset in PAIR]
-    sources = (rates_in, seg_in, k_in, q_in, o_in, *w_pair)
-    targets = (rates, seg_row, k, q, o, *(w.at[i] for i in range(len(PAIR))))
+    w_first = [w_in.at[destination(place, offset, w_in.shape[0])] for offset in FIRST]
+    sources = (rates_in, seg_in, k_in, q_in, o_in, *w_first)
+    targets = (rates, seg_row, k, q, o, *(w.at[i] for i in range(len(FIRST))))
     rates_copy, seg_copy, *others = fetch(sources, targets, sems)
     others, w_copies = others[:3], others[3:]
     rates_copy.wait()
@@ -120,7 +120,7 @@
         weight = decay_weight(cum[:, h : h + 1], cum_t[h : h + 1, :], keep)
         ks = scores(q[0, :, cols], k[0, :, cols], weight)
         gv[:, cols] = dot(ks, o[0, :, cols], ((0,), (0,)))
-        gain[:, cols] = jnp.broadcast_to(behind[:, h : h + 1], (n, dh))
+    gain[...] = jnp.pad(behind, ((0, 0), (0, gain.shape[1] - heads)))
     for copy in w_copies:
         copy.wait()
 
@@ -178,20 +178,20 @@
     return lax.rem(place[0] + groups + place[1] * offset, groups)
 
 
-PAIR = (-4, -2)
-SINGLE = (3,)
-SOON = (-3, 2, 0)
-LATER = (-1, 1)
-
-
-def far_kernel(place, local, gain, k, states, w, gv, pair):
+FIRST = (-4, -2, 3)
+SOON = (-3, 2)
+LATER = (-1, 1, 0)
+
+
+def far_kernel(local, gain, k, states, w, gv, pair, single):
     dh = states.shape[2]
     for h in range(gv.shape[1] // dh):
         cols = slice(h * dh, (h + 1) * dh)
         far = dot(k[0, :, cols], head_state(states, h, True), ((1,), (0,)))
-        gv[:, cols] = (local[:, cols] + gain[:, cols] * far).astype(bf16)
-    for i in range(len(PAIR)):
+        gv[:, cols] = (local[:, cols] + gain[:, h : h + 1] * far).astype(bf16)
+    for i in range(pair.shape[0]):
         pair[i] = dot(gv[...], w[i], ((1,), (1,))).astype(bf16)
+    single[...] = dot(gv[...], w[pair.shape[0]], ((1,), (1,))).astype(bf16)
 
 
 def partial_kernel(wanted, place, gv, w_in, out, *rest):
@@ -240,7 +240,7 @@
         far_q = dot(o[0, :, cols], f, ((1,), (1,)))
         far_k = dot(v[0, :, cols], b, ((1,), (1,)))
         dq[:, cols] = (dot(vs, k[0, :, cols], ((1,), (0,))) + reach[:, h : h + 1] * far_q).astype(bf16)
-        dk[:, cols] = (dot(vs, q[0, :, cols], ((0,), (0,))) + gain[:, cols] * far_k).astype(bf16)
+        dk[:, cols] = (dot(vs, q[0, :, cols], ((0,), (0,))) + gain[:, h : h + 1] * far_k).astype(bf16)
 
 
 IN_VMEM = pl.BlockSpec(memory_space=pltpu.VMEM)
@@ -301,22 +301,19 @@
     states = exchange(scanned)
     place = jnp.stack([lax.axis_index("head"), 1 - 2 * (lax.axis_index("pipe") & 1)]).astype(jnp.int32)
     weights = w_value.reshape(groups, step, width)
-    gv_local, gain, keys_near, w_pair = call(
+    gv_local, gain, keys_near, w_first = call(
         near_kernel,
-        (pltpu.VMEM((n, width), f32), pltpu.VMEM((n, width), f32), block, pltpu.VMEM((len(PAIR), step, width), bf16)),
+        (pltpu.VMEM((n, width), f32), pltpu.VMEM((n, dh), f32), block, pltpu.VMEM((len(FIRST), step, width), bf16)),
         "near",
         mib=12,
         in_specs=[IN_SMEM] + [IN_HBM] * 6,
-        scratch=[*small, block, block, dma((5 + len(PAIR),))],
+        scratch=[*small, block, block, dma((5 + len(FIRST),))],
     )(place, log_decay, segment_ids, keys, queries, out_grad, weights)
 
     part = pltpu.VMEM((n, step), bf16)
-    near_gv, pair = call(
-        far_kernel,
-        (pltpu.VMEM((n, width), bf16), pltpu.VMEM((2, n, step), bf16)),
-        "far",
-        in_specs=[IN_SMEM] + [IN_VMEM] * 5,
-    )(place, gv_local, gain, keys_near, states, w_pair)
+    near_gv, pair, single = call(
+        far_kernel, (pltpu.VMEM((n, width), bf16), pltpu.VMEM((2, n, step), bf16), part), "far"
+    )(gv_local, gain, keys_near, states, w_first)
 
     def products(wanted, gv, name, writes):
         count = len(wanted)
@@ -345,19 +342,17 @@
         return call(lambda *refs: add_kernel(own, picks, *refs), part, name)(partials, *arrived)
 
     pair_got = hop(pair, -1)
-    (single,) = products(SINGLE, near_gv, "partial_single", False)
     single_got = hop(single, 1)
     (soon,) = products(SOON, near_gv, "partial_soon", False)
-    own_got = hop(soon[2:], 0, True)
     long = add(soon, 0, (0,), "add_long", pair_got)
-    short = add(soon, 1, (0,), "add_short", single_got)
-    long, short, near_gv, own_got = lax.optimization_barrier((long, short, near_gv, own_got))
+    short = add(soon, 1, (None,), "add_short", single_got)
+    long, short, near_gv = lax.optimization_barrier((long, short, near_gv))
     later, grad_value = products(LATER, near_gv, "partial_later", True)
     long_got = hop(long, -2)
     short_got = hop(short, 1)
     long = add(later, 0, (1, None), "add_long_last", pair_got, long_got)
     short = add(later, 1, (None,), "add_short_last", short_got)
-    long, short, states, gain = lax.optimization_barrier((long, short, states, gain))
+    long, short, own, states, gain = lax.optimization_barrier((long, short, later[2:], states, gain))
     sections = lax.axis_size("pipe")
 
     def hop(array, distance, cross=False):
@@ -372,19 +367,17 @@
         return call(lambda *refs: add_kernel(own, picks, *refs), part, name)(partials, *arrived)
 
     pair_got = hop(pair, -1)
-    (single,) = products(SINGLE, near_gv, "partial_single", False)
     single_got = hop(single, 1)
     (soon,) = products(SOON, near_gv, "partial_soon", False)
-    own_got = hop(soon[2:], 0, True)
     long = add(soon, 0, (0,), "add_long", pair_got)
-    short = add(soon, 1, (0,), "add_short", single_got)
-    long, short, near_gv, own_got = lax.optimization_barrier((long, short, near_gv, own_got))
+    short = add(soon, 1, (None,), "add_short", single_got)
+    long, short, near_gv = lax.optimization_barrier((long, short, near_gv))
     later, grad_value = products(LATER, near_gv, "partial_later", True)
     long_got = hop(long, -2)
     short_got = hop(short, 1)
     long = add(later, 0, (1, None), "add_long_last", pair_got, long_got)
     short = add(later, 1, (None,), "add_short_last", short_got)
-    long, short, states, gain = lax.optimization_barrier((long, short, states, gain))
+    long, short, own, states, gain = lax.optimization_barrier((long, short, later[2:], states, gain))
     grad_query, grad_key = call(
         query_key_kernel,
         (jax.ShapeDtypeStruct((n, width), bf16), jax.ShapeDtypeStruct((n, width), bf16)),
@@ -395,6 +388,7 @@
     )(log_decay, segment_ids, queries, keys, values, out_grad, states, gain)
     long_got = hop(long, -1, True)
     short_got = hop(short, 1, True)
+    own_got = hop(own, 0, True)
     long_got, short_got, grad_query, grad_key = lax.optimization_barrier((long_got, short_got, grad_query, grad_key))
     grad_input = call(
         lambda *refs: add_kernel(0, (None, None), *refs), jax.ShapeDtypeStruct((n, step), bf16), "add_last"

time: 103 us -> 100 us (0.971)
  Pallas kernels: 20 us -> 17.6 us
  waiting for transfers between devices: 22.1 us -> 23.3 us
    pallas_call x14 -> x13, Pallas kernels: 20 us -> 17.6 us  [run(): pl.pallas_call(kernel, in_specs=specs, out_specs=jax.tree.map(lambda _: I...]
    ppermute x7, waiting for transfers between devices: 14.9 us -> 16.1 us  [hop(): return lax.ppermute(array, ('head', 'pipe'), pairs)]
  transfers between devices with their start and end apart: 10 -> 10, of which waited for: 6 -> 7; matrix products, arithmetic and copies ran while one was open for 0% -> 0% of each run, Pallas kernels for 14% -> 12%
where the time goes in v7:
time: 100 us; the launch traced here: 99.9 us
  starting transfers between devices  40.5 us (40%)
  waiting for transfers between devices  23.3 us (23%)
  Pallas kernels  17.6 us (18%)
  blocking collectives  17.6 us (18%)
    ppermute x7, starting transfers between devices, hop(): return lax.ppermute(array, ('head', 'pipe'), pairs)  29.1 us
    pallas_call x13, Pallas kernels, run(): pl.pallas_call(kernel, in_specs=specs, out_specs=jax.tree.map(lambda _: I...  17.6 us
    all_to_all x1, blocking collectives, exchange(): return lax.all_to_all(array, 'line', 0, 0, tiled=True)  17.6 us
    ppermute x7, waiting for transfers between devices, hop(): return lax.ppermute(array, ('head', 'pipe'), pairs)  16.1 us
    ppermute x1, starting transfers between devices, body(): carried_forward = lax.ppermute(total_forward, 'plane', up)  6.69 us
    all_to_all x1, waiting for transfers between devices, exchange(): return lax.all_to_all(array, 'line', 0, 0, tiled=True)  6.33 us
    all_to_all x1, starting transfers between devices, exchange(): return lax.all_to_all(array, 'line', 0, 0, tiled=True)  3.41 us
  transfers between devices with their start and end apart: 10, of which 7 were waited for; matrix products, arithmetic and copies ran while one was open for 0% of the time, Pallas kernels for 12%

profile of v7, /device:TPU:1, one launch (start us, length us, event | category | flops | bytes accessed | tf_op | source)
XLA Modules:
  0.0 99.9 jit_solution(16744039859610371527)
XLA Ops:
  0.6 2.2 %local.1 = bf16[8,144,128]{2,1,0:T(8,128)(2,1)S(1)} custom-call(f32[1,4,256]{2,1,0:T(4,128)} %rates_in.5, s32[1,256]{1,0:T(1,128)} %seg_in.5, bf16[1,256,512]{2,1,0:T(8,128)(2,1)} %q_in.5, bf16[1,256,512]{2,1,0:T(8,128)(2,1)} %o_in.5, bf16[1,256,512]{2,1,0:T(8,128)(2,1)} %k_in.5, bf16[1,256,512]{2,1,0:T(8,128)(2,1)} %v_in.3), custom_call_target="tpu_custom_call" | custom-call | tf_op jit(solution)/shard_map/local/pallas_call | solution.py:255
  2.8 17.6 %all_to_all.10.msg = bf16[8,144,128]{2,1,0:T(8,128)(2,1)S(1)} all-to-all(bf16[8,144,128]{2,1,0:T(8,128)(2,1)S(1)} %local.1), channel_id=1, replica_groups=mesh['plane'=8,'line'=8,'head'=8,'pipe'=2] {'line'}, dimensions={0} | all-to-all | bytes 589824 | tf_op jit(solution)/shard_map/all_to_all | solution.py:281
  20.5 1.3 %collective-permute-start = (bf16[80,128]{1,0:T(8,128)(2,1)S(1)}, bf16[80,128]{1,0:T(8,128)(2,1)S(1)}, u32[]{:S(2)}, u32[]{:S(2)}) collective-permute-start(bf16[80,128]{1,0:T(8,128)(2,1)S(1)} %get-tuple-element.34), channel_id=1, source_target_pairs={{128,0},{256,128},{384,256},{512,384},{640,512},{768,640},{896,768... | collective-permute-start | bytes 61448 | tf_op jit(solution)/shard_map/ppermute | solution.py:296
  21.8 6.7 %collective-permute-start.1 = (bf16[80,128]{1,0:T(8,128)(2,1)S(1)}, bf16[80,128]{1,0:T(8,128)(2,1)S(1)}, u32[]{:S(2)}, u32[]{:S(2)}) collective-permute-start(bf16[80,128]{1,0:T(8,128)(2,1)S(1)} %get-tuple-element.35), channel_id=1, source_target_pairs={{0,128},{128,256},{256,384},{384,512},{512,640},{640,768},{768,896... | collective-permute-start | bytes 61448 | tf_op jit(solution)/shard_map/ppermute | solution.py:297
  30.2 3.4 %all-to-all-start.1 = ((bf16[8,128,128]{2,1,0:T(8,128)(2,1)}), bf16[8,128,128]{2,1,0:T(8,128)(2,1)S(1)}, u32[]{:S(2)}, u32[]{:S(2)}) async-start(bf16[8,128,128]{2,1,0:T(8,128)(2,1)} %row_scan.1), calls=%async_computation.1 | async-start | bytes 524288 | tf_op jit(solution)/shard_map/all_to_all | solution.py:281
  33.7 2.8 %near.1 = (f32[256,512]{1,0:T(8,128)S(1)}, f32[256,128]{1,0:T(8,128)S(1)}, bf16[1,256,512]{2,1,0:T(8,128)(2,1)S(1)}, bf16[3,768,512]{2,1,0:T(8,128)(2,1)S(1)}) custom-call(s32[2]{0:T(128)S(1)} %pad_add_fusion.place.refs_0_, f32[1,4,256]{2,1,0:T(4,128)} %rates_in.5, s32[1,256]{1,0:T(1,128)} %seg_in.5, bf16[1,256,512]{2,1,0:T(8,128)(2,1)} %k_in.5, ...), custom_call_target="tpu_custom_call" | custom-call | tf_op jit(solution)/shard_map/near/pallas_call | solution.py:255
  36.5 6.3 %all-to-all-done.1.states = bf16[8,128,128]{2,1,0:T(8,128)(2,1)S(1)} async-done(((bf16[8,128,128]{2,1,0:T(8,128)(2,1)}), bf16[8,128,128]{2,1,0:T(8,128)(2,1)S(1)}, u32[]{:S(2)}, u32[]{:S(2)}) %all-to-all-start.1) | async-done | bytes 262176 | tf_op jit(solution)/shard_map/all_to_all | solution.py:281
  42.9 1.1 %far.1 = (bf16[256,512]{1,0:T(8,128)(2,1)S(1)}, bf16[2,256,768]{2,1,0:T(8,128)(2,1)S(1)}, bf16[256,768]{1,0:T(8,128)(2,1)S(1)}) custom-call(f32[256,512]{1,0:T(8,128)S(1)} %get-tuple-element.31.local, f32[256,128]{1,0:T(8,128)S(1)} %get-tuple-element.49.gain, bf16[1,256,512]{2,1,0:T(8,128)(2,1)S(1)} %get-tuple-element.33.k, ...), custom_call_target="tpu_custom_call" | custom-call | tf_op jit(solution)/shard_map/far/pallas_call | solution.py:255
  43.9 3.3 %collective-permute-start.2 = (bf16[2,256,768]{2,1,0:T(8,128)(2,1)S(1)}, bf16[2,256,768]{2,1,0:T(8,128)(2,1)S(1)}, u32[]{:S(2)}, u32[]{:S(2)}) collective-permute-start(bf16[2,256,768]{2,1,0:T(8,128)(2,1)S(1)} %get-tuple-element.38), channel_id=1, source_target_pairs={{0,14},{1,3},{2,0},{3,5},{4,2},{5,7},{6,4},{7,9},{8,6},{9,11},{10,... | collective-permute-start | bytes 2359304 | tf_op jit(solution)/shard_map/ppermute | solution.py:339
  47.2 3.3 %collective-permute-start.3 = (bf16[256,768]{1,0:T(8,128)(2,1)S(1)}, bf16[256,768]{1,0:T(8,128)(2,1)S(1)}, u32[]{:S(2)}, u32[]{:S(2)}) collective-permute-start(bf16[256,768]{1,0:T(8,128)(2,1)S(1)} %get-tuple-element.39), channel_id=1, source_target_pairs={{0,2},{1,15},{2,4},{3,1},{4,6},{5,3},{6,8},{7,5},{8,10},{9,7},{10,... | collective-permute-start | bytes 1179656 | tf_op jit(solution)/shard_map/ppermute | solution.py:339
  50.6 2.7 %partial_soon.2.refs_0_ = bf16[2,256,768]{2,1,0:T(8,128)(2,1)S(1)} custom-call(s32[2]{0:T(128)S(1)} %pad_add_fusion.place.refs_0_, bf16[256,512]{1,0:T(8,128)(2,1)S(1)} %get-tuple-element.40.refs_1_, bf16[8,768,512]{2,1,0:T(8,128)(2,1)} %bitcast.8), custom_call_target="tpu_custom_call" | custom-call | tf_op jit(solution)/shard_map/partial_soon/pallas_call | solution.py:255
  53.2 2.5 %collective-permute-done.3.refs_1_ = bf16[256,768]{1,0:T(8,128)(2,1)S(1)} collective-permute-done((bf16[256,768]{1,0:T(8,128)(2,1)S(1)}, bf16[256,768]{1,0:T(8,128)(2,1)S(1)}, u32[]{:S(2)}, u32[]{:S(2)}) %collective-permute-start.3) | collective-permute-done | bytes 393248 | tf_op jit(solution)/shard_map/ppermute | solution.py:339
  55.8 2.2 %collective-permute-done.2.refs_1_ = bf16[2,256,768]{2,1,0:T(8,128)(2,1)S(1)} collective-permute-done((bf16[2,256,768]{2,1,0:T(8,128)(2,1)S(1)}, bf16[2,256,768]{2,1,0:T(8,128)(2,1)S(1)}, u32[]{:S(2)}, u32[]{:S(2)}) %collective-permute-start.2) | collective-permute-done | bytes 786464 | tf_op jit(solution)/shard_map/ppermute | solution.py:339
  58.1 6.5 %collective-permute-start.4 = (bf16[256,768]{1,0:T(8,128)(2,1)S(1)}, bf16[256,768]{1,0:T(8,128)(2,1)S(1)}, u32[]{:S(2)}, u32[]{:S(2)}) collective-permute-start(bf16[256,768]{1,0:T(8,128)(2,1)S(1)} %add_long.2), channel_id=1, source_target_pairs={{0,12},{1,5},{2,14},{3,7},{4,0},{5,9},{6,2},{7,11},{8,4},{9,13},{1... | collective-permute-start | bytes 1179656 | tf_op jit(solution)/shard_map/ppermute | solution.py:364
  64.6 1.9 %collective-permute-start.5 = (bf16[256,768]{1,0:T(8,128)(2,1)S(1)}, bf16[256,768]{1,0:T(8,128)(2,1)S(1)}, u32[]{:S(2)}, u32[]{:S(2)}) collective-permute-start(bf16[256,768]{1,0:T(8,128)(2,1)S(1)} %add_short.2), channel_id=1, source_target_pairs={{0,2},{1,15},{2,4},{3,1},{4,6},{5,3},{6,8},{7,5},{8,10},{9,7},{10,... | collective-permute-start | bytes 1179656 | tf_op jit(solution)/shard_map/ppermute | solution.py:364
  66.6 3.2 %partial_later.2 = (bf16[3,256,768]{2,1,0:T(8,128)(2,1)S(1)}, bf16[256,512]{1,0:T(8,128)(2,1)}) custom-call(s32[2]{0:T(128)S(1)} %pad_add_fusion.place.refs_0_, bf16[256,512]{1,0:T(8,128)(2,1)S(1)} %get-tuple-element.40.refs_1_, bf16[8,768,512]{2,1,0:T(8,128)(2,1)} %bitcast.9), custom_call_target="tpu_custom_call" | custom-call | tf_op jit(solution)/shard_map/partial_later/pallas_call | solution.py:255
  69.8 2.1 %collective-permute-done.4.refs_2_ = bf16[256,768]{1,0:T(8,128)(2,1)S(1)} collective-permute-done((bf16[256,768]{1,0:T(8,128)(2,1)S(1)}, bf16[256,768]{1,0:T(8,128)(2,1)S(1)}, u32[]{:S(2)}, u32[]{:S(2)}) %collective-permute-start.4) | collective-permute-done | bytes 393248 | tf_op jit(solution)/shard_map/ppermute | solution.py:364
  72.0 6.5 %collective-permute-done.5.refs_1_ = bf16[256,768]{1,0:T(8,128)(2,1)S(1)} collective-permute-done((bf16[256,768]{1,0:T(8,128)(2,1)S(1)}, bf16[256,768]{1,0:T(8,128)(2,1)S(1)}, u32[]{:S(2)}, u32[]{:S(2)}) %collective-permute-start.5) | collective-permute-done | bytes 393248 | tf_op jit(solution)/shard_map/ppermute | solution.py:364
  78.6 7.6 %collective-permute-start.6 = (bf16[256,768]{1,0:T(8,128)(2,1)S(1)}, bf16[256,768]{1,0:T(8,128)(2,1)S(1)}, u32[]{:S(2)}, u32[]{:S(2)}) collective-permute-start(bf16[256,768]{1,0:T(8,128)(2,1)S(1)} %add_long_last.2), channel_id=1, source_target_pairs={{0,15},{1,2},{2,1},{3,4},{4,3},{5,6},{6,5},{7,8},{8,7},{9,10},{10,... | collective-permute-start | bytes 1179656 | tf_op jit(solution)/shard_map/ppermute | solution.py:364
  86.3 2.1 %collective-permute-start.7 = (bf16[256,768]{1,0:T(8,128)(2,1)S(1)}, bf16[256,768]{1,0:T(8,128)(2,1)S(1)}, u32[]{:S(2)}, u32[]{:S(2)}) collective-permute-start(bf16[256,768]{1,0:T(8,128)(2,1)S(1)} %add_short_last.2), channel_id=1, source_target_pairs={{0,3},{1,14},{2,5},{3,0},{4,7},{5,2},{6,9},{7,4},{8,11},{9,6},{10,... | collective-permute-start | bytes 1179656 | tf_op jit(solution)/shard_map/ppermute | solution.py:364
  88.4 4.3 %collective-permute-start.8 = (bf16[1,256,768]{2,1,0:T(8,128)(2,1)S(1)}, bf16[1,256,768]{2,1,0:T(8,128)(2,1)S(1)}, u32[]{:S(2)}, u32[]{:S(2)}) collective-permute-start(bf16[1,256,768]{2,1,0:T(8,128)(2,1)S(1)} %slice.4), channel_id=1, source_target_pairs={{0,1},{1,0},{2,3},{3,2},{4,5},{5,4},{6,7},{7,6},{8,9},{9,8},{10,11... | collective-permute-start | bytes 1179656 | tf_op jit(solution)/shard_map/ppermute | solution.py:364
  92.7 3.5 %query_key.1 = (bf16[256,512]{1,0:T(8,128)(2,1)}, bf16[256,512]{1,0:T(8,128)(2,1)}) custom-call(f32[1,4,256]{2,1,0:T(4,128)} %rates_in.5, s32[1,256]{1,0:T(1,128)} %seg_in.5, bf16[1,256,512]{2,1,0:T(8,128)(2,1)} %q_in.5, bf16[1,256,512]{2,1,0:T(8,128)(2,1)} %k_in.5, bf16[1,256,512]{2,1,0:T(8,128)(2,1)} %v_in.3, bf16[1,256,512]{2,1,0:T(8,128)(2,1)} %o_in.5, ...), custom_call_target="tpu_custom_call" | custom-call | tf_op jit(solution)/shard_map/query_key/pallas_call | solution.py:255
  96.2 2.8 %collective-permute-done.7.refs_2_ = bf16[256,768]{1,0:T(8,128)(2,1)S(1)} collective-permute-done((bf16[256,768]{1,0:T(8,128)(2,1)S(1)}, bf16[256,768]{1,0:T(8,128)(2,1)S(1)}, u32[]{:S(2)}, u32[]{:S(2)}) %collective-permute-start.7) | collective-permute-done | bytes 393248 | tf_op jit(solution)/shard_map/ppermute | solution.py:364
  99.0 0.9 add_last.1
  (12 shorter events, 2.3 us)
Async XLA Ops:
  20.5 8.0 %collective-permute-start = (bf16[80,128]{1,0:T(8,128)(2,1)S(1)}, bf16[80,128]{1,0:T(8,128)(2,1)S(1)}, u32[]{:S(2)}, u32[]{:S(2)}) collective-permute-start(bf16[80,128]{1,0:T(8,128)(2,1)S(1)} %get-tuple-element.34), channel_id=1, source_target_pairs={{128,0},{256,128},{384,256},{512,384},{640,512},{768,640},{896,768... | collective-permute-start | bytes 61448 | tf_op jit(solution)/shard_map/ppermute | solution.py:296
  21.8 7.6 %collective-permute-start.1 = (bf16[80,128]{1,0:T(8,128)(2,1)S(1)}, bf16[80,128]{1,0:T(8,128)(2,1)S(1)}, u32[]{:S(2)}, u32[]{:S(2)}) collective-permute-start(bf16[80,128]{1,0:T(8,128)(2,1)S(1)} %get-tuple-element.35), channel_id=1, source_target_pairs={{0,128},{128,256},{256,384},{384,512},{512,640},{640,768},{768,896... | collective-permute-start | bytes 61448 | tf_op jit(solution)/shard_map/ppermute | solution.py:297
  30.2 12.7 %all-to-all-start.1 = ((bf16[8,128,128]{2,1,0:T(8,128)(2,1)}), bf16[8,128,128]{2,1,0:T(8,128)(2,1)S(1)}, u32[]{:S(2)}, u32[]{:S(2)}) async-start(bf16[8,128,128]{2,1,0:T(8,128)(2,1)} %row_scan.1), calls=%async_computation.1 | async-start | bytes 524288 | tf_op jit(solution)/shard_map/all_to_all | solution.py:281
  43.9 14.1 %collective-permute-start.2 = (bf16[2,256,768]{2,1,0:T(8,128)(2,1)S(1)}, bf16[2,256,768]{2,1,0:T(8,128)(2,1)S(1)}, u32[]{:S(2)}, u32[]{:S(2)}) collective-permute-start(bf16[2,256,768]{2,1,0:T(8,128)(2,1)S(1)} %get-tuple-element.38), channel_id=1, source_target_pairs={{0,14},{1,3},{2,0},{3,5},{4,2},{5,7},{6,4},{7,9},{8,6},{9,11},{10,... | collective-permute-start | bytes 2359304 | tf_op jit(solution)/shard_map/ppermute | solution.py:339
  47.2 8.5 %collective-permute-start.3 = (bf16[256,768]{1,0:T(8,128)(2,1)S(1)}, bf16[256,768]{1,0:T(8,128)(2,1)S(1)}, u32[]{:S(2)}, u32[]{:S(2)}) collective-permute-start(bf16[256,768]{1,0:T(8,128)(2,1)S(1)} %get-tuple-element.39), channel_id=1, source_target_pairs={{0,2},{1,15},{2,4},{3,1},{4,6},{5,3},{6,8},{7,5},{8,10},{9,7},{10,... | collective-permute-start | bytes 1179656 | tf_op jit(solution)/shard_map/ppermute | solution.py:339
  58.1 13.8 %collective-permute-start.4 = (bf16[256,768]{1,0:T(8,128)(2,1)S(1)}, bf16[256,768]{1,0:T(8,128)(2,1)S(1)}, u32[]{:S(2)}, u32[]{:S(2)}) collective-permute-start(bf16[256,768]{1,0:T(8,128)(2,1)S(1)} %add_long.2), channel_id=1, source_target_pairs={{0,12},{1,5},{2,14},{3,7},{4,0},{5,9},{6,2},{7,11},{8,4},{9,13},{1... | collective-permute-start | bytes 1179656 | tf_op jit(solution)/shard_map/ppermute | solution.py:364
  64.6 13.9 %collective-permute-start.5 = (bf16[256,768]{1,0:T(8,128)(2,1)S(1)}, bf16[256,768]{1,0:T(8,128)(2,1)S(1)}, u32[]{:S(2)}, u32[]{:S(2)}) collective-permute-start(bf16[256,768]{1,0:T(8,128)(2,1)S(1)} %add_short.2), channel_id=1, source_target_pairs={{0,2},{1,15},{2,4},{3,1},{4,6},{5,3},{6,8},{7,5},{8,10},{9,7},{10,... | collective-permute-start | bytes 1179656 | tf_op jit(solution)/shard_map/ppermute | solution.py:364
  78.6 17.6 %collective-permute-start.6 = (bf16[256,768]{1,0:T(8,128)(2,1)S(1)}, bf16[256,768]{1,0:T(8,128)(2,1)S(1)}, u32[]{:S(2)}, u32[]{:S(2)}) collective-permute-start(bf16[256,768]{1,0:T(8,128)(2,1)S(1)} %add_long_last.2), channel_id=1, source_target_pairs={{0,15},{1,2},{2,1},{3,4},{4,3},{5,6},{6,5},{7,8},{8,7},{9,10},{10,... | collective-permute-start | bytes 1179656 | tf_op jit(solution)/shard_map/ppermute | solution.py:364
  86.3 12.8 %collective-permute-start.7 = (bf16[256,768]{1,0:T(8,128)(2,1)S(1)}, bf16[256,768]{1,0:T(8,128)(2,1)S(1)}, u32[]{:S(2)}, u32[]{:S(2)}) collective-permute-start(bf16[256,768]{1,0:T(8,128)(2,1)S(1)} %add_short_last.2), channel_id=1, source_target_pairs={{0,3},{1,14},{2,5},{3,0},{4,7},{5,2},{6,9},{7,4},{8,11},{9,6},{10,... | collective-permute-start | bytes 1179656 | tf_op jit(solution)/shard_map/ppermute | solution.py:364
  88.4 10.6 %collective-permute-start.8 = (bf16[1,256,768]{2,1,0:T(8,128)(2,1)S(1)}, bf16[1,256,768]{2,1,0:T(8,128)(2,1)S(1)}, u32[]{:S(2)}, u32[]{:S(2)}) collective-permute-start(bf16[1,256,768]{2,1,0:T(8,128)(2,1)S(1)} %slice.4), channel_id=1, source_target_pairs={{0,1},{1,0},{2,3},{3,2},{4,5},{5,4},{6,7},{7,6},{8,9},{9,8},{10,11... | collective-permute-start | bytes 1179656 | tf_op jit(solution)/shard_map/ppermute | solution.py:364

commit v8 on v7

--- a/solution.py
+++ b/solution.py
@@ -34,18 +34,15 @@
     return lax.dot_general(rates, upper, (((1,), (0,)), ((), ())), precision=HIGHEST, preferred_element_type=f32)
 
 
-def write_message(out, h, states, first, last, through, width):
-    share = states[0].shape[0] // 2
+def write_message(out, piece, state, entry, leave, through, width):
+    rows = state.shape[0]
     high = through.astype(bf16)
     low = (through - high.astype(f32)).astype(bf16)
     row = lax.broadcasted_iota(jnp.int32, (META, width), 0)
-    meta = jnp.where(row == 0, first, jnp.where(row == 1, last, 0.0))
+    meta = jnp.where(row == 0, entry, jnp.where(row == 1, leave, 0.0))
     meta = jnp.where(row == 2, high.astype(f32), jnp.where(row == 3, low.astype(f32), meta)).astype(bf16)
-    for half in range(2):
-        p = 2 * h + half
-        for i, state in enumerate(states):
-            out[p, i * share : (i + 1) * share, :] = state[half * share : (half + 1) * share].astype(bf16)
-        out[p, 2 * share : 2 * share + META, :] = meta
+    out[piece, 0:rows, :] = state.astype(bf16)
+    out[piece, rows : rows + META, :] = meta
 
 
 def ids_column(seg_row):
@@ -66,7 +63,7 @@
     return copies
 
 
-def local_kernel(rates_in, seg_in, q_in, o_in, k_in, v_in, out, rates, seg_row, q, o, k, v, sems):
+def local_kernel(_, rates_in, seg_in, q_in, o_in, k_in, v_in, out, rates, seg_row, q, o, k, v, sems):
     sources = (rates_in, seg_in, q_in, o_in, k_in, v_in)
     rates_copy, seg_copy, *others = fetch(sources, (rates, seg_row, q, o, k, v), sems)
     rates_copy.wait()
@@ -85,8 +82,9 @@
         cols = slice(h * dh, (h + 1) * dh)
         scaled_q = (q[0, :, cols].astype(f32) * ahead[:, h : h + 1]).astype(bf16)
         scaled_k = (k[0, :, cols].astype(f32) * behind[:, h : h + 1]).astype(bf16)
-        states = (dot(scaled_q, o[0, :, cols], ((0,), (0,))), dot(scaled_k, v[0, :, cols], ((0,), (0,))))
-        write_message(out, h, states, first, last, jnp.exp(cum[n - 1 : n, h : h + 1]), dh)
+        through = jnp.exp(cum[n - 1 : n, h : h + 1])
+        write_message(out, h, dot(scaled_q, o[0, :, cols], ((0,), (0,))), last, first, through, dh)
+        write_message(out, heads + h, dot(scaled_k, v[0, :, cols], ((0,), (0,))), first, last, through, dh)
 
 
 def scores(a, b, weight):
@@ -125,53 +123,40 @@
         copy.wait()
 
 
-def unpack(msg, y, reverse):
-    share = (msg.shape[1] - META) // 2
-    start = 0 if reverse else share
-    meta = msg[y, 2 * share : 2 * share + META, :].astype(f32)
-    state = msg[y, start : start + share, :].astype(f32)
-    return state, meta[0:1], meta[1:2], meta[2:3] + meta[3:4]
-
-
-def order(reverse):
-    return range(ROW - 1, -1, -1) if reverse else range(ROW)
-
-
-def row_total_kernel(msg, out_backward, out_forward):
-    for out, reverse in ((out_backward, True), (out_forward, False)):
-        share = out.shape[0] - META
-        tag, total = None, None
-        for y in order(reverse):
-            state, first, last, through = unpack(msg, y, reverse)
-            if total is None:
-                total = state
-            else:
-                same = jnp.where((first == last) & (tag == last), through, 0.0)
-                total = same * total + state
-            tag = first if reverse else last
-        out[0:share, :] = total.astype(bf16)
-        out[share:, :] = jnp.broadcast_to(tag, (META, tag.shape[1])).astype(bf16)
-
-
-def row_scan_kernel(msg, carried_backward, carried_forward, out):
-    for carried, reverse in ((carried_backward, True), (carried_forward, False)):
-        share = carried.shape[0] - META
-        start = 0 if reverse else share
-        running = carried[0:share, :].astype(f32)
-        tag = carried[share : share + META, :].astype(f32)[0:1]
-        for y in order(reverse):
-            state, first, last, through = unpack(msg, y, reverse)
-            edge = last if reverse else first
-            out[y, start : start + share, :] = jnp.where(edge == tag, running, 0.0).astype(bf16)
-            same = jnp.where((first == last) & (tag == last), through, 0.0)
-            running = same * running + state
-            tag = first if reverse else last
-
-
-def head_state(states, h, reverse):
-    share = states.shape[1] // 2
-    start = 0 if reverse else share
-    return jnp.concatenate([states[2 * h + half, start : start + share, :] for half in range(2)], axis=0)
+def unpack(msg, y):
+    rows = msg.shape[1] - META
+    block = msg[y].astype(f32)
+    meta = block[rows:]
+    return block[:rows], meta[0:1], meta[1:2], meta[2:3] + meta[3:4]
+
+
+def block_at(place, k):
+    return jnp.where(place[2] > 0, ROW - 1 - k, k)
+
+
+def row_total_kernel(place, msg, out):
+    rows = out.shape[0] - META
+    total, _, tag, _ = unpack(msg, block_at(place, 0))
+    for k in range(1, ROW):
+        state, entry, leave, through = unpack(msg, block_at(place, k))
+        same = jnp.where((entry == leave) & (tag == entry), through, 0.0)
+        total = same * total + state
+        tag = leave
+    out[0:rows, :] = total.astype(bf16)
+    out[rows:, :] = jnp.broadcast_to(tag, (META, tag.shape[1])).astype(bf16)
+
+
+def row_scan_kernel(place, msg, carried, out):
+    rows = carried.shape[0] - META
+    running = carried[0:rows, :].astype(f32)
+    tag = carried[rows : rows + META, :].astype(f32)[0:1]
+    for k in range(ROW):
+        y = block_at(place, k)
+        state, entry, leave, through = unpack(msg, y)
+        out[y] = jnp.where(entry == tag, running, 0.0).astype(bf16)
+        same = jnp.where((entry == leave) & (tag == entry), through, 0.0)
+        running = same * running + state
+        tag = leave
 
 
 def destination(place, offset, groups):
@@ -187,7 +172,7 @@
     dh = states.shape[2]
     for h in range(gv.shape[1] // dh):
         cols = slice(h * dh, (h + 1) * dh)
-        far = dot(k[0, :, cols], head_state(states, h, True), ((1,), (0,)))
+        far = dot(k[0, :, cols], states[h], ((1,), (0,)))
         gv[:, cols] = (local[:, cols] + gain[:, h : h + 1] * far).astype(bf16)
     for i in range(pair.shape[0]):
         pair[i] = dot(gv[...], w[i], ((1,), (1,))).astype(bf16)
@@ -235,8 +220,8 @@
         cols = slice(h * dh, (h + 1) * dh)
         weight = decay_weight(cum[:, h : h + 1], cum_t[h : h + 1, :], keep)
         vs = scores(o[0, :, cols], v[0, :, cols], weight)
-        f = head_state(states, h, False)
-        b = head_state(states, h, True)
+        f = states[heads + h]
+        b = states[h]
         far_q = dot(o[0, :, cols], f, ((1,), (1,)))
         far_k = dot(v[0, :, cols], b, ((1,), (1,)))
         dq[:, cols] = (dot(vs, k[0, :, cols], ((1,), (0,))) + reach[:, h : h + 1] * far_q).astype(bf16)
@@ -271,7 +256,6 @@
     dh = width // heads
     planes = lax.axis_size("plane")
     groups = lax.axis_size("head")
-    share = heads * dh // ROW
     step = w_value.shape[1] // groups
     block = pltpu.VMEM((1, n, width), bf16)
     small = [pltpu.VMEM(log_decay.shape, f32), pltpu.VMEM(segment_ids.shape, jnp.int32)]
@@ -280,26 +264,33 @@
     def exchange(array):
         return lax.all_to_all(array, "line", 0, 0, tiled=True)
 
+    lines = lax.axis_size("line")
+    back = lines // 2
+    scans_back = (lax.axis_index("line") < back).astype(jnp.int32)
+    place = jnp.stack([lax.axis_index("head"), 1 - 2 * (lax.axis_index("pipe") & 1), scans_back]).astype(jnp.int32)
     sent = call(
         local_kernel,
-        pltpu.VMEM((ROW, 2 * share + META, dh), bf16),
+        pltpu.VMEM((ROW, dh + META, dh), bf16),
         "local",
         mib=12,
-        in_specs=[IN_HBM] * 6,
+        in_specs=[IN_SMEM] + [IN_HBM] * 6,
         scratch=[*small, block, block, block, block, dma((6,))],
-    )(log_decay, segment_ids, queries, out_grad, keys, values)
+    )(place, log_decay, segment_ids, queries, out_grad, keys, values)
     got = exchange(sent)
-    total = pltpu.VMEM((share + META, dh), bf16)
-    total_backward, total_forward = call(row_total_kernel, (total, total), "row_total")(got)
-    up = [(z - 1, z) for z in range(1, planes)]
-    down = [(z, z - 1) for z in range(1, planes)]
-    carried_backward = lax.ppermute(total_backward, "plane", down)
-    carried_forward = lax.ppermute(total_forward, "plane", up)
-    scanned = call(row_scan_kernel, pltpu.VMEM((ROW, 2 * share, dh), bf16), "row_scan")(
-        got, carried_backward, carried_forward
+    total = call(row_total_kernel, pltpu.VMEM((dh + META, dh), bf16), "row_total", in_specs=[IN_SMEM, IN_VMEM])(
+        place, got
     )
+    pairs = []
+    for z in range(planes):
+        for y in range(lines):
+            to = z - 1 if y < back else z + 1
+            if 0 <= to < planes:
+                pairs.append((z * lines + y, to * lines + y))
+    carried = lax.ppermute(total, ("plane", "line"), pairs)
+    scanned = call(
+        row_scan_kernel, pltpu.VMEM((ROW, dh, dh), bf16), "row_scan", in_specs=[IN_SMEM, IN_VMEM, IN_VMEM]
+    )(place, got, carried)
     states = exchange(scanned)
-    place = jnp.stack([lax.axis_index("head"), 1 - 2 * (lax.axis_index("pipe") & 1)]).astype(jnp.int32)
     weights = w_value.reshape(groups, step, width)
     gv_local, gain, keys_near, w_first = call(
         near_kernel,

time: 100 us -> 101 us (1.010)
  starting transfers between devices: 40.5 us -> 33.4 us
  waiting for transfers between devices: 23.3 us -> 29.1 us
  Pallas kernels: 17.6 us -> 19.3 us
    ppermute x2 -> x1, starting transfers between devices: 7.99 us -> 1.29 us  [body(): carried = lax.ppermute(total, ('plane', 'line'), pairs)]
    ppermute x2 -> x1, waiting for transfers between devices: 0.88 us -> 6.41 us  [body(): carried = lax.ppermute(total, ('plane', 'line'), pairs)]
    pallas_call x13, Pallas kernels: 17.6 us -> 19.3 us  [run(): pl.pallas_call(kernel, in_specs=specs, out_specs=jax.tree.map(lambda _: I...]
  transfers between devices with their start and end apart: 10 -> 9, of which waited for: 7 -> 7; matrix products, arithmetic and copies ran while one was open for 0% -> 0% of each run, Pallas kernels for 12% -> 12%
where the time goes in v8:
time: 101 us; the launch traced here: 100 us
  starting transfers between devices  33.4 us (33%)
  waiting for transfers between devices  29.1 us (29%)
  Pallas kernels  19.3 us (19%)
  blocking collectives  17.6 us (17%)
    ppermute x7, starting transfers between devices, hop(): return lax.ppermute(array, ('head', 'pipe'), pairs)  28.7 us
    pallas_call x13, Pallas kernels, run(): pl.pallas_call(kernel, in_specs=specs, out_specs=jax.tree.map(lambda _: I...  19.3 us
    all_to_all x1, blocking collectives, exchange(): return lax.all_to_all(array, 'line', 0, 0, tiled=True)  17.6 us
    ppermute x7, waiting for transfers between devices, hop(): return lax.ppermute(array, ('head', 'pipe'), pairs)  16.2 us
    ppermute x1, waiting for transfers between devices, body(): carried = lax.ppermute(total, ('plane', 'line'), pairs)  6.41 us
    all_to_all x1, waiting for transfers between devices, exchange(): return lax.all_to_all(array, 'line', 0, 0, tiled=True)  6.4 us
    all_to_all x1, starting transfers between devices, exchange(): return lax.all_to_all(array, 'line', 0, 0, tiled=True)  3.41 us
  transfers between devices with their start and end apart: 9, of which 7 were waited for; matrix products, arithmetic and copies ran while one was open for 0% of the time, Pallas kernels for 12%

profile of v8, /device:TPU:1, one launch (start us, length us, event | category | flops | bytes accessed | tf_op | source)
XLA Modules:
  0.0 100.2 jit_solution(3757113907202768137)
XLA Ops:
  0.7 2.8 %local.1 = bf16[8,144,128]{2,1,0:T(8,128)(2,1)S(1)} custom-call(s32[3]{0:T(128)S(1)} %pad_add_fusion.place._.refs_0_, f32[1,4,256]{2,1,0:T(4,128)} %rates_in.5, s32[1,256]{1,0:T(1,128)} %seg_in.5, bf16[1,256,512]{2,1,0:T(8,128)(2,1)} %q_in.5, bf16[1,256,512]{2,1,0:T(8,128)(2,1)} %o_in.5, bf16[1,256,512]{2,1,0:T(8,128)(2,1)} %k_in.5, bf16[1,256,512]{2,1,0:T(8,128)(2,1)} %v_in.3), custom_call_target="tpu_custom_call" | custom-call | tf_op jit(solution)/shard_map/local/pallas_call | solution.py:240
  3.5 17.6 %all_to_all.10.msg = bf16[8,144,128]{2,1,0:T(8,128)(2,1)S(1)} all-to-all(bf16[8,144,128]{2,1,0:T(8,128)(2,1)S(1)} %local.1), channel_id=1, replica_groups=mesh['plane'=8,'line'=8,'head'=8,'pipe'=2] {'line'}, dimensions={0} | all-to-all | bytes 589824 | tf_op jit(solution)/shard_map/all_to_all | solution.py:265
  21.7 1.3 %collective-permute-start = (bf16[144,128]{1,0:T(8,128)(2,1)S(1)}, bf16[144,128]{1,0:T(8,128)(2,1)S(1)}, u32[]{:S(2)}, u32[]{:S(2)}) collective-permute-start(bf16[144,128]{1,0:T(8,128)(2,1)S(1)} %row_total.1), channel_id=1, source_target_pairs={{64,192},{80,208},{96,224},{112,240},{128,0},{144,16},{160,32},{17... | collective-permute-start | bytes 110600 | tf_op jit(solution)/shard_map/ppermute | solution.py:289
  23.0 6.4 %collective-permute-done.carried = bf16[144,128]{1,0:T(8,128)(2,1)S(1)} collective-permute-done((bf16[144,128]{1,0:T(8,128)(2,1)S(1)}, bf16[144,128]{1,0:T(8,128)(2,1)S(1)}, u32[]{:S(2)}, u32[]{:S(2)}) %collective-permute-start) | collective-permute-done | bytes 36896 | tf_op jit(solution)/shard_map/ppermute | solution.py:289
  29.4 1.3 %row_scan.1 = bf16[8,128,128]{2,1,0:T(8,128)(2,1)} custom-call(s32[3]{0:T(128)S(1)} %pad_add_fusion.place._.refs_0_, bf16[8,144,128]{2,1,0:T(8,128)(2,1)S(1)} %all_to_all.10.msg, bf16[144,128]{1,0:T(8,128)(2,1)S(1)} %collective-permute-done.carried), custom_call_target="tpu_custom_call" | custom-call | tf_op jit(solution)/shard_map/row_scan/pallas_call | solution.py:240
  30.8 3.4 %all-to-all-start.1 = ((bf16[8,128,128]{2,1,0:T(8,128)(2,1)}), bf16[8,128,128]{2,1,0:T(8,128)(2,1)S(1)}, u32[]{:S(2)}, u32[]{:S(2)}) async-start(bf16[8,128,128]{2,1,0:T(8,128)(2,1)} %row_scan.1), calls=%async_computation.1 | async-start | bytes 524288 | tf_op jit(solution)/shard_map/all_to_all | solution.py:265
  34.2 2.8 %near.1 = (f32[256,512]{1,0:T(8,128)S(1)}, f32[256,128]{1,0:T(8,128)S(1)}, bf16[1,256,512]{2,1,0:T(8,128)(2,1)S(1)}, bf16[3,768,512]{2,1,0:T(8,128)(2,1)S(1)}) custom-call(s32[3]{0:T(128)S(1)} %pad_add_fusion.place._.refs_0_, f32[1,4,256]{2,1,0:T(4,128)} %rates_in.5, s32[1,256]{1,0:T(1,128)} %seg_in.5, bf16[1,256,512]{2,1,0:T(8,128)(2,1)} %k_in.5, ...), custom_call_target="tpu_custom_call" | custom-call | tf_op jit(solution)/shard_map/near/pallas_call | solution.py:240
  37.0 6.4 %all-to-all-done.1.states = bf16[8,128,128]{2,1,0:T(8,128)(2,1)S(1)} async-done(((bf16[8,128,128]{2,1,0:T(8,128)(2,1)}), bf16[8,128,128]{2,1,0:T(8,128)(2,1)S(1)}, u32[]{:S(2)}, u32[]{:S(2)}) %all-to-all-start.1) | async-done | bytes 262176 | tf_op jit(solution)/shard_map/all_to_all | solution.py:265
  43.4 1.1 %far.1 = (bf16[256,512]{1,0:T(8,128)(2,1)S(1)}, bf16[2,256,768]{2,1,0:T(8,128)(2,1)S(1)}, bf16[256,768]{1,0:T(8,128)(2,1)S(1)}) custom-call(f32[256,512]{1,0:T(8,128)S(1)} %get-tuple-element.29.local, f32[256,128]{1,0:T(8,128)S(1)} %get-tuple-element.45.gain, bf16[1,256,512]{2,1,0:T(8,128)(2,1)S(1)} %get-tuple-element.31.k, ...), custom_call_target="tpu_custom_call" | custom-call | tf_op jit(solution)/shard_map/far/pallas_call | solution.py:240
  44.5 3.0 %collective-permute-start.1 = (bf16[2,256,768]{2,1,0:T(8,128)(2,1)S(1)}, bf16[2,256,768]{2,1,0:T(8,128)(2,1)S(1)}, u32[]{:S(2)}, u32[]{:S(2)}) collective-permute-start(bf16[2,256,768]{2,1,0:T(8,128)(2,1)S(1)} %get-tuple-element.34), channel_id=1, source_target_pairs={{0,14},{1,3},{2,0},{3,5},{4,2},{5,7},{6,4},{7,9},{8,6},{9,11},{10,... | collective-permute-start | bytes 2359304 | tf_op jit(solution)/shard_map/ppermute | solution.py:330
  47.5 3.5 %collective-permute-start.2 = (bf16[256,768]{1,0:T(8,128)(2,1)S(1)}, bf16[256,768]{1,0:T(8,128)(2,1)S(1)}, u32[]{:S(2)}, u32[]{:S(2)}) collective-permute-start(bf16[256,768]{1,0:T(8,128)(2,1)S(1)} %get-tuple-element.35), channel_id=1, source_target_pairs={{0,2},{1,15},{2,4},{3,1},{4,6},{5,3},{6,8},{7,5},{8,10},{9,7},{10,... | collective-permute-start | bytes 1179656 | tf_op jit(solution)/shard_map/ppermute | solution.py:330
  51.0 2.7 %partial_soon.2.refs_0_ = bf16[2,256,768]{2,1,0:T(8,128)(2,1)S(1)} custom-call(s32[3]{0:T(128)S(1)} %pad_add_fusion.place._.refs_0_, bf16[256,512]{1,0:T(8,128)(2,1)S(1)} %get-tuple-element.36.refs_1_, bf16[8,768,512]{2,1,0:T(8,128)(2,1)} %bitcast.9), custom_call_target="tpu_custom_call" | custom-call | tf_op jit(solution)/shard_map/partial_soon/pallas_call | solution.py:240
  53.7 2.3 %collective-permute-done.2.refs_1_ = bf16[256,768]{1,0:T(8,128)(2,1)S(1)} collective-permute-done((bf16[256,768]{1,0:T(8,128)(2,1)S(1)}, bf16[256,768]{1,0:T(8,128)(2,1)S(1)}, u32[]{:S(2)}, u32[]{:S(2)}) %collective-permute-start.2) | collective-permute-done | bytes 393248 | tf_op jit(solution)/shard_map/ppermute | solution.py:330
  56.1 2.3 %collective-permute-done.1.refs_1_ = bf16[2,256,768]{2,1,0:T(8,128)(2,1)S(1)} collective-permute-done((bf16[2,256,768]{2,1,0:T(8,128)(2,1)S(1)}, bf16[2,256,768]{2,1,0:T(8,128)(2,1)S(1)}, u32[]{:S(2)}, u32[]{:S(2)}) %collective-permute-start.1) | collective-permute-done | bytes 786464 | tf_op jit(solution)/shard_map/ppermute | solution.py:330
  58.5 6.4 %collective-permute-start.3 = (bf16[256,768]{1,0:T(8,128)(2,1)S(1)}, bf16[256,768]{1,0:T(8,128)(2,1)S(1)}, u32[]{:S(2)}, u32[]{:S(2)}) collective-permute-start(bf16[256,768]{1,0:T(8,128)(2,1)S(1)} %add_long.2), channel_id=1, source_target_pairs={{0,12},{1,5},{2,14},{3,7},{4,0},{5,9},{6,2},{7,11},{8,4},{9,13},{1... | collective-permute-start | bytes 1179656 | tf_op jit(solution)/shard_map/ppermute | solution.py:355
  64.9 1.9 %collective-permute-start.4 = (bf16[256,768]{1,0:T(8,128)(2,1)S(1)}, bf16[256,768]{1,0:T(8,128)(2,1)S(1)}, u32[]{:S(2)}, u32[]{:S(2)}) collective-permute-start(bf16[256,768]{1,0:T(8,128)(2,1)S(1)} %add_short.2), channel_id=1, source_target_pairs={{0,2},{1,15},{2,4},{3,1},{4,6},{5,3},{6,8},{7,5},{8,10},{9,7},{10,... | collective-permute-start | bytes 1179656 | tf_op jit(solution)/shard_map/ppermute | solution.py:355
  66.9 3.2 %partial_later.2 = (bf16[3,256,768]{2,1,0:T(8,128)(2,1)S(1)}, bf16[256,512]{1,0:T(8,128)(2,1)}) custom-call(s32[3]{0:T(128)S(1)} %pad_add_fusion.place._.refs_0_, bf16[256,512]{1,0:T(8,128)(2,1)S(1)} %get-tuple-element.36.refs_1_, bf16[8,768,512]{2,1,0:T(8,128)(2,1)} %bitcast.10), custom_call_target="tpu_custom_call" | custom-call | tf_op jit(solution)/shard_map/partial_later/pallas_call | solution.py:240
  70.1 2.3 %collective-permute-done.3.refs_2_ = bf16[256,768]{1,0:T(8,128)(2,1)S(1)} collective-permute-done((bf16[256,768]{1,0:T(8,128)(2,1)S(1)}, bf16[256,768]{1,0:T(8,128)(2,1)S(1)}, u32[]{:S(2)}, u32[]{:S(2)}) %collective-permute-start.3) | collective-permute-done | bytes 393248 | tf_op jit(solution)/shard_map/ppermute | solution.py:355
  72.5 6.5 %collective-permute-done.4.refs_1_ = bf16[256,768]{1,0:T(8,128)(2,1)S(1)} collective-permute-done((bf16[256,768]{1,0:T(8,128)(2,1)S(1)}, bf16[256,768]{1,0:T(8,128)(2,1)S(1)}, u32[]{:S(2)}, u32[]{:S(2)}) %collective-permute-start.4) | collective-permute-done | bytes 393248 | tf_op jit(solution)/shard_map/ppermute | solution.py:355
  79.1 7.4 %collective-permute-start.5 = (bf16[256,768]{1,0:T(8,128)(2,1)S(1)}, bf16[256,768]{1,0:T(8,128)(2,1)S(1)}, u32[]{:S(2)}, u32[]{:S(2)}) collective-permute-start(bf16[256,768]{1,0:T(8,128)(2,1)S(1)} %add_long_last.2), channel_id=1, source_target_pairs={{0,15},{1,2},{2,1},{3,4},{4,3},{5,6},{6,5},{7,8},{8,7},{9,10},{10,... | collective-permute-start | bytes 1179656 | tf_op jit(solution)/shard_map/ppermute | solution.py:355
  86.5 2.3 %collective-permute-start.6 = (bf16[256,768]{1,0:T(8,128)(2,1)S(1)}, bf16[256,768]{1,0:T(8,128)(2,1)S(1)}, u32[]{:S(2)}, u32[]{:S(2)}) collective-permute-start(bf16[256,768]{1,0:T(8,128)(2,1)S(1)} %add_short_last.2), channel_id=1, source_target_pairs={{0,3},{1,14},{2,5},{3,0},{4,7},{5,2},{6,9},{7,4},{8,11},{9,6},{10,... | collective-permute-start | bytes 1179656 | tf_op jit(solution)/shard_map/ppermute | solution.py:355
  88.8 4.2 %collective-permute-start.7 = (bf16[1,256,768]{2,1,0:T(8,128)(2,1)S(1)}, bf16[1,256,768]{2,1,0:T(8,128)(2,1)S(1)}, u32[]{:S(2)}, u32[]{:S(2)}) collective-permute-start(bf16[1,256,768]{2,1,0:T(8,128)(2,1)S(1)} %slice.4), channel_id=1, source_target_pairs={{0,1},{1,0},{2,3},{3,2},{4,5},{5,4},{6,7},{7,6},{8,9},{9,8},{10,11... | collective-permute-start | bytes 1179656 | tf_op jit(solution)/shard_map/ppermute | solution.py:355
  93.0 3.5 %query_key.1 = (bf16[256,512]{1,0:T(8,128)(2,1)}, bf16[256,512]{1,0:T(8,128)(2,1)}) custom-call(f32[1,4,256]{2,1,0:T(4,128)} %rates_in.5, s32[1,256]{1,0:T(1,128)} %seg_in.5, bf16[1,256,512]{2,1,0:T(8,128)(2,1)} %q_in.5, bf16[1,256,512]{2,1,0:T(8,128)(2,1)} %k_in.5, bf16[1,256,512]{2,1,0:T(8,128)(2,1)} %v_in.3, bf16[1,256,512]{2,1,0:T(8,128)(2,1)} %o_in.5, ...), custom_call_target="tpu_custom_call" | custom-call | tf_op jit(solution)/shard_map/query_key/pallas_call | solution.py:240
  96.6 2.8 %collective-permute-done.6.refs_2_ = bf16[256,768]{1,0:T(8,128)(2,1)S(1)} collective-permute-done((bf16[256,768]{1,0:T(8,128)(2,1)S(1)}, bf16[256,768]{1,0:T(8,128)(2,1)S(1)}, u32[]{:S(2)}, u32[]{:S(2)}) %collective-permute-start.6) | collective-permute-done | bytes 393248 | tf_op jit(solution)/shard_map/ppermute | solution.py:355
  (10 shorter events, 2.0 us)
Async XLA Ops:
  21.7 7.7 %collective-permute-start = (bf16[144,128]{1,0:T(8,128)(2,1)S(1)}, bf16[144,128]{1,0:T(8,128)(2,1)S(1)}, u32[]{:S(2)}, u32[]{:S(2)}) collective-permute-start(bf16[144,128]{1,0:T(8,128)(2,1)S(1)} %row_total.1), channel_id=1, source_target_pairs={{64,192},{80,208},{96,224},{112,240},{128,0},{144,16},{160,32},{17... | collective-permute-start | bytes 110600 | tf_op jit(solution)/shard_map/ppermute | solution.py:289
  30.8 12.7 %all-to-all-start.1 = ((bf16[8,128,128]{2,1,0:T(8,128)(2,1)}), bf16[8,128,128]{2,1,0:T(8,128)(2,1)S(1)}, u32[]{:S(2)}, u32[]{:S(2)}) async-start(bf16[8,128,128]{2,1,0:T(8,128)(2,1)} %row_scan.1), calls=%async_computation.1 | async-start | bytes 524288 | tf_op jit(solution)/shard_map/all_to_all | solution.py:265
  44.5 13.9 %collective-permute-start.1 = (bf16[2,256,768]{2,1,0:T(8,128)(2,1)S(1)}, bf16[2,256,768]{2,1,0:T(8,128)(2,1)S(1)}, u32[]{:S(2)}, u32[]{:S(2)}) collective-permute-start(bf16[2,256,768]{2,1,0:T(8,128)(2,1)S(1)} %get-tuple-element.34), channel_id=1, source_target_pairs={{0,14},{1,3},{2,0},{3,5},{4,2},{5,7},{6,4},{7,9},{8,6},{9,11},{10,... | collective-permute-start | bytes 2359304 | tf_op jit(solution)/shard_map/ppermute | solution.py:330
  47.5 8.5 %collective-permute-start.2 = (bf16[256,768]{1,0:T(8,128)(2,1)S(1)}, bf16[256,768]{1,0:T(8,128)(2,1)S(1)}, u32[]{:S(2)}, u32[]{:S(2)}) collective-permute-start(bf16[256,768]{1,0:T(8,128)(2,1)S(1)} %get-tuple-element.35), channel_id=1, source_target_pairs={{0,2},{1,15},{2,4},{3,1},{4,6},{5,3},{6,8},{7,5},{8,10},{9,7},{10,... | collective-permute-start | bytes 1179656 | tf_op jit(solution)/shard_map/ppermute | solution.py:330
  58.5 13.8 %collective-permute-start.3 = (bf16[256,768]{1,0:T(8,128)(2,1)S(1)}, bf16[256,768]{1,0:T(8,128)(2,1)S(1)}, u32[]{:S(2)}, u32[]{:S(2)}) collective-permute-start(bf16[256,768]{1,0:T(8,128)(2,1)S(1)} %add_long.2), channel_id=1, source_target_pairs={{0,12},{1,5},{2,14},{3,7},{4,0},{5,9},{6,2},{7,11},{8,4},{9,13},{1... | collective-permute-start | bytes 1179656 | tf_op jit(solution)/shard_map/ppermute | solution.py:355
  64.9 14.1 %collective-permute-start.4 = (bf16[256,768]{1,0:T(8,128)(2,1)S(1)}, bf16[256,768]{1,0:T(8,128)(2,1)S(1)}, u32[]{:S(2)}, u32[]{:S(2)}) collective-permute-start(bf16[256,768]{1,0:T(8,128)(2,1)S(1)} %add_short.2), channel_id=1, source_target_pairs={{0,2},{1,15},{2,4},{3,1},{4,6},{5,3},{6,8},{7,5},{8,10},{9,7},{10,... | collective-permute-start | bytes 1179656 | tf_op jit(solution)/shard_map/ppermute | solution.py:355
  79.1 17.4 %collective-permute-start.5 = (bf16[256,768]{1,0:T(8,128)(2,1)S(1)}, bf16[256,768]{1,0:T(8,128)(2,1)S(1)}, u32[]{:S(2)}, u32[]{:S(2)}) collective-permute-start(bf16[256,768]{1,0:T(8,128)(2,1)S(1)} %add_long_last.2), channel_id=1, source_target_pairs={{0,15},{1,2},{2,1},{3,4},{4,3},{5,6},{6,5},{7,8},{8,7},{9,10},{10,... | collective-permute-start | bytes 1179656 | tf_op jit(solution)/shard_map/ppermute | solution.py:355
  86.5 12.8 %collective-permute-start.6 = (bf16[256,768]{1,0:T(8,128)(2,1)S(1)}, bf16[256,768]{1,0:T(8,128)(2,1)S(1)}, u32[]{:S(2)}, u32[]{:S(2)}) collective-permute-start(bf16[256,768]{1,0:T(8,128)(2,1)S(1)} %add_short_last.2), channel_id=1, source_target_pairs={{0,3},{1,14},{2,5},{3,0},{4,7},{5,2},{6,9},{7,4},{8,11},{9,6},{10,... | collective-permute-start | bytes 1179656 | tf_op jit(solution)/shard_map/ppermute | solution.py:355
  88.8 10.5 %collective-permute-start.7 = (bf16[1,256,768]{2,1,0:T(8,128)(2,1)S(1)}, bf16[1,256,768]{2,1,0:T(8,128)(2,1)S(1)}, u32[]{:S(2)}, u32[]{:S(2)}) collective-permute-start(bf16[1,256,768]{2,1,0:T(8,128)(2,1)S(1)} %slice.4), channel_id=1, source_target_pairs={{0,1},{1,0},{2,3},{3,2},{4,5},{5,4},{6,7},{7,6},{8,9},{9,8},{10,11... | collective-permute-start | bytes 1179656 | tf_op jit(solution)/shard_map/ppermute | solution.py:355

commit v9 on v8

--- a/solution.py
+++ b/solution.py
@@ -63,7 +63,7 @@
     return copies
 
 
-def local_kernel(_, rates_in, seg_in, q_in, o_in, k_in, v_in, out, rates, seg_row, q, o, k, v, sems):
+def local_kernel(rates_in, seg_in, q_in, o_in, k_in, v_in, out, rates, seg_row, q, o, k, v, sems):
     sources = (rates_in, seg_in, q_in, o_in, k_in, v_in)
     rates_copy, seg_copy, *others = fetch(sources, (rates, seg_row, q, o, k, v), sems)
     rates_copy.wait()
@@ -95,8 +95,8 @@
     return jnp.exp(jnp.where(keep, cum_col - cum_row, NEVER))
 
 
-def near_kernel(place, rates_in, seg_in, k_in, q_in, o_in, w_in, gv, gain, k, w, rates, seg_row, q, o, sems):
-    w_first = [w_in.at[destination(place, offset, w_in.shape[0])] for offset in FIRST]
+def near_kernel(rates_in, seg_in, k_in, q_in, o_in, w_in, gv, gain, k, w, rates, seg_row, q, o, sems):
+    w_first = [w_in.at[destination(offset, w_in.shape[0])] for offset in FIRST]
     sources = (rates_in, seg_in, k_in, q_in, o_in, *w_first)
     targets = (rates, seg_row, k, q, o, *(w.at[i] for i in range(len(FIRST))))
     rates_copy, seg_copy, *others = fetch(sources, targets, sems)
@@ -130,15 +130,15 @@
     return block[:rows], meta[0:1], meta[1:2], meta[2:3] + meta[3:4]
 
 
-def block_at(place, k):
-    return jnp.where(place[2] > 0, ROW - 1 - k, k)
-
-
-def row_total_kernel(place, msg, out):
+def block_at(k):
+    return jnp.where(lax.axis_index("line") < ROW // 2, ROW - 1 - k, k)
+
+
+def row_total_kernel(msg, out):
     rows = out.shape[0] - META
-    total, _, tag, _ = unpack(msg, block_at(place, 0))
+    total, _, tag, _ = unpack(msg, block_at(0))
     for k in range(1, ROW):
-        state, entry, leave, through = unpack(msg, block_at(place, k))
+        state, entry, leave, through = unpack(msg, block_at(k))
         same = jnp.where((entry == leave) & (tag == entry), through, 0.0)
         total = same * total + state
         tag = leave
@@ -146,12 +146,12 @@
     out[rows:, :] = jnp.broadcast_to(tag, (META, tag.shape[1])).astype(bf16)
 
 
-def row_scan_kernel(place, msg, carried, out):
+def row_scan_kernel(msg, carried, out):
     rows = carried.shape[0] - META
     running = carried[0:rows, :].astype(f32)
     tag = carried[rows : rows + META, :].astype(f32)[0:1]
     for k in range(ROW):
-        y = block_at(place, k)
+        y = block_at(k)
         state, entry, leave, through = unpack(msg, y)
         out[y] = jnp.where(entry == tag, running, 0.0).astype(bf16)
         same = jnp.where((entry == leave) & (tag == entry), through, 0.0)
@@ -159,8 +159,9 @@
         tag = leave
 
 
-def destination(place, offset, groups):
-    return lax.rem(place[0] + groups + place[1] * offset, groups)
+def destination(offset, groups):
+    sign = 1 - 2 * (lax.axis_index("pipe") & 1)
+    return lax.rem(lax.axis_index("head") + groups + sign * offset, groups)
 
 
 FIRST = (-4, -2, 3)
@@ -179,10 +180,10 @@
     single[...] = dot(gv[...], w[pair.shape[0]], ((1,), (1,))).astype(bf16)
 
 
-def partial_kernel(wanted, place, gv, w_in, out, *rest):
+def partial_kernel(wanted, gv, w_in, out, *rest):
     *gv_out, w, sems = rest
     groups = w_in.shape[0]
-    sources = [w_in.at[destination(place, offset, groups)] for offset in wanted]
+    sources = [w_in.at[destination(offset, groups)] for offset in wanted]
     copies = fetch(sources, [w.at[i] for i in range(len(wanted))], sems)
     for target in gv_out:
         copies.append(pltpu.make_async_copy(gv, target, sems.at[len(wanted)]))
@@ -229,7 +230,6 @@
 
 
 IN_VMEM = pl.BlockSpec(memory_space=pltpu.VMEM)
-IN_SMEM = pl.BlockSpec(memory_space=pltpu.SMEM)
 IN_HBM = pl.BlockSpec(memory_space=pltpu.HBM)
 
 
@@ -266,20 +266,16 @@
 
     lines = lax.axis_size("line")
     back = lines // 2
-    scans_back = (lax.axis_index("line") < back).astype(jnp.int32)
-    place = jnp.stack([lax.axis_index("head"), 1 - 2 * (lax.axis_index("pipe") & 1), scans_back]).astype(jnp.int32)
     sent = call(
         local_kernel,
         pltpu.VMEM((ROW, dh + META, dh), bf16),
         "local",
         mib=12,
-        in_specs=[IN_SMEM] + [IN_HBM] * 6,
+        in_specs=[IN_HBM] * 6,
         scratch=[*small, block, block, block, block, dma((6,))],
-    )(place, log_decay, segment_ids, queries, out_grad, keys, values)
+    )(log_decay, segment_ids, queries, out_grad, keys, values)
     got = exchange(sent)
-    total = call(row_total_kernel, pltpu.VMEM((dh + META, dh), bf16), "row_total", in_specs=[IN_SMEM, IN_VMEM])(
-        place, got
-    )
+    total = call(row_total_kernel, pltpu.VMEM((dh + META, dh), bf16), "row_total")(got)
     pairs = []
     for z in range(planes):
         for y in range(lines):
@@ -287,9 +283,7 @@
             if 0 <= to < planes:
                 pairs.append((z * lines + y, to * lines + y))
     carried = lax.ppermute(total, ("plane", "line"), pairs)
-    scanned = call(
-        row_scan_kernel, pltpu.VMEM((ROW, dh, dh), bf16), "row_scan", in_specs=[IN_SMEM, IN_VMEM, IN_VMEM]
-    )(place, got, carried)
+    scanned = call(row_scan_kernel, pltpu.VMEM((ROW, dh, dh), bf16), "row_scan")(got, carried)
     states = exchange(scanned)
     weights = w_value.reshape(groups, step, width)
     gv_local, gain, keys_near, w_first = call(
@@ -297,9 +291,9 @@
         (pltpu.VMEM((n, width), f32), pltpu.VMEM((n, dh), f32), block, pltpu.VMEM((len(FIRST), step, width), bf16)),
         "near",
         mib=12,
-        in_specs=[IN_SMEM] + [IN_HBM] * 6,
+        in_specs=[IN_HBM] * 6,
         scratch=[*small, block, block, dma((5 + len(FIRST),))],
-    )(place, log_decay, segment_ids, keys, queries, out_grad, weights)
+    )(log_decay, segment_ids, keys, queries, out_grad, weights)
 
     part = pltpu.VMEM((n, step), bf16)
     near_gv, pair, single = call(
@@ -314,10 +308,10 @@
             (pltpu.VMEM((count, n, step), bf16), *extra),
             name,
             mib=4 * count,
-            in_specs=[IN_SMEM, IN_VMEM, IN_HBM],
+            in_specs=[IN_VMEM, IN_HBM],
             out_specs=(IN_VMEM, *(IN_HBM for _ in extra)),
             scratch=[pltpu.VMEM((count, step, width), bf16), dma((count + 1,))],
-        )(place, gv, weights)
+        )(gv, weights)
 
     sections = lax.axis_size("pipe")
 

time: 101 us -> 98.9 us (0.979)
  Pallas kernels: 19.3 us -> 16 us
  waiting for transfers between devices: 29.1 us -> 30.5 us
    pallas_call x13, Pallas kernels: 19.3 us -> 16 us  [run(): pl.pallas_call(kernel, in_specs=specs, out_specs=jax.tree.map(lambda _: I...]
  transfers between devices with their start and end apart: 9 -> 9, of which waited for: 7 -> 7; matrix products, arithmetic and copies ran while one was open for 0% -> 0% of each run, Pallas kernels for 12% -> 11%
where the time goes in v9:
time: 98.9 us; the launch traced here: 98.4 us
  starting transfers between devices  33.5 us (34%)
  waiting for transfers between devices  30.5 us (31%)
  blocking collectives  17.6 us (18%)
  Pallas kernels  16 us (16%)
    ppermute x7, starting transfers between devices, hop(): return lax.ppermute(array, ('head', 'pipe'), pairs)  28.8 us
    all_to_all x1, blocking collectives, exchange(): return lax.all_to_all(array, 'line', 0, 0, tiled=True)  17.6 us
    ppermute x7, waiting for transfers between devices, hop(): return lax.ppermute(array, ('head', 'pipe'), pairs)  17.1 us
    pallas_call x13, Pallas kernels, run(): pl.pallas_call(kernel, in_specs=specs, out_specs=jax.tree.map(lambda _: I...  16 us
    all_to_all x1, waiting for transfers between devices, exchange(): return lax.all_to_all(array, 'line', 0, 0, tiled=True)  6.94 us
    ppermute x1, waiting for transfers between devices, body(): carried = lax.ppermute(total, ('plane', 'line'), pairs)  6.39 us
    all_to_all x1, starting transfers between devices, exchange(): return lax.all_to_all(array, 'line', 0, 0, tiled=True)  3.41 us
  transfers between devices with their start and end apart: 9, of which 7 were waited for; matrix products, arithmetic and copies ran while one was open for 0% of the time, Pallas kernels for 11%

profile of v9, /device:TPU:1, one launch (start us, length us, event | category | flops | bytes accessed | tf_op | source)
XLA Modules:
  0.0 98.4 jit_solution(1059851645499884535)
XLA Ops:
  0.6 2.2 %local.1 = bf16[8,144,128]{2,1,0:T(8,128)(2,1)S(1)} custom-call(f32[1,4,256]{2,1,0:T(4,128)} %rates_in.5, s32[1,256]{1,0:T(1,128)} %seg_in.5, bf16[1,256,512]{2,1,0:T(8,128)(2,1)} %q_in.5, bf16[1,256,512]{2,1,0:T(8,128)(2,1)} %o_in.5, bf16[1,256,512]{2,1,0:T(8,128)(2,1)} %k_in.5, bf16[1,256,512]{2,1,0:T(8,128)(2,1)} %v_in.3), custom_call_target="tpu_custom_call" | custom-call | tf_op jit(solution)/shard_map/local/pallas_call | solution.py:240
  2.9 17.6 %all_to_all.10.msg = bf16[8,144,128]{2,1,0:T(8,128)(2,1)S(1)} all-to-all(bf16[8,144,128]{2,1,0:T(8,128)(2,1)S(1)} %local.1), channel_id=1, replica_groups=mesh['plane'=8,'line'=8,'head'=8,'pipe'=2] {'line'}, dimensions={0} | all-to-all | bytes 589824 | tf_op jit(solution)/shard_map/all_to_all | solution.py:265
  20.5 1.3 %collective-permute-start = (bf16[144,128]{1,0:T(8,128)(2,1)S(1)}, bf16[144,128]{1,0:T(8,128)(2,1)S(1)}, u32[]{:S(2)}, u32[]{:S(2)}) collective-permute-start(bf16[144,128]{1,0:T(8,128)(2,1)S(1)} %row_total.1), channel_id=1, source_target_pairs={{64,192},{80,208},{96,224},{112,240},{128,0},{144,16},{160,32},{17... | collective-permute-start | bytes 110600 | tf_op jit(solution)/shard_map/ppermute | solution.py:285
  21.8 6.4 %collective-permute-done.carried = bf16[144,128]{1,0:T(8,128)(2,1)S(1)} collective-permute-done((bf16[144,128]{1,0:T(8,128)(2,1)S(1)}, bf16[144,128]{1,0:T(8,128)(2,1)S(1)}, u32[]{:S(2)}, u32[]{:S(2)}) %collective-permute-start) | collective-permute-done | bytes 36896 | tf_op jit(solution)/shard_map/ppermute | solution.py:285
  29.0 3.4 %all-to-all-start.1 = ((bf16[8,128,128]{2,1,0:T(8,128)(2,1)}), bf16[8,128,128]{2,1,0:T(8,128)(2,1)S(1)}, u32[]{:S(2)}, u32[]{:S(2)}) async-start(bf16[8,128,128]{2,1,0:T(8,128)(2,1)} %row_scan.1), calls=%async_computation.1 | async-start | bytes 524288 | tf_op jit(solution)/shard_map/all_to_all | solution.py:265
  32.4 2.3 %near.1 = (f32[256,512]{1,0:T(8,128)S(1)}, f32[256,128]{1,0:T(8,128)S(1)}, bf16[1,256,512]{2,1,0:T(8,128)(2,1)S(1)}, bf16[3,768,512]{2,1,0:T(8,128)(2,1)S(1)}) custom-call(f32[1,4,256]{2,1,0:T(4,128)} %rates_in.5, s32[1,256]{1,0:T(1,128)} %seg_in.5, bf16[1,256,512]{2,1,0:T(8,128)(2,1)} %k_in.5, bf16[1,256,512]{2,1,0:T(8,128)(2,1)} %q_in.5, ...), custom_call_target="tpu_custom_call" | custom-call | tf_op jit(solution)/shard_map/near/pallas_call | solution.py:240
  34.7 6.9 %all-to-all-done.1.states = bf16[8,128,128]{2,1,0:T(8,128)(2,1)S(1)} async-done(((bf16[8,128,128]{2,1,0:T(8,128)(2,1)}), bf16[8,128,128]{2,1,0:T(8,128)(2,1)S(1)}, u32[]{:S(2)}, u32[]{:S(2)}) %all-to-all-start.1) | async-done | bytes 262176 | tf_op jit(solution)/shard_map/all_to_all | solution.py:265
  41.7 1.0 %far.1 = (bf16[256,512]{1,0:T(8,128)(2,1)S(1)}, bf16[2,256,768]{2,1,0:T(8,128)(2,1)S(1)}, bf16[256,768]{1,0:T(8,128)(2,1)S(1)}) custom-call(f32[256,512]{1,0:T(8,128)S(1)} %get-tuple-element.29.local, f32[256,128]{1,0:T(8,128)S(1)} %get-tuple-element.45.gain, bf16[1,256,512]{2,1,0:T(8,128)(2,1)S(1)} %get-tuple-element.31.k, ...), custom_call_target="tpu_custom_call" | custom-call | tf_op jit(solution)/shard_map/far/pallas_call | solution.py:240
  42.7 3.0 %collective-permute-start.1 = (bf16[2,256,768]{2,1,0:T(8,128)(2,1)S(1)}, bf16[2,256,768]{2,1,0:T(8,128)(2,1)S(1)}, u32[]{:S(2)}, u32[]{:S(2)}) collective-permute-start(bf16[2,256,768]{2,1,0:T(8,128)(2,1)S(1)} %get-tuple-element.34), channel_id=1, source_target_pairs={{0,14},{1,3},{2,0},{3,5},{4,2},{5,7},{6,4},{7,9},{8,6},{9,11},{10,... | collective-permute-start | bytes 2359304 | tf_op jit(solution)/shard_map/ppermute | solution.py:324
  45.8 3.5 %collective-permute-start.2 = (bf16[256,768]{1,0:T(8,128)(2,1)S(1)}, bf16[256,768]{1,0:T(8,128)(2,1)S(1)}, u32[]{:S(2)}, u32[]{:S(2)}) collective-permute-start(bf16[256,768]{1,0:T(8,128)(2,1)S(1)} %get-tuple-element.35), channel_id=1, source_target_pairs={{0,2},{1,15},{2,4},{3,1},{4,6},{5,3},{6,8},{7,5},{8,10},{9,7},{10,... | collective-permute-start | bytes 1179656 | tf_op jit(solution)/shard_map/ppermute | solution.py:324
  49.2 2.1 %partial_soon.2.refs_0_ = bf16[2,256,768]{2,1,0:T(8,128)(2,1)S(1)} custom-call(bf16[256,512]{1,0:T(8,128)(2,1)S(1)} %get-tuple-element.36.refs_0_, bf16[8,768,512]{2,1,0:T(8,128)(2,1)} %bitcast.6), custom_call_target="tpu_custom_call" | custom-call | tf_op jit(solution)/shard_map/partial_soon/pallas_call | solution.py:240
  51.4 2.9 %collective-permute-done.2.refs_1_ = bf16[256,768]{1,0:T(8,128)(2,1)S(1)} collective-permute-done((bf16[256,768]{1,0:T(8,128)(2,1)S(1)}, bf16[256,768]{1,0:T(8,128)(2,1)S(1)}, u32[]{:S(2)}, u32[]{:S(2)}) %collective-permute-start.2) | collective-permute-done | bytes 393248 | tf_op jit(solution)/shard_map/ppermute | solution.py:324
  54.4 2.3 %collective-permute-done.1.refs_1_ = bf16[2,256,768]{2,1,0:T(8,128)(2,1)S(1)} collective-permute-done((bf16[2,256,768]{2,1,0:T(8,128)(2,1)S(1)}, bf16[2,256,768]{2,1,0:T(8,128)(2,1)S(1)}, u32[]{:S(2)}, u32[]{:S(2)}) %collective-permute-start.1) | collective-permute-done | bytes 786464 | tf_op jit(solution)/shard_map/ppermute | solution.py:324
  56.8 6.3 %collective-permute-start.3 = (bf16[256,768]{1,0:T(8,128)(2,1)S(1)}, bf16[256,768]{1,0:T(8,128)(2,1)S(1)}, u32[]{:S(2)}, u32[]{:S(2)}) collective-permute-start(bf16[256,768]{1,0:T(8,128)(2,1)S(1)} %add_long.2), channel_id=1, source_target_pairs={{0,12},{1,5},{2,14},{3,7},{4,0},{5,9},{6,2},{7,11},{8,4},{9,13},{1... | collective-permute-start | bytes 1179656 | tf_op jit(solution)/shard_map/ppermute | solution.py:349
  63.1 1.9 %collective-permute-start.4 = (bf16[256,768]{1,0:T(8,128)(2,1)S(1)}, bf16[256,768]{1,0:T(8,128)(2,1)S(1)}, u32[]{:S(2)}, u32[]{:S(2)}) collective-permute-start(bf16[256,768]{1,0:T(8,128)(2,1)S(1)} %add_short.2), channel_id=1, source_target_pairs={{0,2},{1,15},{2,4},{3,1},{4,6},{5,3},{6,8},{7,5},{8,10},{9,7},{10,... | collective-permute-start | bytes 1179656 | tf_op jit(solution)/shard_map/ppermute | solution.py:349
  65.0 2.6 %partial_later.2 = (bf16[3,256,768]{2,1,0:T(8,128)(2,1)S(1)}, bf16[256,512]{1,0:T(8,128)(2,1)}) custom-call(bf16[256,512]{1,0:T(8,128)(2,1)S(1)} %get-tuple-element.36.refs_0_, bf16[8,768,512]{2,1,0:T(8,128)(2,1)} %bitcast.7), custom_call_target="tpu_custom_call" | custom-call | tf_op jit(solution)/shard_map/partial_later/pallas_call | solution.py:240
  67.7 2.8 %collective-permute-done.3.refs_2_ = bf16[256,768]{1,0:T(8,128)(2,1)S(1)} collective-permute-done((bf16[256,768]{1,0:T(8,128)(2,1)S(1)}, bf16[256,768]{1,0:T(8,128)(2,1)S(1)}, u32[]{:S(2)}, u32[]{:S(2)}) %collective-permute-start.3) | collective-permute-done | bytes 393248 | tf_op jit(solution)/shard_map/ppermute | solution.py:349
  70.6 6.4 %collective-permute-done.4.refs_1_ = bf16[256,768]{1,0:T(8,128)(2,1)S(1)} collective-permute-done((bf16[256,768]{1,0:T(8,128)(2,1)S(1)}, bf16[256,768]{1,0:T(8,128)(2,1)S(1)}, u32[]{:S(2)}, u32[]{:S(2)}) %collective-permute-start.4) | collective-permute-done | bytes 393248 | tf_op jit(solution)/shard_map/ppermute | solution.py:349
  77.1 7.7 %collective-permute-start.5 = (bf16[256,768]{1,0:T(8,128)(2,1)S(1)}, bf16[256,768]{1,0:T(8,128)(2,1)S(1)}, u32[]{:S(2)}, u32[]{:S(2)}) collective-permute-start(bf16[256,768]{1,0:T(8,128)(2,1)S(1)} %add_long_last.2), channel_id=1, source_target_pairs={{0,15},{1,2},{2,1},{3,4},{4,3},{5,6},{6,5},{7,8},{8,7},{9,10},{10,... | collective-permute-start | bytes 1179656 | tf_op jit(solution)/shard_map/ppermute | solution.py:349
  84.8 2.2 %collective-permute-start.6 = (bf16[256,768]{1,0:T(8,128)(2,1)S(1)}, bf16[256,768]{1,0:T(8,128)(2,1)S(1)}, u32[]{:S(2)}, u32[]{:S(2)}) collective-permute-start(bf16[256,768]{1,0:T(8,128)(2,1)S(1)} %add_short_last.2), channel_id=1, source_target_pairs={{0,3},{1,14},{2,5},{3,0},{4,7},{5,2},{6,9},{7,4},{8,11},{9,6},{10,... | collective-permute-start | bytes 1179656 | tf_op jit(solution)/shard_map/ppermute | solution.py:349
  87.0 4.2 %collective-permute-start.7 = (bf16[1,256,768]{2,1,0:T(8,128)(2,1)S(1)}, bf16[1,256,768]{2,1,0:T(8,128)(2,1)S(1)}, u32[]{:S(2)}, u32[]{:S(2)}) collective-permute-start(bf16[1,256,768]{2,1,0:T(8,128)(2,1)S(1)} %slice.4), channel_id=1, source_target_pairs={{0,1},{1,0},{2,3},{3,2},{4,5},{5,4},{6,7},{7,6},{8,9},{9,8},{10,11... | collective-permute-start | bytes 1179656 | tf_op jit(solution)/shard_map/ppermute | solution.py:349
  91.2 3.5 %query_key.1 = (bf16[256,512]{1,0:T(8,128)(2,1)}, bf16[256,512]{1,0:T(8,128)(2,1)}) custom-call(f32[1,4,256]{2,1,0:T(4,128)} %rates_in.5, s32[1,256]{1,0:T(1,128)} %seg_in.5, bf16[1,256,512]{2,1,0:T(8,128)(2,1)} %q_in.5, bf16[1,256,512]{2,1,0:T(8,128)(2,1)} %k_in.5, bf16[1,256,512]{2,1,0:T(8,128)(2,1)} %v_in.3, bf16[1,256,512]{2,1,0:T(8,128)(2,1)} %o_in.5, ...), custom_call_target="tpu_custom_call" | custom-call | tf_op jit(solution)/shard_map/query_key/pallas_call | solution.py:240
  94.7 2.8 %collective-permute-done.6.refs_2_ = bf16[256,768]{1,0:T(8,128)(2,1)S(1)} collective-permute-done((bf16[256,768]{1,0:T(8,128)(2,1)S(1)}, bf16[256,768]{1,0:T(8,128)(2,1)S(1)}, u32[]{:S(2)}, u32[]{:S(2)}) %collective-permute-start.6) | collective-permute-done | bytes 393248 | tf_op jit(solution)/shard_map/ppermute | solution.py:349
  97.5 0.9 add_last.1
  (9 shorter events, 1.3 us)
Async XLA Ops:
  20.5 7.7 %collective-permute-start = (bf16[144,128]{1,0:T(8,128)(2,1)S(1)}, bf16[144,128]{1,0:T(8,128)(2,1)S(1)}, u32[]{:S(2)}, u32[]{:S(2)}) collective-permute-start(bf16[144,128]{1,0:T(8,128)(2,1)S(1)} %row_total.1), channel_id=1, source_target_pairs={{64,192},{80,208},{96,224},{112,240},{128,0},{144,16},{160,32},{17... | collective-permute-start | bytes 110600 | tf_op jit(solution)/shard_map/ppermute | solution.py:285
  29.0 12.7 %all-to-all-start.1 = ((bf16[8,128,128]{2,1,0:T(8,128)(2,1)}), bf16[8,128,128]{2,1,0:T(8,128)(2,1)S(1)}, u32[]{:S(2)}, u32[]{:S(2)}) async-start(bf16[8,128,128]{2,1,0:T(8,128)(2,1)} %row_scan.1), calls=%async_computation.1 | async-start | bytes 524288 | tf_op jit(solution)/shard_map/all_to_all | solution.py:265
  42.7 13.9 %collective-permute-start.1 = (bf16[2,256,768]{2,1,0:T(8,128)(2,1)S(1)}, bf16[2,256,768]{2,1,0:T(8,128)(2,1)S(1)}, u32[]{:S(2)}, u32[]{:S(2)}) collective-permute-start(bf16[2,256,768]{2,1,0:T(8,128)(2,1)S(1)} %get-tuple-element.34), channel_id=1, source_target_pairs={{0,14},{1,3},{2,0},{3,5},{4,2},{5,7},{6,4},{7,9},{8,6},{9,11},{10,... | collective-permute-start | bytes 2359304 | tf_op jit(solution)/shard_map/ppermute | solution.py:324
  45.8 8.5 %collective-permute-start.2 = (bf16[256,768]{1,0:T(8,128)(2,1)S(1)}, bf16[256,768]{1,0:T(8,128)(2,1)S(1)}, u32[]{:S(2)}, u32[]{:S(2)}) collective-permute-start(bf16[256,768]{1,0:T(8,128)(2,1)S(1)} %get-tuple-element.35), channel_id=1, source_target_pairs={{0,2},{1,15},{2,4},{3,1},{4,6},{5,3},{6,8},{7,5},{8,10},{9,7},{10,... | collective-permute-start | bytes 1179656 | tf_op jit(solution)/shard_map/ppermute | solution.py:324
  56.8 13.7 %collective-permute-start.3 = (bf16[256,768]{1,0:T(8,128)(2,1)S(1)}, bf16[256,768]{1,0:T(8,128)(2,1)S(1)}, u32[]{:S(2)}, u32[]{:S(2)}) collective-permute-start(bf16[256,768]{1,0:T(8,128)(2,1)S(1)} %add_long.2), channel_id=1, source_target_pairs={{0,12},{1,5},{2,14},{3,7},{4,0},{5,9},{6,2},{7,11},{8,4},{9,13},{1... | collective-permute-start | bytes 1179656 | tf_op jit(solution)/shard_map/ppermute | solution.py:349
  63.1 13.9 %collective-permute-start.4 = (bf16[256,768]{1,0:T(8,128)(2,1)S(1)}, bf16[256,768]{1,0:T(8,128)(2,1)S(1)}, u32[]{:S(2)}, u32[]{:S(2)}) collective-permute-start(bf16[256,768]{1,0:T(8,128)(2,1)S(1)} %add_short.2), channel_id=1, source_target_pairs={{0,2},{1,15},{2,4},{3,1},{4,6},{5,3},{6,8},{7,5},{8,10},{9,7},{10,... | collective-permute-start | bytes 1179656 | tf_op jit(solution)/shard_map/ppermute | solution.py:349
  77.1 17.6 %collective-permute-start.5 = (bf16[256,768]{1,0:T(8,128)(2,1)S(1)}, bf16[256,768]{1,0:T(8,128)(2,1)S(1)}, u32[]{:S(2)}, u32[]{:S(2)}) collective-permute-start(bf16[256,768]{1,0:T(8,128)(2,1)S(1)} %add_long_last.2), channel_id=1, source_target_pairs={{0,15},{1,2},{2,1},{3,4},{4,3},{5,6},{6,5},{7,8},{8,7},{9,10},{10,... | collective-permute-start | bytes 1179656 | tf_op jit(solution)/shard_map/ppermute | solution.py:349
  84.8 12.7 %collective-permute-start.6 = (bf16[256,768]{1,0:T(8,128)(2,1)S(1)}, bf16[256,768]{1,0:T(8,128)(2,1)S(1)}, u32[]{:S(2)}, u32[]{:S(2)}) collective-permute-start(bf16[256,768]{1,0:T(8,128)(2,1)S(1)} %add_short_last.2), channel_id=1, source_target_pairs={{0,3},{1,14},{2,5},{3,0},{4,7},{5,2},{6,9},{7,4},{8,11},{9,6},{10,... | collective-permute-start | bytes 1179656 | tf_op jit(solution)/shard_map/ppermute | solution.py:349
  87.0 10.5 %collective-permute-start.7 = (bf16[1,256,768]{2,1,0:T(8,128)(2,1)S(1)}, bf16[1,256,768]{2,1,0:T(8,128)(2,1)S(1)}, u32[]{:S(2)}, u32[]{:S(2)}) collective-permute-start(bf16[1,256,768]{2,1,0:T(8,128)(2,1)S(1)} %slice.4), channel_id=1, source_target_pairs={{0,1},{1,0},{2,3},{3,2},{4,5},{5,4},{6,7},{7,6},{8,9},{9,8},{10,11... | collective-permute-start | bytes 1179656 | tf_op jit(solution)/shard_map/ppermute | solution.py:349
